TPU v7x, 512 devices: a whole 4x4x16 slice. The times are simulated.
512 devices in a mesh: ctx: 16 (over x, z_hi), fsdp: 32 (over z_lo, y, core).
Axes of the slice: x: 4, y: 4, z: 16 (z_hi: 4, z_lo: 4; z = z_hi * 4 + z_lo), core: 2. Of those that a mesh axis runs over, the one named last changes fastest.
Arguments:
- block_pos: int32 [8, 16], P(None, 'ctx'), may hold values from 0 to 15, each once within a row
- queries: bfloat16 [32, 2048, 640], P('fsdp', 'ctx'), may hold values from -6 to 6
- keys: bfloat16 [32, 2048, 128], P('fsdp', 'ctx'), may hold values from -6 to 6
- values: bfloat16 [32, 2048, 128], P('fsdp', 'ctx'), may hold values from -12 to 12
- attention_output: bfloat16 [32, 2048, 640], P('fsdp', 'ctx'), may hold values from -6 to 6
- output_gradient: bfloat16 [32, 2048, 640], P('fsdp', 'ctx'), may hold values from -24 to 24
- log_softmax_norm: float32 [32, 5, 2048], P('fsdp', None, 'ctx'), may hold values from 6 to 9
- features: bfloat16 [8, 2048, 2560], P(None, 'ctx', 'fsdp'), may hold values from -0.119628906 to 0.119628906
Outputs:
- grad_q: bfloat16 [32, 2048, 640], P('fsdp', 'ctx')
- key_gradient: bfloat16 [32, 2048, 128], P('fsdp', 'ctx')
- value_gradient: bfloat16 [32, 2048, 128], P('fsdp', 'ctx')
- grad_wk: float32 [2560, 512], P('fsdp')
Inputs may be any that keep to these rules, and one draw needn't show every extreme that they name: Each row of block_pos holds every block place 0 to 15 once.
All inputs are finite; a program needn't handle non-finite values.
Results may differ from a plain program's by a relative error of at most 0.0058.
Values may be sent and summed in bfloat16 or wider, within the bound.
No kernel may reach another device: no remote copies, remote signals or barrier semaphores. Data moves between devices by JAX's collectives and lax.ppermute only.
A program may use at most 64 MiB of HBM per device.

v0:
```python
import jax
import jax.numpy as jnp
from jax import lax
from jax.sharding import PartitionSpec as P

QUERY_HEADS = 20
KEY_VALUE_HEADS = 4
HEAD_SIZE = 128
HEAD_GROUPS = 4


def from_behind(value, axis, steps):
    count = lax.axis_size(axis)
    pairs = [(source, (source + steps) % count) for source in range(count)]
    return lax.ppermute(value, axis, pairs)


def shortened(shard):

    def short(part):
        return part.astype(jnp.bfloat16) if part.dtype == jnp.float32 else part

    return jax.tree.map(short, shard)


def block_grads(
    heads_of_queries,
    head_gradient,
    delta_heads,
    heads_of_norm,
    block_of_keys,
    block_of_values,
    key_place,
    key_offset,
    own_place,
):
    query_rows = heads_of_queries.shape[0]
    key_rows = block_of_keys.shape[0]
    score_scale = heads_of_queries.shape[-1] ** (-0.5)
    query_pos = own_place * query_rows + lax.iota(jnp.int32, query_rows)
    key_pos = key_place[0] * query_rows + key_offset + lax.iota(jnp.int32, key_rows)
    visible = key_pos[None, :] <= query_pos[:, None]
    scores = (
        jnp.einsum(
            "tkgd,ukd->kgtu", heads_of_queries, block_of_keys, preferred_element_type=jnp.float32
        )
        * score_scale
    )
    soft_probs = jnp.where(visible, jnp.exp(scores - heads_of_norm[..., None]), 0.0)
    dprobs = jnp.einsum(
        "tkgd,ukd->kgtu", head_gradient, block_of_values, preferred_element_type=jnp.float32
    )
    dscores = (soft_probs * (dprobs - delta_heads[..., None]) * score_scale).astype(jnp.bfloat16)
    probs_low = soft_probs.astype(jnp.bfloat16)
    grad_query = jnp.einsum(
        "kgtu,ukd->tkgd", dscores, block_of_keys, preferred_element_type=jnp.float32
    )
    gradient_for_key = jnp.einsum(
        "kgtu,tkgd->ukd", dscores, heads_of_queries, preferred_element_type=jnp.float32
    )
    gradient_for_value = jnp.einsum(
        "kgtu,tkgd->ukd", probs_low, head_gradient, preferred_element_type=jnp.float32
    )
    return (grad_query, gradient_for_key, gradient_for_value)


def local(
    block_pos, queries, keys, values, attention_output, output_gradient, log_softmax_norm, features
):
    rows_per_block = queries.shape[1]
    group_size = QUERY_HEADS // KEY_VALUE_HEADS
    kv_local = keys.shape[-1] // HEAD_SIZE
    sequence_index = lax.axis_index("fsdp") // HEAD_GROUPS
    own_row = lax.dynamic_slice_in_dim(block_pos, sequence_index, 1, 0)
    own_place = own_row[0, 0]
    key_place = own_row[0, 0:1]
    heads_of_queries = queries[0].reshape(rows_per_block, kv_local, group_size, HEAD_SIZE)
    head_gradient = output_gradient[0].reshape(rows_per_block, kv_local, group_size, HEAD_SIZE)
    heads_of_output = attention_output[0].reshape(rows_per_block, kv_local, group_size, HEAD_SIZE)
    delta = jnp.sum(
        head_gradient.astype(jnp.float32) * heads_of_output.astype(jnp.float32), axis=-1
    )
    delta_heads = jnp.transpose(delta, (1, 2, 0))
    heads_of_norm = log_softmax_norm[0].reshape(kv_local, group_size, rows_per_block)
    block_of_keys = keys[0].reshape(rows_per_block, kv_local, HEAD_SIZE)
    block_of_values = values[0].reshape(rows_per_block, kv_local, HEAD_SIZE)
    cycle_length = lax.axis_size("ctx")
    zero_key_gradient = jnp.zeros((rows_per_block, kv_local, HEAD_SIZE), jnp.float32)
    zero_query_gradient = jnp.zeros((rows_per_block, kv_local, group_size, HEAD_SIZE), jnp.float32)

    def visit_rows(query_acc, blocks, grad_pair, key_offset):
        add_query, add_key, add_value = block_grads(
            heads_of_queries,
            head_gradient,
            delta_heads,
            heads_of_norm,
            blocks[0],
            blocks[1],
            blocks[2],
            key_offset,
            own_place,
        )
        return (query_acc + add_query, (grad_pair[0] + add_key, grad_pair[1] + add_value))

    def visit(query_acc, blocks, grad_pair):
        return visit_rows(query_acc, blocks, grad_pair, 0)

    def pass_grads(grad_pair):
        return from_behind(grad_pair, "ctx", 1)

    def cycle_step(step_index, cycle_state):
        query_acc, blocks, grad_pair = cycle_state
        query_acc, grad_pair = visit(query_acc, blocks, grad_pair)
        blocks = jax.tree.map(
            lambda part, own: part.astype(own.dtype),
            from_behind(shortened(blocks), "ctx", 1),
            blocks,
        )
        grad_pair = pass_grads(grad_pair)
        return (query_acc, blocks, grad_pair)

    cycle_state = (
        zero_query_gradient,
        (block_of_keys, block_of_values, key_place),
        (zero_key_gradient, zero_key_gradient),
    )
    query_acc, blocks, grad_pair = lax.fori_loop(0, cycle_length - 1, cycle_step, cycle_state)
    query_acc, grad_pair = visit(query_acc, blocks, grad_pair)
    grad_pair = pass_grads(grad_pair)
    key_gradient_sum = grad_pair[0]
    value_gradient_sum = grad_pair[1]
    grad_q = query_acc.reshape(rows_per_block, -1).astype(jnp.bfloat16)
    key_gradient = key_gradient_sum.reshape(rows_per_block, -1).astype(jnp.bfloat16)
    value_gradient = value_gradient_sum.reshape(rows_per_block, -1).astype(jnp.bfloat16)
    local_width = key_gradient.shape[-1]
    feature_cols = features.shape[-1]
    piece = lax.all_gather(key_gradient[None], "fsdp", axis=0, tiled=True)
    count = piece.shape[0]
    indices = lax.iota(jnp.int32, count)
    seq_ids = indices // HEAD_GROUPS
    group_ids = indices % HEAD_GROUPS
    chosen = jnp.take(features, seq_ids, axis=0)
    contrib = jnp.einsum("pti,ptj->pij", chosen, piece, preferred_element_type=jnp.float32)
    rounded = lax.optimization_barrier(contrib.astype(jnp.bfloat16)).astype(jnp.float32)
    placing = (group_ids[:, None] == lax.iota(jnp.int32, HEAD_GROUPS)[None, :]).astype(jnp.float32)
    summed = jnp.einsum("pij,pr->irj", rounded, placing)
    summed = summed.reshape(feature_cols, HEAD_GROUPS * local_width)
    grad_wk = lax.psum(summed, "ctx")
    return (grad_q[None], key_gradient[None], value_gradient[None], grad_wk)


def solution(mesh):
    return jax.shard_map(
        local,
        mesh=mesh,
        in_specs=(
            P(None, "ctx"),
            P("fsdp", "ctx", None),
            P("fsdp", "ctx", None),
            P("fsdp", "ctx", None),
            P("fsdp", "ctx", None),
            P("fsdp", "ctx", None),
            P("fsdp", None, "ctx"),
            P(None, "ctx", "fsdp"),
        ),
        out_specs=(
            P("fsdp", "ctx", None),
            P("fsdp", "ctx", None),
            P("fsdp", "ctx", None),
            P("fsdp", None),
        ),
        check_vma=False,
    )
```

profile of v0, /device:TPU:2, one launch (start us, length us, event | category | flops | bytes accessed | tf_op | source)
XLA Modules:
  0.0 845.0 jit_solution(10300200507523520744)
XLA Ops:
  12.6 541.2 %while.23 = (s32[]{:T(128)}, f32[128,1,5,128]{3,0,2,1:T(8,128)S(1)}, bf16[128,1,128]{2,0,1:T(8,128)(2,1)S(1)}, bf16[128,1,128]{2,0,1:T(8,128)(2,1)S(1)}, s32[1]{...) while((s32[]{:T(128)}, ...), condition=%wide.region_2.3_spmd.clone, body=%wide.region_1.2_spmd.clone.sunk | while | flops 105726208 | bytes 4103563 | solution.py:127
  12.6 9.1 %collective-permute-start = (bf16[128,1,128]{2,0,1:T(8,128)(2,1)S(1)}, bf16[128,1,128]{2,0,1:T(8,128)(2,1)S(1)}, u32[]{:S(2)}, u32[]{:S(2)}) collective-permute-start(bf16[128,1,128]{2,0,1:T(8,128)(2,1)S(1)} %copy.66), channel_id=1, source_target_pairs={{0,32},{32,64},{64,96},{96,128},{128,160},{160,192},{192,224},{224... | collective-permute-start | bytes 98312 | tf_op jit(solution)/shard_map/while/body/eval_jaxpr/ppermute | solution.py:15
  21.7 9.1 %collective-permute-start.1 = (bf16[128,1,128]{2,0,1:T(8,128)(2,1)S(1)}, bf16[128,1,128]{2,0,1:T(8,128)(2,1)S(1)}, u32[]{:S(2)}, u32[]{:S(2)}) collective-permute-start(bf16[128,1,128]{2,0,1:T(8,128)(2,1)S(1)} %copy.67), channel_id=1, source_target_pairs={{0,32},{32,64},{64,96},{96,128},{128,160},{160,192},{192,224},{224... | collective-permute-start | bytes 98312 | tf_op jit(solution)/shard_map/while/body/eval_jaxpr/ppermute | solution.py:15
  31.4 5.6 collective-permute-start.2
  45.9 7.4 collective-permute-done.3
  57.8 8.3 collective-permute-start.1
  94.6 8.3 collective-permute-start.1
  119.1 6.7 collective-permute-done.4
  125.8 8.3 collective-permute-start
  148.5 7.0 collective-permute-start.4
  160.6 6.0 collective-permute-start
  166.6 6.5 collective-permute-start.1
  180.2 6.9 collective-permute-start.3
  192.3 5.9 collective-permute-done.4
  201.6 6.5 collective-permute-start.1
  208.6 7.9 collective-permute-start.2
  236.2 6.1 collective-permute-start.1
  247.4 7.0 collective-permute-start.3
  254.6 8.1 collective-permute-start.4
  266.0 6.8 collective-permute-start
  272.8 5.9 collective-permute-start.1
  284.9 6.5 collective-permute-start.3
  291.6 5.5 collective-permute-start.4
  297.5 7.8 collective-permute-done.4
  308.2 8.9 %collective-permute-start.1 = (bf16[128,1,128]{2,0,1:T(8,128)(2,1)S(1)}, bf16[128,1,128]{2,0,1:T(8,128)(2,1)S(1)}, u32[]{:S(2)}, u32[]{:S(2)}) collective-permute-start(bf16[128,1,128]{2,0,1:T(8,128)(2,1)S(1)} %copy.67), channel_id=1, source_target_pairs={{0,32},{32,64},{64,96},{96,128},{128,160},{160,192},{192,224},{224... | collective-permute-start | bytes 98312 | tf_op jit(solution)/shard_map/while/body/eval_jaxpr/ppermute | solution.py:15
  322.3 6.0 collective-permute-start.3
  333.6 6.4 collective-permute-done.4
  341.9 7.4 collective-permute-start.1
  349.8 9.7 %collective-permute-start.2 = (s32[1]{0:T(128)}, s32[1]{0:T(128)}, u32[]{:S(2)}, u32[]{:S(2)}) collective-permute-start(s32[1]{0:T(128)} %copy.68), channel_id=1, source_target_pairs={{0,32},{32,64},{64,96},{96,128},{128,160},{160,192},{192,224},{224... | collective-permute-start | bytes 20 | tf_op jit(solution)/shard_map/while/body/eval_jaxpr/ppermute | solution.py:15
  367.1 6.4 collective-permute-done.3
  384.5 7.4 collective-permute-start.2
  398.7 6.0 collective-permute-start.4
  405.2 5.6 collective-permute-done.4
  415.0 7.3 collective-permute-start.1
  422.8 6.1 collective-permute-start.2
  435.3 6.0 collective-permute-start.4
  446.3 6.5 collective-permute-start
  452.8 6.1 collective-permute-start.1
  465.1 5.7 collective-permute-start.3
  476.0 6.7 collective-permute-done.4
  490.0 9.6 %collective-permute-start.2 = (s32[1]{0:T(128)}, s32[1]{0:T(128)}, u32[]{:S(2)}, u32[]{:S(2)}) collective-permute-start(s32[1]{0:T(128)} %copy.68), channel_id=1, source_target_pairs={{0,32},{32,64},{64,96},{96,128},{128,160},{160,192},{192,224},{224... | collective-permute-start | bytes 20 | tf_op jit(solution)/shard_map/while/body/eval_jaxpr/ppermute | solution.py:15
  512.0 6.8 collective-permute-done.4
  523.2 8.2 collective-permute-start.2
  532.8 9.4 %collective-permute-start.3 = (f32[128,1,128]{2,0,1:T(8,128)S(1)}, f32[128,1,128]{2,0,1:T(8,128)S(1)}, u32[]{:S(2)}, u32[]{:S(2)}) collective-permute-start(f32[128,1,128]{2,0,1:T(8,128)S(1)} %fusion.89), channel_id=1, source_target_pairs={{0,32},{32,64},{64,96},{96,128},{128,160},{160,192},{192,224},{224... | collective-permute-start | bytes 196616 | tf_op jit(solution)/shard_map/while/body/eval_jaxpr/ppermute | solution.py:15
  544.7 9.1 %collective-permute-done.4 = f32[128,1,128]{2,0,1:T(8,128)S(1)} collective-permute-done((f32[128,1,128]{2,0,1:T(8,128)S(1)}, f32[128,1,128]{2,0,1:T(8,128)S(1)}, u32[]{:S(2)}, u32[]{:S(2)}) %collective-permute-start.4) | collective-permute-done | bytes 65568 | tf_op jit(solution)/shard_map/while/body/eval_jaxpr/ppermute | solution.py:15
  557.7 8.7 %collective-permute-done.5 = bf16[128,1,128]{2,0,1:T(8,128)(2,1)S(1)} collective-permute-done((bf16[128,1,128]{2,0,1:T(8,128)(2,1)S(1)}, bf16[128,1,128]{2,0,1:T(8,128)(2,1)S(1)}, u32[]{:S(2)}, u32[]{:S(2)}) %collective-permute-start.5) | collective-permute-done | bytes 32800 | tf_op jit(solution)/shard_map/ppermute | solution.py:15
  570.1 63.8 %all-gather.3.cloned.1.call-done = bf16[4096,1,128]{2,0,1:T(8,128)(2,1)} async-done(((bf16[128,1,128]{2,0,1:T(8,128)(2,1)}), bf16[4096,1,128]{2,0,1:T(8,128)(2,1)}) %all-gather.3.cloned.1.call-update) | async-done | bytes 1048592 | tf_op jit(solution)/shard_map/all_gather | solution.py:137
  637.8 197.5 %all-reduce.2.cloned.1.call-done = f32[80,512]{1,0:T(8,128)} async-done(((f32[80,512]{1,0:T(8,128)}), f32[80,512]{1,0:T(8,128)}) %all-reduce.2.cloned.1.call-update) | async-done | bytes 163856 | tf_op jit(solution)/shard_map/psum | solution.py:148
  (315 shorter events, 235.7 us)
Async XLA Ops:
  7.2 626.7 %all-gather.3.cloned.1.call-start = ((), (), s32[]{:S(2)}) async-start(), calls=%async_computation.1 | async-start | bytes 1081344 | tf_op jit(solution)/shard_map/all_gather | solution.py:137
  12.6 33.3 %collective-permute-start = (bf16[128,1,128]{2,0,1:T(8,128)(2,1)S(1)}, bf16[128,1,128]{2,0,1:T(8,128)(2,1)S(1)}, u32[]{:S(2)}, u32[]{:S(2)}) collective-permute-start(bf16[128,1,128]{2,0,1:T(8,128)(2,1)S(1)} %copy.66), channel_id=1, source_target_pairs={{0,32},{32,64},{64,96},{96,128},{128,160},{160,192},{192,224},{224... | collective-permute-start | bytes 98312 | tf_op jit(solution)/shard_map/while/body/eval_jaxpr/ppermute | solution.py:15
  21.7 24.2 %collective-permute-start.1 = (bf16[128,1,128]{2,0,1:T(8,128)(2,1)S(1)}, bf16[128,1,128]{2,0,1:T(8,128)(2,1)S(1)}, u32[]{:S(2)}, u32[]{:S(2)}) collective-permute-start(bf16[128,1,128]{2,0,1:T(8,128)(2,1)S(1)} %copy.67), channel_id=1, source_target_pairs={{0,32},{32,64},{64,96},{96,128},{128,160},{160,192},{192,224},{224... | collective-permute-start | bytes 98312 | tf_op jit(solution)/shard_map/while/body/eval_jaxpr/ppermute | solution.py:15
  31.4 14.5 %collective-permute-start.2 = (s32[1]{0:T(128)}, s32[1]{0:T(128)}, u32[]{:S(2)}, u32[]{:S(2)}) collective-permute-start(s32[1]{0:T(128)} %copy.68), channel_id=1, source_target_pairs={{0,32},{32,64},{64,96},{96,128},{128,160},{160,192},{192,224},{224... | collective-permute-start | bytes 20 | tf_op jit(solution)/shard_map/while/body/eval_jaxpr/ppermute | solution.py:15
  38.3 15.0 %collective-permute-start.3 = (f32[128,1,128]{2,0,1:T(8,128)S(1)}, f32[128,1,128]{2,0,1:T(8,128)S(1)}, u32[]{:S(2)}, u32[]{:S(2)}) collective-permute-start(f32[128,1,128]{2,0,1:T(8,128)S(1)} %fusion.89), channel_id=1, source_target_pairs={{0,32},{32,64},{64,96},{96,128},{128,160},{160,192},{192,224},{224... | collective-permute-start | bytes 196616 | tf_op jit(solution)/shard_map/while/body/eval_jaxpr/ppermute | solution.py:15
  54.0 27.8 %collective-permute-start = (bf16[128,1,128]{2,0,1:T(8,128)(2,1)S(1)}, bf16[128,1,128]{2,0,1:T(8,128)(2,1)S(1)}, u32[]{:S(2)}, u32[]{:S(2)}) collective-permute-start(bf16[128,1,128]{2,0,1:T(8,128)(2,1)S(1)} %copy.66), channel_id=1, source_target_pairs={{0,32},{32,64},{64,96},{96,128},{128,160},{160,192},{192,224},{224... | collective-permute-start | bytes 98312 | tf_op jit(solution)/shard_map/while/body/eval_jaxpr/ppermute | solution.py:15
  57.8 24.0 %collective-permute-start.1 = (bf16[128,1,128]{2,0,1:T(8,128)(2,1)S(1)}, bf16[128,1,128]{2,0,1:T(8,128)(2,1)S(1)}, u32[]{:S(2)}, u32[]{:S(2)}) collective-permute-start(bf16[128,1,128]{2,0,1:T(8,128)(2,1)S(1)} %copy.67), channel_id=1, source_target_pairs={{0,32},{32,64},{64,96},{96,128},{128,160},{160,192},{192,224},{224... | collective-permute-start | bytes 98312 | tf_op jit(solution)/shard_map/while/body/eval_jaxpr/ppermute | solution.py:15
  66.7 15.1 %collective-permute-start.2 = (s32[1]{0:T(128)}, s32[1]{0:T(128)}, u32[]{:S(2)}, u32[]{:S(2)}) collective-permute-start(s32[1]{0:T(128)} %copy.68), channel_id=1, source_target_pairs={{0,32},{32,64},{64,96},{96,128},{128,160},{160,192},{192,224},{224... | collective-permute-start | bytes 20 | tf_op jit(solution)/shard_map/while/body/eval_jaxpr/ppermute | solution.py:15
  89.6 28.9 %collective-permute-start = (bf16[128,1,128]{2,0,1:T(8,128)(2,1)S(1)}, bf16[128,1,128]{2,0,1:T(8,128)(2,1)S(1)}, u32[]{:S(2)}, u32[]{:S(2)}) collective-permute-start(bf16[128,1,128]{2,0,1:T(8,128)(2,1)S(1)} %copy.66), channel_id=1, source_target_pairs={{0,32},{32,64},{64,96},{96,128},{128,160},{160,192},{192,224},{224... | collective-permute-start | bytes 98312 | tf_op jit(solution)/shard_map/while/body/eval_jaxpr/ppermute | solution.py:15
  94.6 23.9 %collective-permute-start.1 = (bf16[128,1,128]{2,0,1:T(8,128)(2,1)S(1)}, bf16[128,1,128]{2,0,1:T(8,128)(2,1)S(1)}, u32[]{:S(2)}, u32[]{:S(2)}) collective-permute-start(bf16[128,1,128]{2,0,1:T(8,128)(2,1)S(1)} %copy.67), channel_id=1, source_target_pairs={{0,32},{32,64},{64,96},{96,128},{128,160},{160,192},{192,224},{224... | collective-permute-start | bytes 98312 | tf_op jit(solution)/shard_map/while/body/eval_jaxpr/ppermute | solution.py:15
  103.5 15.0 %collective-permute-start.2 = (s32[1]{0:T(128)}, s32[1]{0:T(128)}, u32[]{:S(2)}, u32[]{:S(2)}) collective-permute-start(s32[1]{0:T(128)} %copy.68), channel_id=1, source_target_pairs={{0,32},{32,64},{64,96},{96,128},{128,160},{160,192},{192,224},{224... | collective-permute-start | bytes 20 | tf_op jit(solution)/shard_map/while/body/eval_jaxpr/ppermute | solution.py:15
  125.8 30.1 %collective-permute-start = (bf16[128,1,128]{2,0,1:T(8,128)(2,1)S(1)}, bf16[128,1,128]{2,0,1:T(8,128)(2,1)S(1)}, u32[]{:S(2)}, u32[]{:S(2)}) collective-permute-start(bf16[128,1,128]{2,0,1:T(8,128)(2,1)S(1)} %copy.66), channel_id=1, source_target_pairs={{0,32},{32,64},{64,96},{96,128},{128,160},{160,192},{192,224},{224... | collective-permute-start | bytes 98312 | tf_op jit(solution)/shard_map/while/body/eval_jaxpr/ppermute | solution.py:15
  134.1 21.8 %collective-permute-start.1 = (bf16[128,1,128]{2,0,1:T(8,128)(2,1)S(1)}, bf16[128,1,128]{2,0,1:T(8,128)(2,1)S(1)}, u32[]{:S(2)}, u32[]{:S(2)}) collective-permute-start(bf16[128,1,128]{2,0,1:T(8,128)(2,1)S(1)} %copy.67), channel_id=1, source_target_pairs={{0,32},{32,64},{64,96},{96,128},{128,160},{160,192},{192,224},{224... | collective-permute-start | bytes 98312 | tf_op jit(solution)/shard_map/while/body/eval_jaxpr/ppermute | solution.py:15
  138.2 17.6 %collective-permute-start.2 = (s32[1]{0:T(128)}, s32[1]{0:T(128)}, u32[]{:S(2)}, u32[]{:S(2)}) collective-permute-start(s32[1]{0:T(128)} %copy.68), channel_id=1, source_target_pairs={{0,32},{32,64},{64,96},{96,128},{128,160},{160,192},{192,224},{224... | collective-permute-start | bytes 20 | tf_op jit(solution)/shard_map/while/body/eval_jaxpr/ppermute | solution.py:15
  160.6 30.4 %collective-permute-start = (bf16[128,1,128]{2,0,1:T(8,128)(2,1)S(1)}, bf16[128,1,128]{2,0,1:T(8,128)(2,1)S(1)}, u32[]{:S(2)}, u32[]{:S(2)}) collective-permute-start(bf16[128,1,128]{2,0,1:T(8,128)(2,1)S(1)} %copy.66), channel_id=1, source_target_pairs={{0,32},{32,64},{64,96},{96,128},{128,160},{160,192},{192,224},{224... | collective-permute-start | bytes 98312 | tf_op jit(solution)/shard_map/while/body/eval_jaxpr/ppermute | solution.py:15
  166.6 24.4 %collective-permute-start.1 = (bf16[128,1,128]{2,0,1:T(8,128)(2,1)S(1)}, bf16[128,1,128]{2,0,1:T(8,128)(2,1)S(1)}, u32[]{:S(2)}, u32[]{:S(2)}) collective-permute-start(bf16[128,1,128]{2,0,1:T(8,128)(2,1)S(1)} %copy.67), channel_id=1, source_target_pairs={{0,32},{32,64},{64,96},{96,128},{128,160},{160,192},{192,224},{224... | collective-permute-start | bytes 98312 | tf_op jit(solution)/shard_map/while/body/eval_jaxpr/ppermute | solution.py:15
  173.7 17.4 %collective-permute-start.2 = (s32[1]{0:T(128)}, s32[1]{0:T(128)}, u32[]{:S(2)}, u32[]{:S(2)}) collective-permute-start(s32[1]{0:T(128)} %copy.68), channel_id=1, source_target_pairs={{0,32},{32,64},{64,96},{96,128},{128,160},{160,192},{192,224},{224... | collective-permute-start | bytes 20 | tf_op jit(solution)/shard_map/while/body/eval_jaxpr/ppermute | solution.py:15
  198.3 27.4 %collective-permute-start = (bf16[128,1,128]{2,0,1:T(8,128)(2,1)S(1)}, bf16[128,1,128]{2,0,1:T(8,128)(2,1)S(1)}, u32[]{:S(2)}, u32[]{:S(2)}) collective-permute-start(bf16[128,1,128]{2,0,1:T(8,128)(2,1)S(1)} %copy.66), channel_id=1, source_target_pairs={{0,32},{32,64},{64,96},{96,128},{128,160},{160,192},{192,224},{224... | collective-permute-start | bytes 98312 | tf_op jit(solution)/shard_map/while/body/eval_jaxpr/ppermute | solution.py:15
  201.6 24.1 %collective-permute-start.1 = (bf16[128,1,128]{2,0,1:T(8,128)(2,1)S(1)}, bf16[128,1,128]{2,0,1:T(8,128)(2,1)S(1)}, u32[]{:S(2)}, u32[]{:S(2)}) collective-permute-start(bf16[128,1,128]{2,0,1:T(8,128)(2,1)S(1)} %copy.67), channel_id=1, source_target_pairs={{0,32},{32,64},{64,96},{96,128},{128,160},{160,192},{192,224},{224... | collective-permute-start | bytes 98312 | tf_op jit(solution)/shard_map/while/body/eval_jaxpr/ppermute | solution.py:15
  208.6 17.0 %collective-permute-start.2 = (s32[1]{0:T(128)}, s32[1]{0:T(128)}, u32[]{:S(2)}, u32[]{:S(2)}) collective-permute-start(s32[1]{0:T(128)} %copy.68), channel_id=1, source_target_pairs={{0,32},{32,64},{64,96},{96,128},{128,160},{160,192},{192,224},{224... | collective-permute-start | bytes 20 | tf_op jit(solution)/shard_map/while/body/eval_jaxpr/ppermute | solution.py:15
  233.6 29.4 %collective-permute-start = (bf16[128,1,128]{2,0,1:T(8,128)(2,1)S(1)}, bf16[128,1,128]{2,0,1:T(8,128)(2,1)S(1)}, u32[]{:S(2)}, u32[]{:S(2)}) collective-permute-start(bf16[128,1,128]{2,0,1:T(8,128)(2,1)S(1)} %copy.66), channel_id=1, source_target_pairs={{0,32},{32,64},{64,96},{96,128},{128,160},{160,192},{192,224},{224... | collective-permute-start | bytes 98312 | tf_op jit(solution)/shard_map/while/body/eval_jaxpr/ppermute | solution.py:15
  236.2 26.9 %collective-permute-start.1 = (bf16[128,1,128]{2,0,1:T(8,128)(2,1)S(1)}, bf16[128,1,128]{2,0,1:T(8,128)(2,1)S(1)}, u32[]{:S(2)}, u32[]{:S(2)}) collective-permute-start(bf16[128,1,128]{2,0,1:T(8,128)(2,1)S(1)} %copy.67), channel_id=1, source_target_pairs={{0,32},{32,64},{64,96},{96,128},{128,160},{160,192},{192,224},{224... | collective-permute-start | bytes 98312 | tf_op jit(solution)/shard_map/while/body/eval_jaxpr/ppermute | solution.py:15
  242.8 20.2 %collective-permute-start.2 = (s32[1]{0:T(128)}, s32[1]{0:T(128)}, u32[]{:S(2)}, u32[]{:S(2)}) collective-permute-start(s32[1]{0:T(128)} %copy.68), channel_id=1, source_target_pairs={{0,32},{32,64},{64,96},{96,128},{128,160},{160,192},{192,224},{224... | collective-permute-start | bytes 20 | tf_op jit(solution)/shard_map/while/body/eval_jaxpr/ppermute | solution.py:15
  247.4 15.6 %collective-permute-start.3 = (f32[128,1,128]{2,0,1:T(8,128)S(1)}, f32[128,1,128]{2,0,1:T(8,128)S(1)}, u32[]{:S(2)}, u32[]{:S(2)}) collective-permute-start(f32[128,1,128]{2,0,1:T(8,128)S(1)} %fusion.89), channel_id=1, source_target_pairs={{0,32},{32,64},{64,96},{96,128},{128,160},{160,192},{192,224},{224... | collective-permute-start | bytes 196616 | tf_op jit(solution)/shard_map/while/body/eval_jaxpr/ppermute | solution.py:15
  266.0 31.5 %collective-permute-start = (bf16[128,1,128]{2,0,1:T(8,128)(2,1)S(1)}, bf16[128,1,128]{2,0,1:T(8,128)(2,1)S(1)}, u32[]{:S(2)}, u32[]{:S(2)}) collective-permute-start(bf16[128,1,128]{2,0,1:T(8,128)(2,1)S(1)} %copy.66), channel_id=1, source_target_pairs={{0,32},{32,64},{64,96},{96,128},{128,160},{160,192},{192,224},{224... | collective-permute-start | bytes 98312 | tf_op jit(solution)/shard_map/while/body/eval_jaxpr/ppermute | solution.py:15
  272.8 24.7 %collective-permute-start.1 = (bf16[128,1,128]{2,0,1:T(8,128)(2,1)S(1)}, bf16[128,1,128]{2,0,1:T(8,128)(2,1)S(1)}, u32[]{:S(2)}, u32[]{:S(2)}) collective-permute-start(bf16[128,1,128]{2,0,1:T(8,128)(2,1)S(1)} %copy.67), channel_id=1, source_target_pairs={{0,32},{32,64},{64,96},{96,128},{128,160},{160,192},{192,224},{224... | collective-permute-start | bytes 98312 | tf_op jit(solution)/shard_map/while/body/eval_jaxpr/ppermute | solution.py:15
  279.3 18.2 %collective-permute-start.2 = (s32[1]{0:T(128)}, s32[1]{0:T(128)}, u32[]{:S(2)}, u32[]{:S(2)}) collective-permute-start(s32[1]{0:T(128)} %copy.68), channel_id=1, source_target_pairs={{0,32},{32,64},{64,96},{96,128},{128,160},{160,192},{192,224},{224... | collective-permute-start | bytes 20 | tf_op jit(solution)/shard_map/while/body/eval_jaxpr/ppermute | solution.py:15
  305.3 25.5 %collective-permute-start = (bf16[128,1,128]{2,0,1:T(8,128)(2,1)S(1)}, bf16[128,1,128]{2,0,1:T(8,128)(2,1)S(1)}, u32[]{:S(2)}, u32[]{:S(2)}) collective-permute-start(bf16[128,1,128]{2,0,1:T(8,128)(2,1)S(1)} %copy.66), channel_id=1, source_target_pairs={{0,32},{32,64},{64,96},{96,128},{128,160},{160,192},{192,224},{224... | collective-permute-start | bytes 98312 | tf_op jit(solution)/shard_map/while/body/eval_jaxpr/ppermute | solution.py:15
  308.2 22.6 %collective-permute-start.1 = (bf16[128,1,128]{2,0,1:T(8,128)(2,1)S(1)}, bf16[128,1,128]{2,0,1:T(8,128)(2,1)S(1)}, u32[]{:S(2)}, u32[]{:S(2)}) collective-permute-start(bf16[128,1,128]{2,0,1:T(8,128)(2,1)S(1)} %copy.67), channel_id=1, source_target_pairs={{0,32},{32,64},{64,96},{96,128},{128,160},{160,192},{192,224},{224... | collective-permute-start | bytes 98312 | tf_op jit(solution)/shard_map/while/body/eval_jaxpr/ppermute | solution.py:15
  340.0 27.1 %collective-permute-start = (bf16[128,1,128]{2,0,1:T(8,128)(2,1)S(1)}, bf16[128,1,128]{2,0,1:T(8,128)(2,1)S(1)}, u32[]{:S(2)}, u32[]{:S(2)}) collective-permute-start(bf16[128,1,128]{2,0,1:T(8,128)(2,1)S(1)} %copy.66), channel_id=1, source_target_pairs={{0,32},{32,64},{64,96},{96,128},{128,160},{160,192},{192,224},{224... | collective-permute-start | bytes 98312 | tf_op jit(solution)/shard_map/while/body/eval_jaxpr/ppermute | solution.py:15
  341.9 25.1 %collective-permute-start.1 = (bf16[128,1,128]{2,0,1:T(8,128)(2,1)S(1)}, bf16[128,1,128]{2,0,1:T(8,128)(2,1)S(1)}, u32[]{:S(2)}, u32[]{:S(2)}) collective-permute-start(bf16[128,1,128]{2,0,1:T(8,128)(2,1)S(1)} %copy.67), channel_id=1, source_target_pairs={{0,32},{32,64},{64,96},{96,128},{128,160},{160,192},{192,224},{224... | collective-permute-start | bytes 98312 | tf_op jit(solution)/shard_map/while/body/eval_jaxpr/ppermute | solution.py:15
  349.8 17.2 %collective-permute-start.2 = (s32[1]{0:T(128)}, s32[1]{0:T(128)}, u32[]{:S(2)}, u32[]{:S(2)}) collective-permute-start(s32[1]{0:T(128)} %copy.68), channel_id=1, source_target_pairs={{0,32},{32,64},{64,96},{96,128},{128,160},{160,192},{192,224},{224... | collective-permute-start | bytes 20 | tf_op jit(solution)/shard_map/while/body/eval_jaxpr/ppermute | solution.py:15
  375.7 29.3 %collective-permute-start = (bf16[128,1,128]{2,0,1:T(8,128)(2,1)S(1)}, bf16[128,1,128]{2,0,1:T(8,128)(2,1)S(1)}, u32[]{:S(2)}, u32[]{:S(2)}) collective-permute-start(bf16[128,1,128]{2,0,1:T(8,128)(2,1)S(1)} %copy.66), channel_id=1, source_target_pairs={{0,32},{32,64},{64,96},{96,128},{128,160},{160,192},{192,224},{224... | collective-permute-start | bytes 98312 | tf_op jit(solution)/shard_map/while/body/eval_jaxpr/ppermute | solution.py:15
  378.6 26.4 %collective-permute-start.1 = (bf16[128,1,128]{2,0,1:T(8,128)(2,1)S(1)}, bf16[128,1,128]{2,0,1:T(8,128)(2,1)S(1)}, u32[]{:S(2)}, u32[]{:S(2)}) collective-permute-start(bf16[128,1,128]{2,0,1:T(8,128)(2,1)S(1)} %copy.67), channel_id=1, source_target_pairs={{0,32},{32,64},{64,96},{96,128},{128,160},{160,192},{192,224},{224... | collective-permute-start | bytes 98312 | tf_op jit(solution)/shard_map/while/body/eval_jaxpr/ppermute | solution.py:15
  384.5 20.5 %collective-permute-start.2 = (s32[1]{0:T(128)}, s32[1]{0:T(128)}, u32[]{:S(2)}, u32[]{:S(2)}) collective-permute-start(s32[1]{0:T(128)} %copy.68), channel_id=1, source_target_pairs={{0,32},{32,64},{64,96},{96,128},{128,160},{160,192},{192,224},{224... | collective-permute-start | bytes 20 | tf_op jit(solution)/shard_map/while/body/eval_jaxpr/ppermute | solution.py:15
  410.8 30.8 %collective-permute-start = (bf16[128,1,128]{2,0,1:T(8,128)(2,1)S(1)}, bf16[128,1,128]{2,0,1:T(8,128)(2,1)S(1)}, u32[]{:S(2)}, u32[]{:S(2)}) collective-permute-start(bf16[128,1,128]{2,0,1:T(8,128)(2,1)S(1)} %copy.66), channel_id=1, source_target_pairs={{0,32},{32,64},{64,96},{96,128},{128,160},{160,192},{192,224},{224... | collective-permute-start | bytes 98312 | tf_op jit(solution)/shard_map/while/body/eval_jaxpr/ppermute | solution.py:15
  415.0 26.7 %collective-permute-start.1 = (bf16[128,1,128]{2,0,1:T(8,128)(2,1)S(1)}, bf16[128,1,128]{2,0,1:T(8,128)(2,1)S(1)}, u32[]{:S(2)}, u32[]{:S(2)}) collective-permute-start(bf16[128,1,128]{2,0,1:T(8,128)(2,1)S(1)} %copy.67), channel_id=1, source_target_pairs={{0,32},{32,64},{64,96},{96,128},{128,160},{160,192},{192,224},{224... | collective-permute-start | bytes 98312 | tf_op jit(solution)/shard_map/while/body/eval_jaxpr/ppermute | solution.py:15
  422.8 18.8 %collective-permute-start.2 = (s32[1]{0:T(128)}, s32[1]{0:T(128)}, u32[]{:S(2)}, u32[]{:S(2)}) collective-permute-start(s32[1]{0:T(128)} %copy.68), channel_id=1, source_target_pairs={{0,32},{32,64},{64,96},{96,128},{128,160},{160,192},{192,224},{224... | collective-permute-start | bytes 20 | tf_op jit(solution)/shard_map/while/body/eval_jaxpr/ppermute | solution.py:15
  446.3 26.8 %collective-permute-start = (bf16[128,1,128]{2,0,1:T(8,128)(2,1)S(1)}, bf16[128,1,128]{2,0,1:T(8,128)(2,1)S(1)}, u32[]{:S(2)}, u32[]{:S(2)}) collective-permute-start(bf16[128,1,128]{2,0,1:T(8,128)(2,1)S(1)} %copy.66), channel_id=1, source_target_pairs={{0,32},{32,64},{64,96},{96,128},{128,160},{160,192},{192,224},{224... | collective-permute-start | bytes 98312 | tf_op jit(solution)/shard_map/while/body/eval_jaxpr/ppermute | solution.py:15
  452.8 20.3 %collective-permute-start.1 = (bf16[128,1,128]{2,0,1:T(8,128)(2,1)S(1)}, bf16[128,1,128]{2,0,1:T(8,128)(2,1)S(1)}, u32[]{:S(2)}, u32[]{:S(2)}) collective-permute-start(bf16[128,1,128]{2,0,1:T(8,128)(2,1)S(1)} %copy.67), channel_id=1, source_target_pairs={{0,32},{32,64},{64,96},{96,128},{128,160},{160,192},{192,224},{224... | collective-permute-start | bytes 98312 | tf_op jit(solution)/shard_map/while/body/eval_jaxpr/ppermute | solution.py:15
  482.7 25.7 %collective-permute-start = (bf16[128,1,128]{2,0,1:T(8,128)(2,1)S(1)}, bf16[128,1,128]{2,0,1:T(8,128)(2,1)S(1)}, u32[]{:S(2)}, u32[]{:S(2)}) collective-permute-start(bf16[128,1,128]{2,0,1:T(8,128)(2,1)S(1)} %copy.66), channel_id=1, source_target_pairs={{0,32},{32,64},{64,96},{96,128},{128,160},{160,192},{192,224},{224... | collective-permute-start | bytes 98312 | tf_op jit(solution)/shard_map/while/body/eval_jaxpr/ppermute | solution.py:15
  484.6 23.8 %collective-permute-start.1 = (bf16[128,1,128]{2,0,1:T(8,128)(2,1)S(1)}, bf16[128,1,128]{2,0,1:T(8,128)(2,1)S(1)}, u32[]{:S(2)}, u32[]{:S(2)}) collective-permute-start(bf16[128,1,128]{2,0,1:T(8,128)(2,1)S(1)} %copy.67), channel_id=1, source_target_pairs={{0,32},{32,64},{64,96},{96,128},{128,160},{160,192},{192,224},{224... | collective-permute-start | bytes 98312 | tf_op jit(solution)/shard_map/while/body/eval_jaxpr/ppermute | solution.py:15
  490.0 18.4 %collective-permute-start.2 = (s32[1]{0:T(128)}, s32[1]{0:T(128)}, u32[]{:S(2)}, u32[]{:S(2)}) collective-permute-start(s32[1]{0:T(128)} %copy.68), channel_id=1, source_target_pairs={{0,32},{32,64},{64,96},{96,128},{128,160},{160,192},{192,224},{224... | collective-permute-start | bytes 20 | tf_op jit(solution)/shard_map/while/body/eval_jaxpr/ppermute | solution.py:15
  518.8 25.9 %collective-permute-start = (bf16[128,1,128]{2,0,1:T(8,128)(2,1)S(1)}, bf16[128,1,128]{2,0,1:T(8,128)(2,1)S(1)}, u32[]{:S(2)}, u32[]{:S(2)}) collective-permute-start(bf16[128,1,128]{2,0,1:T(8,128)(2,1)S(1)} %copy.66), channel_id=1, source_target_pairs={{0,32},{32,64},{64,96},{96,128},{128,160},{160,192},{192,224},{224... | collective-permute-start | bytes 98312 | tf_op jit(solution)/shard_map/while/body/eval_jaxpr/ppermute | solution.py:15
  520.7 24.0 %collective-permute-start.1 = (bf16[128,1,128]{2,0,1:T(8,128)(2,1)S(1)}, bf16[128,1,128]{2,0,1:T(8,128)(2,1)S(1)}, u32[]{:S(2)}, u32[]{:S(2)}) collective-permute-start(bf16[128,1,128]{2,0,1:T(8,128)(2,1)S(1)} %copy.67), channel_id=1, source_target_pairs={{0,32},{32,64},{64,96},{96,128},{128,160},{160,192},{192,224},{224... | collective-permute-start | bytes 98312 | tf_op jit(solution)/shard_map/while/body/eval_jaxpr/ppermute | solution.py:15
  523.2 21.5 %collective-permute-start.2 = (s32[1]{0:T(128)}, s32[1]{0:T(128)}, u32[]{:S(2)}, u32[]{:S(2)}) collective-permute-start(s32[1]{0:T(128)} %copy.68), channel_id=1, source_target_pairs={{0,32},{32,64},{64,96},{96,128},{128,160},{160,192},{192,224},{224... | collective-permute-start | bytes 20 | tf_op jit(solution)/shard_map/while/body/eval_jaxpr/ppermute | solution.py:15
  567.0 268.3 %all-reduce.2.cloned.1.call-start = ((), (), s32[]{:S(2)}) async-start(), calls=%async_computation | async-start | bytes 327680 | tf_op jit(solution)/shard_map/psum | solution.py:148
  567.3 70.6 %collective-permute-start.6 = (bf16[128,1,128]{2,0,1:T(8,128)(2,1)S(1)}, bf16[128,1,128]{2,0,1:T(8,128)(2,1)S(1)}, u32[]{:S(2)}, u32[]{:S(2)}) collective-permute-start(bf16[128,1,128]{2,0,1:T(8,128)(2,1)S(1)} %fusion.33), channel_id=1, source_target_pairs={{0,32},{32,64},{64,96},{96,128},{128,160},{160,192},{192,224},{224... | collective-permute-start | bytes 98312 | tf_op jit(solution)/shard_map/ppermute | solution.py:15
  (41 other events, 1141.5 us)
Sparse Core Ops, SparseCore 0:
  567.1 66.7 all-gather.2
  637.4 197.8 all-reduce.1
where the time goes:
time: 848 us; the launch traced here: 845 us
  starting transfers between devices  396 us (47%)
  waiting for transfers between devices  381 us (45%)
  matrix products  19.6 us (2%)
  between operations  14.8 us (2%)
  other arithmetic  12.4 us (1%)
  local copies, waits for them, and re-layouts  10.7 us (1%)
  loops' own time  10.2 us (1%)
    ppermute x77, starting transfers between devices, from_behind(): return lax.ppermute(value, axis, pairs)  396 us
    psum x1, waiting for transfers between devices, local(): grad_wk = lax.psum(summed, 'ctx')  197 us
    ppermute x77, waiting for transfers between devices, from_behind(): return lax.ppermute(value, axis, pairs)  120 us
    all_gather x1, waiting for transfers between devices, local(): piece = lax.all_gather(key_gradient[None], 'fsdp', axis=0, tiled=True)  63.8 us
  transfers between devices with their start and end apart: 79, of which 30 were waited for; matrix products, arithmetic and copies ran while one was open for 4% of the time, Pallas kernels for 0%

commit v1 on v0

v1 whole, which is shorter than its diff:
```python
import jax
import jax.numpy as jnp
from jax import lax
from jax.experimental import pallas as pl
from jax.experimental.pallas import tpu as pltpu
from jax.sharding import Mesh
from jax.sharding import PartitionSpec as P

HEADS = 5
HEAD_SIZE = 128
BLOCK = 128
WIDTH = HEADS * HEAD_SIZE
SIDE = 4
SCALE = HEAD_SIZE ** (-0.5)
CTX = ("x", "zh")
FSDP = ("zl", "y", "c")
Q_ROWS = 2 * BLOCK + 16
KV_ROWS = 2 * BLOCK + 16


def split_parts(value):
    parts = []
    for _ in range(3):
        part = lax.reduce_precision(value, 8, 7)
        parts.append(part.astype(jnp.bfloat16))
        value = value - part
    return parts


def dot(a, b, dims):
    return lax.dot_general(a, b, (dims, ((), ())), preferred_element_type=jnp.float32)


def attention_kernel(q_place, k_place, q_ref, kv_ref, dq_ref, dk_ref, dv_ref, dq_acc, dk_acc, dv_acc):
    dq_acc[...] = jnp.zeros_like(dq_acc)
    dk_acc[...] = jnp.zeros_like(dk_acc)
    dv_acc[...] = jnp.zeros_like(dv_acc)
    key_row = lax.broadcasted_iota(jnp.int32, (BLOCK, BLOCK), 0)
    query_col = lax.broadcasted_iota(jnp.int32, (BLOCK, BLOCK), 1)
    offset = key_row - query_col

    def pair(index, carry):
        j = index // SIDE
        i = index % SIDE
        ahead = (q_place[i] - k_place[j]) * BLOCK

        @pl.when(ahead >= 0)
        def _():
            k = kv_ref[j, :BLOCK, :]
            v = kv_ref[j, BLOCK : 2 * BLOCK, :]
            k_t = k.T
            rows = q_ref[i, 2 * BLOCK :, :].astype(jnp.float32)
            norm = rows[0:1] + rows[1:2] + rows[2:3]
            delta = rows[3:4] + rows[4:5] + rows[5:6]
            visible = offset <= ahead
            dk = dk_acc[j]
            dv = dv_acc[j]
            for h in range(HEADS):
                cols = slice(h * HEAD_SIZE, (h + 1) * HEAD_SIZE)
                q = q_ref[i, :BLOCK, cols]
                g = q_ref[i, BLOCK : 2 * BLOCK, cols]
                scores = dot(k, q, ((1,), (1,))) * SCALE
                probs = jnp.where(visible, jnp.exp(scores - norm[:, cols]), 0.0)
                dprobs = dot(v, g, ((1,), (1,)))
                dscores = (probs * (dprobs - delta[:, cols]) * SCALE).astype(jnp.bfloat16)
                dk = dk + dot(dscores, q, ((1,), (0,)))
                dv = dv + dot(probs.astype(jnp.bfloat16), g, ((1,), (0,)))
                dq_acc[i, :, cols] += dot(k_t, dscores, ((1,), (0,)))
            dk_acc[j] = dk
            dv_acc[j] = dv

        return carry

    lax.fori_loop(0, SIDE * SIDE, pair, 0)
    dq_ref[...] = dq_acc[...].astype(jnp.bfloat16)
    dk_ref[...] = dk_acc[...].astype(jnp.bfloat16)
    dv_ref[...] = dv_acc[...].astype(jnp.bfloat16)


def attention_grads(q_place, k_place, q_all, kv_all):
    smem = pl.BlockSpec(memory_space=pltpu.SMEM)
    vmem = pl.BlockSpec(memory_space=pltpu.VMEM)
    return pl.pallas_call(
        attention_kernel,
        out_shape=(
            jax.ShapeDtypeStruct((SIDE, HEAD_SIZE, WIDTH), jnp.bfloat16),
            jax.ShapeDtypeStruct((SIDE, BLOCK, HEAD_SIZE), jnp.bfloat16),
            jax.ShapeDtypeStruct((SIDE, BLOCK, HEAD_SIZE), jnp.bfloat16),
        ),
        in_specs=[smem, smem, vmem, vmem],
        out_specs=(vmem, vmem, vmem),
        scratch_shapes=[
            pltpu.VMEM((SIDE, HEAD_SIZE, WIDTH), jnp.float32),
            pltpu.VMEM((SIDE, BLOCK, HEAD_SIZE), jnp.float32),
            pltpu.VMEM((SIDE, BLOCK, HEAD_SIZE), jnp.float32),
        ],
        name="attention_grads",
    )(q_place, k_place, q_all, kv_all)


def share(value, axis):
    count = lax.axis_size(axis)
    return lax.all_to_all(
        jnp.broadcast_to(value[None], (count,) + value.shape), axis, 0, 0, tiled=True
    )


def swap_sum(value, axis):
    got = lax.all_to_all(value, axis, 0, 0, tiled=True)
    return jnp.sum(got.astype(jnp.float32), axis=0)


def local(block_pos, queries, keys, values, attention_output, output_gradient, log_softmax_norm, features):
    sequence = lax.axis_index("zl") * 2 + lax.axis_index("y") // 2
    place = lax.dynamic_slice_in_dim(block_pos, sequence, 1, 0)[0, 0].astype(jnp.bfloat16)
    gradient = output_gradient[0]
    product = gradient.astype(jnp.float32) * attention_output[0].astype(jnp.float32)
    delta = jnp.sum(product.reshape(BLOCK, HEADS, HEAD_SIZE), axis=-1).T.reshape(WIDTH)
    norm = log_softmax_norm[0].reshape(WIDTH)
    place_row = jnp.full((WIDTH,), place)
    extra = jnp.stack(split_parts(norm) + split_parts(delta) + [place_row] * 10)
    q_own = jnp.concatenate([queries[0], gradient, extra], axis=0)
    kv_own = jnp.concatenate(
        [keys[0], values[0], jnp.full((16, HEAD_SIZE), place)], axis=0
    )
    kv_all = share(kv_own, "zh")
    q_all = share(q_own, "x")
    q_place = q_all[:, 2 * BLOCK + 6, 0].astype(jnp.int32)
    k_place = kv_all[:, 2 * BLOCK, 0].astype(jnp.int32)
    dq, dk, dv = attention_grads(q_place, k_place, q_all, kv_all)

    key_gradient = swap_sum(dk, "zh").astype(jnp.bfloat16)
    grad_q = swap_sum(dq, "x")
    grad_q = grad_q.reshape(HEAD_SIZE, HEADS, BLOCK).transpose(2, 1, 0).reshape(BLOCK, WIDTH)
    value_gradient = swap_sum(dv, "zh").astype(jnp.bfloat16)

    gathered = share(key_gradient, "zl")
    gathered = share(gathered, "y")
    gathered = share(gathered, "c")
    gathered = gathered.reshape(2, 2, 2, 4, BLOCK, HEAD_SIZE)
    own = features.reshape(4, 2, BLOCK, features.shape[-1])
    partial = jnp.einsum("zhtf,chlztj->lcfj", own, gathered, preferred_element_type=jnp.float32)
    partial = partial.reshape(4, features.shape[-1], HEAD_SIZE)
    mine = swap_sum(partial.astype(jnp.bfloat16), "x")
    mine = jnp.sum(share(mine.astype(jnp.bfloat16), "zh").astype(jnp.float32), axis=0)
    grad_wk = share(mine, "x").transpose(1, 0, 2).reshape(features.shape[-1], 4 * HEAD_SIZE)
    return (grad_q.astype(jnp.bfloat16)[None], key_gradient[None], value_gradient[None], grad_wk)


def solution(mesh):
    fine = Mesh(mesh.devices.reshape(4, 4, 4, 4, 2), CTX + FSDP)
    return jax.shard_map(
        local,
        mesh=fine,
        in_specs=(
            P(None, CTX),
            P(FSDP, CTX, None),
            P(FSDP, CTX, None),
            P(FSDP, CTX, None),
            P(FSDP, CTX, None),
            P(FSDP, CTX, None),
            P(FSDP, None, CTX),
            P(None, CTX, FSDP),
        ),
        out_specs=(P(FSDP, CTX, None), P(FSDP, CTX, None), P(FSDP, CTX, None), P(FSDP, None)),
        check_vma=False,
    )
```

time: 848 us -> 190 us (0.22)
  starting transfers between devices: 396 us -> 32.9 us
  waiting for transfers between devices: 381 us -> 51.8 us
  blocking collectives: 0 us -> 77.4 us
  matrix products: 19.6 us -> 0.31 us
  between operations: 14.8 us -> 0.85 us
  Pallas kernels: 0 us -> 13.2 us
  loops' own time: 10.2 us -> 0 us
    ppermute x77 -> x0, starting transfers between devices: 396 us -> none  [from_behind(): return lax.ppermute(value, axis, pairs)]
    psum x1 -> x0, waiting for transfers between devices: 197 us -> none  [local(): grad_wk = lax.psum(summed, 'ctx')]
    ppermute x77 -> x0, waiting for transfers between devices: 120 us -> none  [from_behind(): return lax.ppermute(value, axis, pairs)]
    all_to_all x0 -> x6, blocking collectives: none -> 77.4 us  [the longest x4 46.1 us: share(): lax.all_to_all(jnp.broadcast_to(value[None], (count,) + value.shape), axi...]
    all_gather x1 -> x0, waiting for transfers between devices: 63.8 us -> none  [local(): piece = lax.all_gather(key_gradient[None], 'fsdp', axis=0, tiled=True)]
    all_to_all x0 -> x5, waiting for transfers between devices: none -> 51.8 us  [the longest x3 30.8 us: share(): lax.all_to_all(jnp.broadcast_to(value[None], (count,) + value.shape), axi...]
    all_to_all x0 -> x5, starting transfers between devices: none -> 32.9 us  [the longest x3 24.7 us: share(): lax.all_to_all(jnp.broadcast_to(value[None], (count,) + value.shape), axi...]
    dot_general x82 -> x1, matrix products: 19.6 us -> 0.31 us  [local(): jnp.einsum('zhtf,chlztj->lcfj', own, gathered, preferred_element_type=jnp...]
  transfers between devices with their start and end apart: 79 -> 5, of which waited for: 30 -> 5; matrix products, arithmetic and copies ran while one was open for 4% -> 3% of each run, Pallas kernels for 0% -> 0%
where the time goes in v1:
time: 190 us; the launch traced here: 189 us
  blocking collectives  77.4 us (41%)
  waiting for transfers between devices  51.8 us (27%)
  starting transfers between devices  32.9 us (17%)
  Pallas kernels  13.2 us (7%)
  local copies, waits for them, and re-layouts  8.02 us (4%)
  other arithmetic  4.58 us (2%)
    all_to_all x4, blocking collectives, share(): lax.all_to_all(jnp.broadcast_to(value[None], (count,) + value.shape), axi...  46.1 us
    all_to_all x2, blocking collectives, swap_sum(): got = lax.all_to_all(value, axis, 0, 0, tiled=True)  31.3 us
    all_to_all x3, waiting for transfers between devices, share(): lax.all_to_all(jnp.broadcast_to(value[None], (count,) + value.shape), axi...  30.8 us
    all_to_all x3, starting transfers between devices, share(): lax.all_to_all(jnp.broadcast_to(value[None], (count,) + value.shape), axi...  24.7 us
    all_to_all x2, waiting for transfers between devices, swap_sum(): got = lax.all_to_all(value, axis, 0, 0, tiled=True)  21 us
    pallas_call x1, Pallas kernels, attention_grads(): pl.pallas_call(attention_kernel, out_shape=(jax.ShapeDtypeStruct((SIDE, H...  13.2 us
    all_to_all x2, starting transfers between devices, swap_sum(): got = lax.all_to_all(value, axis, 0, 0, tiled=True)  8.21 us
  transfers between devices with their start and end apart: 5, of which 5 were waited for; matrix products, arithmetic and copies ran while one was open for 3% of the time, Pallas kernels for 0%

profile of v1, /device:TPU:2, one launch (start us, length us, event | category | flops | bytes accessed | tf_op | source)
XLA Modules:
  0.0 189.0 jit_solution(13155887748435856419)
XLA Ops:
  0.6 0.0 copy-start.2
  0.6 0.0 copy-start.5
  0.7 0.0 copy-start.3
  0.7 1.3 fusion.9
  2.0 0.6 broadcast_in_dim.21
  2.7 0.9 maximum_maximum_fusion
  3.6 0.7 broadcast_in_dim.22
  4.3 15.1 %all-to-all-start.1 = ((bf16[4,272,128]{2,1,0:T(8,128)(2,1)}), bf16[4,272,128]{2,1,0:T(8,128)(2,1)S(1)}, u32[]{:S(2)}, u32[]{:S(2)}) async-start(bf16[4,272,128]{2,1,0:T(8,128)(2,1)} %broadcast_in_dim.22), calls=%async_computation.1 | async-start | bytes 557056 | tf_op jit(solution)/shard_map/all_to_all | solution.py:103
  19.4 1.1 copy.37
  20.5 0.0 copy-done.2
  20.5 0.2 copy.36
  20.7 0.0 copy-done.5
  20.8 0.7 stack_broadcast_in_dim.2
  21.4 0.3 concatenate.6
  21.7 16.5 %all-to-all-done.1.kv_ref = bf16[4,272,128]{2,1,0:T(8,128)(2,1)S(1)} async-done(((bf16[4,272,128]{2,1,0:T(8,128)(2,1)}), bf16[4,272,128]{2,1,0:T(8,128)(2,1)S(1)}, u32[]{:S(2)}, u32[]{:S(2)}) %all-to-all-start.1) | async-done | bytes 278560 | tf_op jit(solution)/shard_map/all_to_all | solution.py:103
  38.2 1.2 broadcast_in_dim.20
  39.4 4.8 %all-to-all-start = ((bf16[4,272,640]{2,1,0:T(8,128)(2,1)}), bf16[4,272,640]{2,1,0:T(8,128)(2,1)S(1)}, u32[]{:S(2)}, u32[]{:S(2)}) async-start(bf16[4,272,640]{2,1,0:T(8,128)(2,1)} %broadcast_in_dim.20), calls=%async_computation | async-start | bytes 2785280 | tf_op jit(solution)/shard_map/all_to_all | solution.py:103
  44.2 0.0 copy-done.1
  44.2 0.7 fusion.7.k_place
  44.9 11.6 %all-to-all-done.q_ref = bf16[4,272,640]{2,1,0:T(8,128)(2,1)S(1)} async-done(((bf16[4,272,640]{2,1,0:T(8,128)(2,1)}), bf16[4,272,640]{2,1,0:T(8,128)(2,1)S(1)}, u32[]{:S(2)}, u32[]{:S(2)}) %all-to-all-start) | async-done | bytes 1392672 | tf_op jit(solution)/shard_map/all_to_all | solution.py:103
  56.5 0.8 fusion.8.q_place
  57.3 0.3 copy-done
  57.6 13.2 %attention_grads.1 = (bf16[4,128,640]{2,1,0:T(8,128)(2,1)}, bf16[4,128,128]{2,1,0:T(8,128)(2,1)}, bf16[4,128,128]{2,1,0:T(8,128)(2,1)}) custom-call(s32[4]{0:T(128)} %fusion.8.q_place, s32[4]{0:T(128)} %fusion.7.k_place, bf16[4,272,640]{2,1,0:T(8,128)(2,1)} %copy-done, bf16[4,272,128]{2,1,0:T(8,128)(2,1)} %copy-done.1), custom_call_target="tpu_custom_call" | custom-call | tf_op jit(solution)/shard_map/attention_grads/pallas_call | solution.py:83
  70.8 20.5 %all_to_all.55 = bf16[4,128,128]{2,1,0:T(8,128)(2,1)S(1)} all-to-all(bf16[4,128,128]{2,1,0:T(8,128)(2,1)} %get-tuple-element.8), channel_id=1, replica_groups=mesh['x'=4,'zh'=4,'zl'=4,'y'=4,'c'=2] {'zh'}, dimensions={0} | all-to-all | bytes 262144 | tf_op jit(solution)/shard_map/all_to_all | solution.py:109
  91.3 0.0 copy-start.4
  91.4 11.4 %all_to_all.56 = bf16[4,128,128]{2,1,0:T(8,128)(2,1)S(1)} all-to-all(bf16[4,128,128]{2,1,0:T(8,128)(2,1)S(1)} %broadcast_in_dim.25), channel_id=1, replica_groups=mesh['x'=4,'zh'=4,'zl'=4,'y'=4,'c'=2] {'zl'}, dimensions={0} | all-to-all | bytes 262144 | tf_op jit(solution)/shard_map/all_to_all | solution.py:103
  102.8 0.1 broadcast_in_dim.26
  102.9 12.5 %all_to_all.57 = bf16[4,4,128,128]{3,2,1,0:T(8,128)(2,1)S(1)} all-to-all(bf16[4,4,128,128]{3,2,1,0:T(8,128)(2,1)S(1)} %broadcast_in_dim.26), channel_id=1, replica_groups=mesh['x'=4,'zh'=4,'zl'=4,'y'=4,'c'=2] {'y'}, dimensions={0} | all-to-all | bytes 1048576 | tf_op jit(solution)/shard_map/all_to_all | solution.py:103
  115.4 0.3 broadcast_in_dim.27
  115.7 0.0 copy-start.6
  115.7 4.7 %all_to_all.58 = bf16[2,4,4,128,128]{4,3,2,1,0:T(8,128)(2,1)S(1)} all-to-all(bf16[2,4,4,128,128]{4,3,2,1,0:T(8,128)(2,1)S(1)} %broadcast_in_dim.27), channel_id=1, replica_groups=mesh['x'=4,'zh'=4,'zl'=4,'y'=4,'c'=2] {'c'}, dimensions={0} | all-to-all | bytes 2097152 | tf_op jit(solution)/shard_map/all_to_all | solution.py:103
  120.5 0.0 copy-done.6
  120.5 0.3 fusion
  120.8 10.7 %all_to_all.59 = bf16[4,80,128]{2,1,0:T(8,128)(2,1)S(1)} all-to-all(bf16[4,80,128]{2,1,0:T(8,128)(2,1)S(1)} %bitcast.50), channel_id=1, replica_groups=mesh['x'=4,'zh'=4,'zl'=4,'y'=4,'c'=2] {'x'}, dimensions={0} | all-to-all | bytes 163840 | tf_op jit(solution)/shard_map/all_to_all | solution.py:109
  131.5 3.3 %all-to-all-start.4 = ((bf16[4,128,128]{2,1,0:T(8,128)(2,1)}), bf16[4,128,128]{2,1,0:T(8,128)(2,1)S(1)}, u32[]{:S(2)}, u32[]{:S(2)}) async-start(bf16[4,128,128]{2,1,0:T(8,128)(2,1)} %get-tuple-element.9), calls=%async_computation.4 | async-start | bytes 262144 | tf_op jit(solution)/shard_map/all_to_all | solution.py:109
  134.9 13.6 %all-to-all-done.4 = bf16[4,128,128]{2,1,0:T(8,128)(2,1)S(1)} async-done(((bf16[4,128,128]{2,1,0:T(8,128)(2,1)}), bf16[4,128,128]{2,1,0:T(8,128)(2,1)S(1)}, u32[]{:S(2)}, u32[]{:S(2)}) %all-to-all-start.4) | async-done | bytes 131104 | tf_op jit(solution)/shard_map/all_to_all | solution.py:109
  148.5 17.4 %all_to_all.60 = bf16[4,80,128]{2,1,0:T(8,128)(2,1)S(1)} all-to-all(bf16[4,80,128]{2,1,0:T(8,128)(2,1)S(1)} %broadcast_in_dim.28), channel_id=1, replica_groups=mesh['x'=4,'zh'=4,'zl'=4,'y'=4,'c'=2] {'zh'}, dimensions={0} | all-to-all | bytes 163840 | tf_op jit(solution)/shard_map/all_to_all | solution.py:103
  166.0 4.9 %all-to-all-start.2 = ((bf16[4,128,640]{2,1,0:T(8,128)(2,1)}), bf16[4,128,640]{2,1,0:T(8,128)(2,1)S(1)}, u32[]{:S(2)}, u32[]{:S(2)}) async-start(bf16[4,128,640]{2,1,0:T(8,128)(2,1)} %get-tuple-element.7), calls=%async_computation.2 | async-start | bytes 1310720 | tf_op jit(solution)/shard_map/all_to_all | solution.py:109
  170.9 7.3 %all-to-all-done.2 = bf16[4,128,640]{2,1,0:T(8,128)(2,1)S(1)} async-done(((bf16[4,128,640]{2,1,0:T(8,128)(2,1)}), bf16[4,128,640]{2,1,0:T(8,128)(2,1)S(1)}, u32[]{:S(2)}, u32[]{:S(2)}) %all-to-all-start.2) | async-done | bytes 655392 | tf_op jit(solution)/shard_map/all_to_all | solution.py:109
  178.2 0.7 broadcast_in_dim.29
  178.8 4.8 %all-to-all-start.10 = ((f32[4,80,128]{2,1,0:T(8,128)}), f32[4,80,128]{2,1,0:T(8,128)S(1)}, u32[]{:S(2)}, u32[]{:S(2)}) async-start(f32[4,80,128]{2,1,0:T(8,128)} %broadcast_in_dim.29), calls=%async_computation.10 | async-start | bytes 327680 | tf_op jit(solution)/shard_map/all_to_all | solution.py:103
  183.6 0.6 reduce_sum.69
  184.3 0.1 reduce_sum.67
  184.4 0.2 copy.38
  184.5 0.2 copy.39
  184.7 0.8 copy.43
  185.5 2.8 %all-to-all-done.10 = f32[4,80,128]{2,1,0:T(8,128)S(1)} async-done(((f32[4,80,128]{2,1,0:T(8,128)}), f32[4,80,128]{2,1,0:T(8,128)S(1)}, u32[]{:S(2)}, u32[]{:S(2)}) %all-to-all-start.10) | async-done | bytes 163872 | tf_op jit(solution)/shard_map/all_to_all | solution.py:103
  188.3 0.7 copy_bitcast_fusion
  (14 shorter events, 0.2 us)
Async XLA Ops:
  0.6 19.8 %copy-start.2 = (bf16[1,128,640]{2,1,0:T(8,128)(2,1)S(1)}, bf16[1,128,640]{2,1,0:T(8,128)(2,1)}, u32[]{:S(2)}) copy-start(bf16[1,128,640]{2,1,0:T(8,128)(2,1)} %param.13) | copy-start | bytes 491524
  0.6 20.1 %copy-start.5 = (f32[1,5,128]{2,0,1:T(1,128)S(1)}, f32[1,5,128]{2,0,1:T(1,128)}, u32[]{:S(2)}) copy-start(f32[1,5,128]{2,0,1:T(1,128)} %param.14) | copy-start | bytes 7684
  0.7 20.8 %copy-start.3 = (bf16[1,128,640]{2,1,0:T(8,128)(2,1)S(1)}, bf16[1,128,640]{2,1,0:T(8,128)(2,1)}, u32[]{:S(2)}) copy-start(bf16[1,128,640]{2,1,0:T(8,128)(2,1)} %param.9) | copy-start | bytes 491524
  4.3 33.9 %all-to-all-start.1 = ((bf16[4,272,128]{2,1,0:T(8,128)(2,1)}), bf16[4,272,128]{2,1,0:T(8,128)(2,1)S(1)}, u32[]{:S(2)}, u32[]{:S(2)}) async-start(bf16[4,272,128]{2,1,0:T(8,128)(2,1)} %broadcast_in_dim.22), calls=%async_computation.1 | async-start | bytes 557056 | tf_op jit(solution)/shard_map/all_to_all | solution.py:103
  38.2 6.0 %copy-start.1 = (bf16[4,272,128]{2,1,0:T(8,128)(2,1)}, bf16[4,272,128]{2,1,0:T(8,128)(2,1)S(1)}, u32[]{:S(2)}) copy-start(bf16[4,272,128]{2,1,0:T(8,128)(2,1)S(1)} %all-to-all-done.1.kv_ref) | copy-start | bytes 835588
  39.4 17.1 %all-to-all-start = ((bf16[4,272,640]{2,1,0:T(8,128)(2,1)}), bf16[4,272,640]{2,1,0:T(8,128)(2,1)S(1)}, u32[]{:S(2)}, u32[]{:S(2)}) async-start(bf16[4,272,640]{2,1,0:T(8,128)(2,1)} %broadcast_in_dim.20), calls=%async_computation | async-start | bytes 2785280 | tf_op jit(solution)/shard_map/all_to_all | solution.py:103
  56.5 1.1 copy-start
  91.3 24.4 %copy-start.4 = (bf16[128,128]{1,0:T(8,128)(2,1)}, bf16[128,128]{1,0:T(8,128)(2,1)S(1)}, u32[]{:S(2)}) copy-start(bf16[128,128]{1,0:T(8,128)(2,1)S(1)} %reduce_sum.68) | copy-start | bytes 98308
  115.7 4.7 %copy-start.6 = (bf16[8,128,80]{1,2,0:T(8,128)(2,1)S(1)}, bf16[8,128,80]{1,2,0:T(8,128)(2,1)}, u32[]{:S(2)}) copy-start(bf16[8,128,80]{1,2,0:T(8,128)(2,1)} %param.15) | copy-start | bytes 491524
  131.5 17.0 %all-to-all-start.4 = ((bf16[4,128,128]{2,1,0:T(8,128)(2,1)}), bf16[4,128,128]{2,1,0:T(8,128)(2,1)S(1)}, u32[]{:S(2)}, u32[]{:S(2)}) async-start(bf16[4,128,128]{2,1,0:T(8,128)(2,1)} %get-tuple-element.9), calls=%async_computation.4 | async-start | bytes 262144 | tf_op jit(solution)/shard_map/all_to_all | solution.py:109
  166.0 12.2 %all-to-all-start.2 = ((bf16[4,128,640]{2,1,0:T(8,128)(2,1)}), bf16[4,128,640]{2,1,0:T(8,128)(2,1)S(1)}, u32[]{:S(2)}, u32[]{:S(2)}) async-start(bf16[4,128,640]{2,1,0:T(8,128)(2,1)} %get-tuple-element.7), calls=%async_computation.2 | async-start | bytes 1310720 | tf_op jit(solution)/shard_map/all_to_all | solution.py:109
  178.8 9.5 %all-to-all-start.10 = ((f32[4,80,128]{2,1,0:T(8,128)}), f32[4,80,128]{2,1,0:T(8,128)S(1)}, u32[]{:S(2)}, u32[]{:S(2)}) async-start(f32[4,80,128]{2,1,0:T(8,128)} %broadcast_in_dim.29), calls=%async_computation.10 | async-start | bytes 327680 | tf_op jit(solution)/shard_map/all_to_all | solution.py:103

commit v2 on v1

v2 whole, which is shorter than its diff:
```python
import jax
import jax.numpy as jnp
from jax import lax
from jax.experimental import pallas as pl
from jax.experimental.pallas import tpu as pltpu
from jax.sharding import Mesh
from jax.sharding import PartitionSpec as P


HEADS = 5
HEAD_SIZE = 128
BLOCK = 128
STACK = HEADS * BLOCK
SIDE = 4
SCALE = HEAD_SIZE ** (-0.5)
CTX = ("x", "zh")
FSDP = ("zl", "yh", "yl", "c")
PIECE = 24
Q_ROWS = 2 * STACK + 32
KV_ROWS = 2 * BLOCK + 16


def dot(a, b, dims):
    return lax.dot_general(a, b, (dims, ((), ())), preferred_element_type=jnp.float32)


def parts_of(value):
    first = value.astype(jnp.bfloat16)
    value = value - first.astype(jnp.float32)
    second = value.astype(jnp.bfloat16)
    value = value - second.astype(jnp.float32)
    return [first.astype(jnp.float32), second.astype(jnp.float32), value]


def own_place(places):
    return places[lax.axis_index("zl") * 2 + lax.axis_index("yh"), 0]


def key_pack_kernel(places, k_ref, v_ref, out_ref):
    tail = jnp.full((16, HEAD_SIZE), own_place(places), jnp.int32)
    tail = tail.astype(jnp.float32).astype(jnp.bfloat16)
    for copy in range(SIDE):
        out_ref[copy, :BLOCK, :] = k_ref[0]
        out_ref[copy, BLOCK : 2 * BLOCK, :] = v_ref[0]
        out_ref[copy, 2 * BLOCK :, :] = tail


def query_pack_kernel(places, q_ref, g_ref, o_ref, norm_ref, out_ref):
    deltas = []
    for h in range(HEADS):
        cols = slice(h * HEAD_SIZE, (h + 1) * HEAD_SIZE)
        rows = slice(h * BLOCK, (h + 1) * BLOCK)
        out_ref[rows, :] = q_ref[0, :, cols]
        g = g_ref[0, :, cols]
        out_ref[STACK + h * BLOCK : STACK + (h + 1) * BLOCK, :] = g
        product = g.astype(jnp.float32) * o_ref[0, :, cols].astype(jnp.float32)
        deltas.append(jnp.sum(product.T, axis=0, keepdims=True))
    delta = jnp.concatenate(deltas, axis=0)
    tail = jnp.full((2, HEAD_SIZE), own_place(places), jnp.int32).astype(jnp.float32)
    extra = jnp.concatenate(parts_of(norm_ref[0]) + parts_of(delta) + [tail], axis=0)
    out_ref[2 * STACK :, :] = extra.astype(jnp.bfloat16)


def place_of(rows):
    return jnp.max(rows.astype(jnp.float32)).astype(jnp.int32)


def attention_kernel(
    q0, q1, q2, q3, kv_ref, dq0, dq1, dq2, dq3, dk_ref, dv_ref, dq_acc, dk_acc, dv_acc, k_t, k_place
):
    dk_acc[...] = jnp.zeros_like(dk_acc)
    dv_acc[...] = jnp.zeros_like(dv_acc)
    key_row = lax.broadcasted_iota(jnp.int32, (BLOCK, STACK), 0)
    query_col = lax.broadcasted_iota(jnp.int32, (BLOCK, STACK), 1) & (BLOCK - 1)
    offset = key_row - query_col
    for j in range(SIDE):
        k_t[j] = kv_ref[j, :BLOCK, :].T
        k_place[j] = place_of(kv_ref[j, 2 * BLOCK :, :])
    for q_ref, dq_ref in ((q0, dq0), (q1, dq1), (q2, dq2), (q3, dq3)):
        dq_acc[...] = jnp.zeros_like(dq_acc)
        extra = q_ref[2 * STACK :, :].astype(jnp.float32)
        norm = extra[0:5] + extra[5:10] + extra[10:15]
        delta = extra[15:20] + extra[20:25] + extra[25:30]
        norm = jnp.concatenate([norm[h : h + 1] for h in range(HEADS)], axis=1)
        delta = jnp.concatenate([delta[h : h + 1] for h in range(HEADS)], axis=1)
        here = place_of(q_ref[2 * STACK + 16 :, :][14:])

        def pair(j, carry):
            ahead = (here - k_place[j]) * BLOCK

            @pl.when(ahead >= 0)
            def _():
                q = q_ref[:STACK, :]
                g = q_ref[STACK : 2 * STACK, :]
                scores = dot(kv_ref[j, :BLOCK, :], q, ((1,), (1,))) * SCALE
                probs = jnp.where(offset <= ahead, jnp.exp(scores - norm), 0.0)
                dprobs = dot(kv_ref[j, BLOCK : 2 * BLOCK, :], g, ((1,), (1,)))
                dscores = (probs * (dprobs - delta) * SCALE).astype(jnp.bfloat16)
                dv_acc[j] += dot(probs.astype(jnp.bfloat16), g, ((1,), (0,)))
                dk_acc[j] += dot(dscores, q, ((1,), (0,)))
                dq_acc[...] += dot(k_t[j], dscores, ((1,), (0,)))

            return carry

        lax.fori_loop(0, SIDE, pair, 0)
        dq_ref[...] = dq_acc[...].astype(jnp.bfloat16)
    dk_ref[...] = dk_acc[...].astype(jnp.bfloat16)
    ring = lax.axis_index("zh")
    for j in range(SIDE):
        dv_ref[j] = dv_acc[(ring + j) % SIDE].astype(jnp.bfloat16)


SMEM = pl.BlockSpec(memory_space=pltpu.SMEM)
VMEM = pl.BlockSpec(memory_space=pltpu.VMEM)


def struct(shape, dtype=jnp.bfloat16):
    return jax.ShapeDtypeStruct(shape, dtype)


def pack_keys(places, keys, values):
    return pl.pallas_call(
        key_pack_kernel,
        out_shape=struct((SIDE, KV_ROWS, HEAD_SIZE)),
        in_specs=[SMEM, VMEM, VMEM],
        out_specs=VMEM,
        name="pack_keys",
    )(places, keys, values)


def pack_queries(places, queries, gradient, output, norm):
    return pl.pallas_call(
        query_pack_kernel,
        out_shape=struct((Q_ROWS, HEAD_SIZE)),
        in_specs=[SMEM] + [VMEM] * 4,
        out_specs=VMEM,
        name="pack_queries",
    )(places, queries, gradient, output, norm)


def attention_grads(q_parts, kv_all):
    return pl.pallas_call(
        attention_kernel,
        out_shape=(struct((HEAD_SIZE, STACK)),) * 4 + (struct((SIDE, BLOCK, HEAD_SIZE)),) * 2,
        in_specs=[VMEM] * 5,
        out_specs=(VMEM,) * 6,
        scratch_shapes=[
            pltpu.VMEM((HEAD_SIZE, STACK), jnp.float32),
            pltpu.VMEM((SIDE, BLOCK, HEAD_SIZE), jnp.float32),
            pltpu.VMEM((SIDE, BLOCK, HEAD_SIZE), jnp.float32),
            pltpu.VMEM((SIDE, HEAD_SIZE, BLOCK), jnp.bfloat16),
            pltpu.SMEM((SIDE,), jnp.int32),
        ],
        name="attention_grads",
    )(*q_parts, kv_all)


def ahead(value, axis, steps):
    count = lax.axis_size(axis)
    pairs = [(source, (source + steps) % count) for source in range(count)]
    return lax.ppermute(value, axis, pairs)


def swap(value, axis):
    return lax.all_to_all(value, axis, 0, 0, tiled=True)


def copies(value, count):
    return jnp.broadcast_to(value[None], (count,) + value.shape)


def total(parts):
    return jnp.sum(parts.astype(jnp.float32), axis=0)


def padded_features(features):
    ft = features.transpose(0, 2, 1)
    ft = ahead_pair(ft, "c")
    ft = ahead_pair(ft, "yl")
    rows = features.shape[-1] // SIDE
    ft = ft.reshape(SIDE, 8, SIDE, rows, BLOCK)
    ft = jnp.pad(ft, ((0, 0), (0, 0), (0, 0), (0, PIECE - rows), (0, 0)))
    return ft.transpose(1, 2, 0, 3, 4).reshape(8, SIDE * SIDE * PIECE, BLOCK)


def ahead_pair(value, axis):
    other = ahead(value, axis, 1)
    first = lax.axis_index(axis) == 0
    return jnp.stack([jnp.where(first, value, other), jnp.where(first, other, value)])


def whole(block_pos, queries, keys, values, attention_output, output_gradient, log_softmax_norm, features):
    kv_own = pack_keys(block_pos, keys, values)
    kv_all = swap(kv_own, "zh")
    q_own = pack_queries(block_pos, queries, output_gradient, attention_output, log_softmax_norm)
    q_parts = [q_own] + [ahead(q_own, "x", s) for s in (1, 2, 3)]
    *dq, dk, dv = attention_grads(q_parts, kv_all)

    key_gradient = total(swap(dk, "zh")).astype(jnp.bfloat16)
    dq = [dq[0]] + [ahead(dq[s], "x", -s) for s in (1, 2, 3)]
    grad_q = total(jnp.stack(dq))
    grad_q = grad_q.reshape(HEAD_SIZE, HEADS, BLOCK).transpose(2, 1, 0).reshape(BLOCK, STACK)
    dv = [dv[0]] + [ahead(dv[s], "zh", s) for s in (1, 2, 3)]
    value_gradient = total(jnp.stack(dv)).astype(jnp.bfloat16)

    weights = padded_features(features)
    gathered = swap(copies(key_gradient, 8), ("zl", "yh"))
    partial = jnp.einsum("smt,stj->mj", weights, gathered, preferred_element_type=jnp.float32)
    partial = partial.astype(jnp.bfloat16).reshape(SIDE, SIDE * PIECE, HEAD_SIZE)
    mine = total(swap(partial, "x"))
    mine = total(swap(copies(mine.astype(jnp.bfloat16), SIDE), "zh"))
    out = swap(copies(mine, SIDE).reshape(16, PIECE, HEAD_SIZE), ("x", "yl", "c"))
    width = features.shape[-1]
    out = out.reshape(SIDE, SIDE, PIECE, HEAD_SIZE)[:, :, : width // SIDE]
    grad_wk = out.transpose(0, 2, 1, 3).reshape(width, SIDE * HEAD_SIZE)
    return (grad_q.astype(jnp.bfloat16)[None], key_gradient[None], value_gradient[None], grad_wk)


def solution(mesh):
    fine = Mesh(mesh.devices.reshape(4, 4, 4, 2, 2, 2), CTX + FSDP)
    return jax.shard_map(
        whole,
        mesh=fine,
        in_specs=(
            P(None, CTX),
            P(FSDP, CTX, None),
            P(FSDP, CTX, None),
            P(FSDP, CTX, None),
            P(FSDP, CTX, None),
            P(FSDP, CTX, None),
            P(FSDP, None, CTX),
            P(None, CTX, FSDP),
        ),
        out_specs=(P(FSDP, CTX, None), P(FSDP, CTX, None), P(FSDP, CTX, None), P(FSDP, None)),
        check_vma=False,
    )
```

time: 190 us -> 159 us (0.84)
  the two profiles are of different devices: /device:TPU:2 before, /device:TPU:1 now
where the time goes in v2:
time: 159 us; the launch traced here: 158 us
  starting transfers between devices  95.5 us (60%)
  waiting for transfers between devices  34.7 us (22%)
  Pallas kernels  9.31 us (6%)
  blocking collectives  8.66 us (5%)
  local copies, waits for them, and re-layouts  7.66 us (5%)
    all_to_all x5, starting transfers between devices, swap(): return lax.all_to_all(value, axis, 0, 0, tiled=True)  49.9 us
    ppermute x11, starting transfers between devices, ahead(): return lax.ppermute(value, axis, pairs)  45.6 us
    all_to_all x5, waiting for transfers between devices, swap(): return lax.all_to_all(value, axis, 0, 0, tiled=True)  17.9 us
    ppermute x11, waiting for transfers between devices, ahead(): return lax.ppermute(value, axis, pairs)  16.9 us
    all_to_all x1, blocking collectives, swap(): return lax.all_to_all(value, axis, 0, 0, tiled=True)  8.66 us
    pallas_call x1, Pallas kernels, attention_grads(): pl.pallas_call(attention_kernel, out_shape=(struct((HEAD_SIZE, STACK)),)...  5.74 us
    unnamed x29, local copies, waits for them, and re-layouts  4.92 us
  transfers between devices with their start and end apart: 16, of which 5 were waited for; matrix products, arithmetic and copies ran while one was open for 2% of the time, Pallas kernels for 5%

profile of v2, /device:TPU:1, one launch (start us, length us, event | category | flops | bytes accessed | tf_op | source)
XLA Modules:
  0.0 158.1 jit_solution(11706186341030910829)
XLA Ops:
  0.6 1.3 copy.34.places
  2.0 1.5 pack_keys.1
  3.5 15.8 %all-to-all-start = ((bf16[4,272,128]{2,1,0:T(8,128)(2,1)}), bf16[4,272,128]{2,1,0:T(8,128)(2,1)S(1)}, u32[]{:S(2)}, u32[]{:S(2)}) async-start(bf16[4,272,128]{2,1,0:T(8,128)(2,1)} %pack_keys.1), calls=%async_computation | async-start | bytes 557056 | tf_op jit(solution)/shard_map/all_to_all | solution.py:165
  19.2 0.6 copy.35.norm_ref
  19.8 2.0 %pack_queries.1.q0 = bf16[1312,128]{1,0:T(8,128)(2,1)} custom-call(s32[8,1]{1,0:T(8,128)} %copy.34.places, bf16[1,128,640]{2,1,0:T(8,128)(2,1)} %q_ref.1, bf16[1,128,640]{2,1,0:T(8,128)(2,1)} %g_ref.1, bf16[1,128,640]{2,1,0:T(8,128)(2,1)} %o_ref.1, f32[1,5,128]{2,1,0:T(8,128)} %copy.35.norm_ref), custom_call_target="tpu_custom_call" | custom-call | tf_op jit(solution)/shard_map/pack_queries/pallas_call | solution.py:132
  21.9 3.1 %collective-permute-start = (bf16[1312,128]{1,0:T(8,128)(2,1)}, bf16[1312,128]{1,0:T(8,128)(2,1)S(1)}, u32[]{:S(2)}, u32[]{:S(2)}) collective-permute-start(bf16[1312,128]{1,0:T(8,128)(2,1)} %pack_queries.1.q0), channel_id=1, source_target_pairs={{0,128},{128,256},{256,384},{384,0},{1,129},{129,257},{257,385},{3... | collective-permute-start | bytes 1007624 | tf_op jit(solution)/shard_map/ppermute | solution.py:161
  25.0 4.4 %collective-permute-start.1 = (bf16[1312,128]{1,0:T(8,128)(2,1)}, bf16[1312,128]{1,0:T(8,128)(2,1)S(1)}, u32[]{:S(2)}, u32[]{:S(2)}) collective-permute-start(bf16[1312,128]{1,0:T(8,128)(2,1)} %pack_queries.1.q0), channel_id=1, source_target_pairs={{0,256},{128,384},{256,0},{384,128},{1,257},{129,385},{257,1},{385... | collective-permute-start | bytes 1007624 | tf_op jit(solution)/shard_map/ppermute | solution.py:161
  29.4 3.1 %collective-permute-start.2 = (bf16[1312,128]{1,0:T(8,128)(2,1)}, bf16[1312,128]{1,0:T(8,128)(2,1)S(1)}, u32[]{:S(2)}, u32[]{:S(2)}) collective-permute-start(bf16[1312,128]{1,0:T(8,128)(2,1)} %pack_queries.1.q0), channel_id=1, source_target_pairs={{0,384},{128,0},{256,128},{384,256},{1,385},{129,1},{257,129},{385... | collective-permute-start | bytes 1007624 | tf_op jit(solution)/shard_map/ppermute | solution.py:161
  32.5 3.7 %collective-permute-start.9 = (bf16[8,80,128]{2,0,1:T(8,128)(2,1)S(1)}, bf16[8,80,128]{2,0,1:T(8,128)(2,1)S(1)}, u32[]{:S(2)}, u32[]{:S(2)}) collective-permute-start(bf16[8,80,128]{2,0,1:T(8,128)(2,1)S(1)} %bitcast.63), channel_id=1, source_target_pairs={{0,1},{1,0},{2,3},{3,2},{4,5},{5,4},{6,7},{7,6},{8,9},{9,8},{10,11... | collective-permute-start | bytes 491528 | tf_op jit(solution)/shard_map/ppermute | solution.py:161
  36.2 0.0 collective-permute-done.q1
  36.2 5.6 %collective-permute-done.1.q2 = bf16[1312,128]{1,0:T(8,128)(2,1)S(1)} collective-permute-done((bf16[1312,128]{1,0:T(8,128)(2,1)}, bf16[1312,128]{1,0:T(8,128)(2,1)S(1)}, u32[]{:S(2)}, u32[]{:S(2)}) %collective-permute-start.1) | collective-permute-done | bytes 335904 | tf_op jit(solution)/shard_map/ppermute | solution.py:161
  41.9 1.9 %collective-permute-done.2.q3 = bf16[1312,128]{1,0:T(8,128)(2,1)S(1)} collective-permute-done((bf16[1312,128]{1,0:T(8,128)(2,1)}, bf16[1312,128]{1,0:T(8,128)(2,1)S(1)}, u32[]{:S(2)}, u32[]{:S(2)}) %collective-permute-start.2) | collective-permute-done | bytes 335904 | tf_op jit(solution)/shard_map/ppermute | solution.py:161
  43.7 0.7 copy-done.4
  44.5 0.7 copy-done
  45.2 5.7 %attention_grads.1 = (bf16[128,640]{1,0:T(8,128)(2,1)}, bf16[128,640]{1,0:T(8,128)(2,1)}, bf16[128,640]{1,0:T(8,128)(2,1)}, bf16[128,640]{1,0:T(8,128)(2,1)}, bf...) custom-call(bf16[1312,128]{1,0:T(8,128)(2,1)} %pack_queries.1.q0, bf16[1312,128]{1,0:T(8,128)(2,1)} %copy-done.2, ...), custom_call_target="tpu_custom_call" | custom-call | tf_op jit(solution)/shard_map/attention_grads/pallas_call | solution.py:142
  50.9 13.5 %all-to-all-start.1 = ((bf16[4,128,128]{2,1,0:T(8,128)(2,1)}), bf16[4,128,128]{2,1,0:T(8,128)(2,1)S(1)}, u32[]{:S(2)}, u32[]{:S(2)}) async-start(bf16[4,128,128]{2,1,0:T(8,128)(2,1)} %get-tuple-element.14), calls=%async_computation.1 | async-start | bytes 262144 | tf_op jit(solution)/shard_map/all_to_all | solution.py:165
  64.4 12.3 %all-to-all-done.1 = bf16[4,128,128]{2,1,0:T(8,128)(2,1)S(1)} async-done(((bf16[4,128,128]{2,1,0:T(8,128)(2,1)}), bf16[4,128,128]{2,1,0:T(8,128)(2,1)S(1)}, u32[]{:S(2)}, u32[]{:S(2)}) %all-to-all-start.1) | async-done | bytes 131104 | tf_op jit(solution)/shard_map/all_to_all | solution.py:165
  76.8 0.0 copy-start.6
  76.8 0.7 broadcast_in_dim.12
  77.5 6.5 %all-to-all-start.2 = ((bf16[8,128,128]{2,1,0:T(8,128)(2,1)}), bf16[8,128,128]{2,1,0:T(8,128)(2,1)S(1)}, u32[]{:S(2)}, u32[]{:S(2)}) async-start(bf16[8,128,128]{2,1,0:T(8,128)(2,1)} %broadcast_in_dim.12), calls=%async_computation.2 | async-start | bytes 524288 | tf_op jit(solution)/shard_map/all_to_all | solution.py:165
  84.1 2.3 %collective-permute-start.10 = (bf16[2,8,80,128]{3,1,2,0:T(8,128)(2,1)S(1)}, bf16[2,8,80,128]{3,1,2,0:T(8,128)(2,1)S(1)}, u32[]{:S(2)}, u32[]{:S(2)}) collective-permute-start(bf16[2,8,80,128]{3,1,2,0:T(8,128)(2,1)S(1)} %pad_maximum_fusion.1), channel_id=1, source_target_pairs={{0,2},{2,0},{1,3},{3,1},{4,6},{6,4},{5,7},{7,5},{8,10},{10,8},{9,1... | collective-permute-start | bytes 983048 | tf_op jit(solution)/shard_map/ppermute | solution.py:161
  86.4 9.3 %collective-permute-done.10 = bf16[2,8,80,128]{3,1,2,0:T(8,128)(2,1)S(1)} collective-permute-done((bf16[2,8,80,128]{3,1,2,0:T(8,128)(2,1)S(1)}, bf16[2,8,80,128]{3,1,2,0:T(8,128)(2,1)S(1)}, u32[]{:S(2)}, u32[]{:S(2)}) %collective-permute-start.10) | collective-permute-done | bytes 327712 | tf_op jit(solution)/shard_map/ppermute | solution.py:161
  95.8 0.1 pad_maximum_fusion
  95.9 0.1 pad_bitcast_fusion
  96.0 0.1 copy.40
  96.1 0.0 all-to-all-done.2
  96.1 0.4 fusion
  96.5 8.7 %all_to_all.30 = bf16[4,96,128]{2,1,0:T(8,128)(2,1)S(1)} all-to-all(bf16[4,96,128]{2,1,0:T(8,128)(2,1)S(1)} %bitcast.62), channel_id=1, replica_groups=mesh['x'=4,'zh'=4,'zl'=4,'yh'=2,'yl'=2,'c'=2] {'x'}, dimensions={0} | all-to-all | bytes 196608 | tf_op jit(solution)/shard_map/all_to_all | solution.py:165
  105.2 0.7 broadcast_in_dim.13
  105.9 4.1 %all-to-all-start.4 = ((bf16[4,96,128]{2,1,0:T(8,128)(2,1)}), bf16[4,96,128]{2,1,0:T(8,128)(2,1)S(1)}, u32[]{:S(2)}, u32[]{:S(2)}) async-start(bf16[4,96,128]{2,1,0:T(8,128)(2,1)} %broadcast_in_dim.13), calls=%async_computation.4 | async-start | bytes 196608 | tf_op jit(solution)/shard_map/all_to_all | solution.py:165
  109.9 7.3 %collective-permute-start.6 = (bf16[128,128]{1,0:T(8,128)(2,1)S(1)}, bf16[128,128]{1,0:T(8,128)(2,1)S(1)}, u32[]{:S(2)}, u32[]{:S(2)}) collective-permute-start(bf16[128,128]{1,0:T(8,128)(2,1)S(1)} %get-tuple-element.32), channel_id=1, source_target_pairs={{0,32},{32,64},{64,96},{96,0},{1,33},{33,65},{65,97},{97,1},{2,34}... | collective-permute-start | bytes 98312 | tf_op jit(solution)/shard_map/ppermute | solution.py:161
  117.2 7.0 %collective-permute-start.7 = (bf16[128,128]{1,0:T(8,128)(2,1)S(1)}, bf16[128,128]{1,0:T(8,128)(2,1)S(1)}, u32[]{:S(2)}, u32[]{:S(2)}) collective-permute-start(bf16[128,128]{1,0:T(8,128)(2,1)S(1)} %get-tuple-element.34), channel_id=1, source_target_pairs={{0,64},{32,96},{64,0},{96,32},{1,65},{33,97},{65,1},{97,33},{2,66}... | collective-permute-start | bytes 98312 | tf_op jit(solution)/shard_map/ppermute | solution.py:161
  124.2 7.0 %collective-permute-start.8 = (bf16[128,128]{1,0:T(8,128)(2,1)S(1)}, bf16[128,128]{1,0:T(8,128)(2,1)S(1)}, u32[]{:S(2)}, u32[]{:S(2)}) collective-permute-start(bf16[128,128]{1,0:T(8,128)(2,1)S(1)} %get-tuple-element.33), channel_id=1, source_target_pairs={{0,96},{32,0},{64,32},{96,64},{1,97},{33,1},{65,33},{97,65},{2,98}... | collective-permute-start | bytes 98312 | tf_op jit(solution)/shard_map/ppermute | solution.py:161
  131.2 2.8 %collective-permute-start.3 = (bf16[128,640]{1,0:T(8,128)(2,1)S(1)}, bf16[128,640]{1,0:T(8,128)(2,1)S(1)}, u32[]{:S(2)}, u32[]{:S(2)}) collective-permute-start(bf16[128,640]{1,0:T(8,128)(2,1)S(1)} %copy-done.11), channel_id=1, source_target_pairs={{0,384},{128,0},{256,128},{384,256},{1,385},{129,1},{257,129},{385... | collective-permute-start | bytes 491528 | tf_op jit(solution)/shard_map/ppermute | solution.py:161
  134.1 3.1 %collective-permute-start.4 = (bf16[128,640]{1,0:T(8,128)(2,1)S(1)}, bf16[128,640]{1,0:T(8,128)(2,1)S(1)}, u32[]{:S(2)}, u32[]{:S(2)}) collective-permute-start(bf16[128,640]{1,0:T(8,128)(2,1)S(1)} %copy-done.10), channel_id=1, source_target_pairs={{0,256},{128,384},{256,0},{384,128},{1,257},{129,385},{257,1},{385... | collective-permute-start | bytes 491528 | tf_op jit(solution)/shard_map/ppermute | solution.py:161
  137.2 1.9 %collective-permute-start.5 = (bf16[128,640]{1,0:T(8,128)(2,1)S(1)}, bf16[128,640]{1,0:T(8,128)(2,1)S(1)}, u32[]{:S(2)}, u32[]{:S(2)}) collective-permute-start(bf16[128,640]{1,0:T(8,128)(2,1)S(1)} %copy-done.9), channel_id=1, source_target_pairs={{0,128},{128,256},{256,384},{384,0},{1,129},{129,257},{257,385},{3... | collective-permute-start | bytes 491528 | tf_op jit(solution)/shard_map/ppermute | solution.py:161
  139.1 0.0 collective-permute-done.7
  139.1 0.0 collective-permute-done.8
  139.1 0.6 fusion.3
  139.7 0.0 all-to-all-done.4
  139.8 0.7 broadcast_in_dim.14
  140.5 10.1 %all-to-all-start.5 = ((f32[16,24,128]{2,1,0:T(8,128)}), f32[16,24,128]{2,1,0:T(8,128)S(1)}, u32[]{:S(2)}, u32[]{:S(2)}) async-start(f32[16,24,128]{2,1,0:T(8,128)} %bitcast.19), calls=%async_computation.5 | async-start | bytes 393216 | tf_op jit(solution)/shard_map/all_to_all | solution.py:165
  150.6 0.0 collective-permute-done.4
  150.7 0.2 copy.37
  150.9 0.2 copy.38
  151.0 0.8 copy.42
  151.8 5.5 %all-to-all-done.5 = f32[16,24,128]{2,1,0:T(8,128)S(1)} async-done(((f32[16,24,128]{2,1,0:T(8,128)}), f32[16,24,128]{2,1,0:T(8,128)S(1)}, u32[]{:S(2)}, u32[]{:S(2)}) %all-to-all-start.5) | async-done | bytes 196640 | tf_op jit(solution)/shard_map/all_to_all | solution.py:165
  157.4 0.7 copy.50
  (37 shorter events, 0.4 us)
Async XLA Ops:
  3.5 15.8 %copy-start.8 = (f32[1,5,128]{2,0,1:T(1,128)S(1)}, f32[1,5,128]{2,0,1:T(1,128)}, u32[]{:S(2)}) copy-start(f32[1,5,128]{2,0,1:T(1,128)} %param.14) | copy-start | bytes 7684
  3.5 40.3 %all-to-all-start = ((bf16[4,272,128]{2,1,0:T(8,128)(2,1)}), bf16[4,272,128]{2,1,0:T(8,128)(2,1)S(1)}, u32[]{:S(2)}, u32[]{:S(2)}) async-start(bf16[4,272,128]{2,1,0:T(8,128)(2,1)} %pack_keys.1), calls=%async_computation | async-start | bytes 557056 | tf_op jit(solution)/shard_map/all_to_all | solution.py:165
  19.8 12.6 %copy-start.1 = (bf16[8,128,80]{1,2,0:T(8,128)(2,1)S(1)}, bf16[8,128,80]{1,2,0:T(8,128)(2,1)}, u32[]{:S(2)}) copy-start(bf16[8,128,80]{1,2,0:T(8,128)(2,1)} %param.15) | copy-start | bytes 491524
  21.9 14.3 %collective-permute-start = (bf16[1312,128]{1,0:T(8,128)(2,1)}, bf16[1312,128]{1,0:T(8,128)(2,1)S(1)}, u32[]{:S(2)}, u32[]{:S(2)}) collective-permute-start(bf16[1312,128]{1,0:T(8,128)(2,1)} %pack_queries.1.q0), channel_id=1, source_target_pairs={{0,128},{128,256},{256,384},{384,0},{1,129},{129,257},{257,385},{3... | collective-permute-start | bytes 1007624 | tf_op jit(solution)/shard_map/ppermute | solution.py:161
  25.0 16.9 %collective-permute-start.1 = (bf16[1312,128]{1,0:T(8,128)(2,1)}, bf16[1312,128]{1,0:T(8,128)(2,1)S(1)}, u32[]{:S(2)}, u32[]{:S(2)}) collective-permute-start(bf16[1312,128]{1,0:T(8,128)(2,1)} %pack_queries.1.q0), channel_id=1, source_target_pairs={{0,256},{128,384},{256,0},{384,128},{1,257},{129,385},{257,1},{385... | collective-permute-start | bytes 1007624 | tf_op jit(solution)/shard_map/ppermute | solution.py:161
  29.4 14.4 %collective-permute-start.2 = (bf16[1312,128]{1,0:T(8,128)(2,1)}, bf16[1312,128]{1,0:T(8,128)(2,1)S(1)}, u32[]{:S(2)}, u32[]{:S(2)}) collective-permute-start(bf16[1312,128]{1,0:T(8,128)(2,1)} %pack_queries.1.q0), channel_id=1, source_target_pairs={{0,384},{128,0},{256,128},{384,256},{1,385},{129,1},{257,129},{385... | collective-permute-start | bytes 1007624 | tf_op jit(solution)/shard_map/ppermute | solution.py:161
  32.5 31.9 %collective-permute-start.9 = (bf16[8,80,128]{2,0,1:T(8,128)(2,1)S(1)}, bf16[8,80,128]{2,0,1:T(8,128)(2,1)S(1)}, u32[]{:S(2)}, u32[]{:S(2)}) collective-permute-start(bf16[8,80,128]{2,0,1:T(8,128)(2,1)S(1)} %bitcast.63), channel_id=1, source_target_pairs={{0,1},{1,0},{2,3},{3,2},{4,5},{5,4},{6,7},{7,6},{8,9},{9,8},{10,11... | collective-permute-start | bytes 491528 | tf_op jit(solution)/shard_map/ppermute | solution.py:161
  36.2 7.5 %copy-start.2 = (bf16[1312,128]{1,0:T(8,128)(2,1)}, bf16[1312,128]{1,0:T(8,128)(2,1)S(1)}, u32[]{:S(2)}) copy-start(bf16[1312,128]{1,0:T(8,128)(2,1)S(1)} %collective-permute-done.q1) | copy-start | bytes 1007620
  41.9 1.9 %copy-start.3 = (bf16[1312,128]{1,0:T(8,128)(2,1)}, bf16[1312,128]{1,0:T(8,128)(2,1)S(1)}, u32[]{:S(2)}) copy-start(bf16[1312,128]{1,0:T(8,128)(2,1)S(1)} %collective-permute-done.1.q2) | copy-start | bytes 1007620
  43.7 0.7 copy-start.4
  44.5 0.7 copy-start
  50.9 25.8 %all-to-all-start.1 = ((bf16[4,128,128]{2,1,0:T(8,128)(2,1)}), bf16[4,128,128]{2,1,0:T(8,128)(2,1)S(1)}, u32[]{:S(2)}, u32[]{:S(2)}) async-start(bf16[4,128,128]{2,1,0:T(8,128)(2,1)} %get-tuple-element.14), calls=%async_computation.1 | async-start | bytes 262144 | tf_op jit(solution)/shard_map/all_to_all | solution.py:165
  76.8 0.8 copy-start.6
  77.5 18.6 %all-to-all-start.2 = ((bf16[8,128,128]{2,1,0:T(8,128)(2,1)}), bf16[8,128,128]{2,1,0:T(8,128)(2,1)S(1)}, u32[]{:S(2)}, u32[]{:S(2)}) async-start(bf16[8,128,128]{2,1,0:T(8,128)(2,1)} %broadcast_in_dim.12), calls=%async_computation.2 | async-start | bytes 524288 | tf_op jit(solution)/shard_map/all_to_all | solution.py:165
  84.1 11.7 %collective-permute-start.10 = (bf16[2,8,80,128]{3,1,2,0:T(8,128)(2,1)S(1)}, bf16[2,8,80,128]{3,1,2,0:T(8,128)(2,1)S(1)}, u32[]{:S(2)}, u32[]{:S(2)}) collective-permute-start(bf16[2,8,80,128]{3,1,2,0:T(8,128)(2,1)S(1)} %pad_maximum_fusion.1), channel_id=1, source_target_pairs={{0,2},{2,0},{1,3},{3,1},{4,6},{6,4},{5,7},{7,5},{8,10},{10,8},{9,1... | collective-permute-start | bytes 983048 | tf_op jit(solution)/shard_map/ppermute | solution.py:161
  105.2 26.1 %copy-start.11 = (bf16[128,640]{1,0:T(8,128)(2,1)S(1)}, bf16[128,640]{1,0:T(8,128)(2,1)}, u32[]{:S(2)}) copy-start(bf16[128,640]{1,0:T(8,128)(2,1)} %get-tuple-element.11) | copy-start | bytes 491524
  105.2 4.7 %copy-start.7 = (bf16[4,128,128]{2,1,0:T(8,128)(2,1)S(1)}, bf16[4,128,128]{2,1,0:T(8,128)(2,1)}, u32[]{:S(2)}) copy-start(bf16[4,128,128]{2,1,0:T(8,128)(2,1)} %get-tuple-element.15) | copy-start | bytes 393220
  105.8 28.2 %copy-start.10 = (bf16[128,640]{1,0:T(8,128)(2,1)S(1)}, bf16[128,640]{1,0:T(8,128)(2,1)}, u32[]{:S(2)}) copy-start(bf16[128,640]{1,0:T(8,128)(2,1)} %get-tuple-element.12) | copy-start | bytes 491524
  105.9 31.3 %copy-start.9 = (bf16[128,640]{1,0:T(8,128)(2,1)S(1)}, bf16[128,640]{1,0:T(8,128)(2,1)}, u32[]{:S(2)}) copy-start(bf16[128,640]{1,0:T(8,128)(2,1)} %get-tuple-element.13) | copy-start | bytes 491524
  105.9 33.9 %all-to-all-start.4 = ((bf16[4,96,128]{2,1,0:T(8,128)(2,1)}), bf16[4,96,128]{2,1,0:T(8,128)(2,1)S(1)}, u32[]{:S(2)}, u32[]{:S(2)}) async-start(bf16[4,96,128]{2,1,0:T(8,128)(2,1)} %broadcast_in_dim.13), calls=%async_computation.4 | async-start | bytes 196608 | tf_op jit(solution)/shard_map/all_to_all | solution.py:165
  109.9 27.2 %collective-permute-start.6 = (bf16[128,128]{1,0:T(8,128)(2,1)S(1)}, bf16[128,128]{1,0:T(8,128)(2,1)S(1)}, u32[]{:S(2)}, u32[]{:S(2)}) collective-permute-start(bf16[128,128]{1,0:T(8,128)(2,1)S(1)} %get-tuple-element.32), channel_id=1, source_target_pairs={{0,32},{32,64},{64,96},{96,0},{1,33},{33,65},{65,97},{97,1},{2,34}... | collective-permute-start | bytes 98312 | tf_op jit(solution)/shard_map/ppermute | solution.py:161
  117.2 21.9 %collective-permute-start.7 = (bf16[128,128]{1,0:T(8,128)(2,1)S(1)}, bf16[128,128]{1,0:T(8,128)(2,1)S(1)}, u32[]{:S(2)}, u32[]{:S(2)}) collective-permute-start(bf16[128,128]{1,0:T(8,128)(2,1)S(1)} %get-tuple-element.34), channel_id=1, source_target_pairs={{0,64},{32,96},{64,0},{96,32},{1,65},{33,97},{65,1},{97,33},{2,66}... | collective-permute-start | bytes 98312 | tf_op jit(solution)/shard_map/ppermute | solution.py:161
  124.2 14.9 %collective-permute-start.8 = (bf16[128,128]{1,0:T(8,128)(2,1)S(1)}, bf16[128,128]{1,0:T(8,128)(2,1)S(1)}, u32[]{:S(2)}, u32[]{:S(2)}) collective-permute-start(bf16[128,128]{1,0:T(8,128)(2,1)S(1)} %get-tuple-element.33), channel_id=1, source_target_pairs={{0,96},{32,0},{64,32},{96,64},{1,97},{33,1},{65,33},{97,65},{2,98}... | collective-permute-start | bytes 98312 | tf_op jit(solution)/shard_map/ppermute | solution.py:161
  131.2 19.4 %collective-permute-start.3 = (bf16[128,640]{1,0:T(8,128)(2,1)S(1)}, bf16[128,640]{1,0:T(8,128)(2,1)S(1)}, u32[]{:S(2)}, u32[]{:S(2)}) collective-permute-start(bf16[128,640]{1,0:T(8,128)(2,1)S(1)} %copy-done.11), channel_id=1, source_target_pairs={{0,384},{128,0},{256,128},{384,256},{1,385},{129,1},{257,129},{385... | collective-permute-start | bytes 491528 | tf_op jit(solution)/shard_map/ppermute | solution.py:161
  134.1 16.6 %collective-permute-start.4 = (bf16[128,640]{1,0:T(8,128)(2,1)S(1)}, bf16[128,640]{1,0:T(8,128)(2,1)S(1)}, u32[]{:S(2)}, u32[]{:S(2)}) collective-permute-start(bf16[128,640]{1,0:T(8,128)(2,1)S(1)} %copy-done.10), channel_id=1, source_target_pairs={{0,256},{128,384},{256,0},{384,128},{1,257},{129,385},{257,1},{385... | collective-permute-start | bytes 491528 | tf_op jit(solution)/shard_map/ppermute | solution.py:161
  137.2 13.4 %collective-permute-start.5 = (bf16[128,640]{1,0:T(8,128)(2,1)S(1)}, bf16[128,640]{1,0:T(8,128)(2,1)S(1)}, u32[]{:S(2)}, u32[]{:S(2)}) collective-permute-start(bf16[128,640]{1,0:T(8,128)(2,1)S(1)} %copy-done.9), channel_id=1, source_target_pairs={{0,128},{128,256},{256,384},{384,0},{1,129},{129,257},{257,385},{3... | collective-permute-start | bytes 491528 | tf_op jit(solution)/shard_map/ppermute | solution.py:161
  140.5 10.2 %copy-start.5 = (bf16[128,640]{1,0:T(8,128)(2,1)S(1)}, bf16[128,640]{1,0:T(8,128)(2,1)}, u32[]{:S(2)}) copy-start(bf16[128,640]{1,0:T(8,128)(2,1)} %get-tuple-element.10) | copy-start | bytes 491524
  140.5 16.9 %all-to-all-start.5 = ((f32[16,24,128]{2,1,0:T(8,128)}), f32[16,24,128]{2,1,0:T(8,128)S(1)}, u32[]{:S(2)}, u32[]{:S(2)}) async-start(f32[16,24,128]{2,1,0:T(8,128)} %bitcast.19), calls=%async_computation.5 | async-start | bytes 393216 | tf_op jit(solution)/shard_map/all_to_all | solution.py:165

commit v3 on v2

v3 whole, which is shorter than its diff:
```python
import jax
import jax.numpy as jnp
from jax import lax
from jax.experimental import pallas as pl
from jax.experimental.pallas import tpu as pltpu
from jax.sharding import Mesh
from jax.sharding import PartitionSpec as P


HEADS = 5
HEAD_SIZE = 128
BLOCK = 128
STACK = HEADS * BLOCK
SIDE = 4
SCALE = HEAD_SIZE ** (-0.5)
LOG2E = 1.4426950408889634
CTX = ("x", "zh")
FSDP = ("zl", "yh", "yl", "c")
GRANT = 16 * 2**20
Q_ROWS = 2 * STACK + 32
KV_ROWS = 2 * BLOCK + 16


def dot(a, b, dims):
    return lax.dot_general(a, b, (dims, ((), ())), preferred_element_type=jnp.float32)


def parts_of(value):
    first = value.astype(jnp.bfloat16)
    value = value - first.astype(jnp.float32)
    second = value.astype(jnp.bfloat16)
    value = value - second.astype(jnp.float32)
    return [first.astype(jnp.float32), second.astype(jnp.float32), value]


def own_place(places):
    return places[0, lax.axis_index("zl") * 2 + lax.axis_index("yh")]


def pack_kernel(places, q_ref, g_ref, o_ref, norm_ref, k_ref, v_ref, q_out, kv_out):
    place = own_place(places)
    deltas = []
    for h in range(HEADS):
        cols = slice(h * HEAD_SIZE, (h + 1) * HEAD_SIZE)
        q = q_ref[0, :, cols]
        g = g_ref[0, :, cols]
        for copy in range(SIDE):
            q_out[copy, h * BLOCK : (h + 1) * BLOCK, :] = q
            q_out[copy, STACK + h * BLOCK : STACK + (h + 1) * BLOCK, :] = g
        product = g.astype(jnp.float32) * o_ref[0, :, cols].astype(jnp.float32)
        deltas.append(jnp.sum(product.T, axis=0, keepdims=True))
    delta = jnp.concatenate(deltas, axis=0)
    norm = norm_ref[:, 0, :] * LOG2E
    tail = jnp.full((2, HEAD_SIZE), place, jnp.int32).astype(jnp.float32)
    extra = jnp.concatenate(parts_of(norm) + parts_of(delta) + [tail], axis=0)
    for copy in range(SIDE):
        q_out[copy, 2 * STACK :, :] = extra.astype(jnp.bfloat16)
    kv_out[:BLOCK, :] = k_ref[0]
    kv_out[BLOCK : 2 * BLOCK, :] = v_ref[0]
    tail = jnp.full((16, HEAD_SIZE), place, jnp.int32)
    kv_out[2 * BLOCK :, :] = tail.astype(jnp.float32).astype(jnp.bfloat16)


def place_of(rows):
    return jnp.max(rows.astype(jnp.float32)).astype(jnp.int32)


def attention_kernel(q_all, kv_ref, dq_ref, dkv_ref, dq_acc, dk_acc, dv_acc, k_t, k_place):
    dk_acc[...] = jnp.zeros_like(dk_acc)
    dv_acc[...] = jnp.zeros_like(dv_acc)
    key_row = lax.broadcasted_iota(jnp.int32, (BLOCK, STACK), 0)
    query_col = lax.broadcasted_iota(jnp.int32, (BLOCK, STACK), 1) & (BLOCK - 1)
    offset = key_row - query_col
    for j in range(SIDE):
        k_t[j] = kv_ref[j, :BLOCK, :].T
        k_place[j] = place_of(kv_ref[j, 2 * BLOCK :, :])
    for i in range(SIDE):
        q_ref = q_all.at[i]
        dq_acc[...] = jnp.zeros_like(dq_acc)
        extra = q_ref[2 * STACK :, :].astype(jnp.float32)
        norm = extra[0:5] + extra[5:10] + extra[10:15]
        delta = extra[15:20] + extra[20:25] + extra[25:30]
        norm = jnp.concatenate([norm[h : h + 1] for h in range(HEADS)], axis=1)
        delta = jnp.concatenate([delta[h : h + 1] for h in range(HEADS)], axis=1)
        here = place_of(extra[30:32])

        def pair(j, carry):
            ahead = (here - k_place[j]) * BLOCK

            @pl.when(ahead >= 0)
            def _():
                q = q_ref[:STACK, :]
                g = q_ref[STACK : 2 * STACK, :]
                scores = dot(kv_ref[j, :BLOCK, :], q, ((1,), (1,))) * (SCALE * LOG2E)
                probs = jnp.where(offset <= ahead, jnp.exp2(scores - norm), 0.0)
                dprobs = dot(kv_ref[j, BLOCK : 2 * BLOCK, :], g, ((1,), (1,)))
                dscores = (probs * (dprobs - delta) * SCALE).astype(jnp.bfloat16)
                dv_acc[j] += dot(probs.astype(jnp.bfloat16), g, ((1,), (0,)))
                dk_acc[j] += dot(dscores, q, ((1,), (0,)))
                dq_acc[...] += dot(k_t[j], dscores, ((1,), (0,)))

            return carry

        lax.fori_loop(0, SIDE, pair, 0)
        dq_ref[i] = dq_acc[...].astype(jnp.bfloat16)
    dkv_ref[:, :BLOCK, :] = dk_acc[...].astype(jnp.bfloat16)
    dkv_ref[:, BLOCK:, :] = dv_acc[...].astype(jnp.bfloat16)


SMEM = pl.BlockSpec(memory_space=pltpu.SMEM)
VMEM = pl.BlockSpec(memory_space=pltpu.VMEM)


def struct(shape, dtype=jnp.bfloat16):
    return jax.ShapeDtypeStruct(shape, dtype)


def pack(places, queries, gradient, output, norm, keys, values):
    return pl.pallas_call(
        pack_kernel,
        out_shape=(struct((SIDE, Q_ROWS, HEAD_SIZE)), struct((KV_ROWS, HEAD_SIZE))),
        in_specs=[SMEM] + [VMEM] * 6,
        out_specs=(VMEM, VMEM),
        name="pack",
    )(places, queries, gradient, output, norm, keys, values)


def attention_grads(q_all, kv_all):
    return pl.pallas_call(
        attention_kernel,
        out_shape=(struct((SIDE, HEAD_SIZE, STACK)), struct((SIDE, 2 * BLOCK, HEAD_SIZE))),
        in_specs=[VMEM] * 2,
        out_specs=(VMEM,) * 2,
        scratch_shapes=[
            pltpu.VMEM((HEAD_SIZE, STACK), jnp.float32),
            pltpu.VMEM((SIDE, BLOCK, HEAD_SIZE), jnp.float32),
            pltpu.VMEM((SIDE, BLOCK, HEAD_SIZE), jnp.float32),
            pltpu.VMEM((SIDE, HEAD_SIZE, BLOCK), jnp.bfloat16),
            pltpu.SMEM((SIDE,), jnp.int32),
        ],
        compiler_params=pltpu.CompilerParams(vmem_limit_bytes=GRANT),
        name="attention_grads",
    )(q_all, kv_all)


def ahead(value, axis, steps):
    count = lax.axis_size(axis)
    pairs = [(source, (source + steps) % count) for source in range(count)]
    return lax.ppermute(value, axis, pairs)


def swap(value, axis):
    return lax.all_to_all(value, axis, 0, 0, tiled=True)


def copies(value, count):
    return jnp.broadcast_to(value[None], (count,) + value.shape)


def total(parts):
    return jnp.sum(parts.astype(jnp.float32), axis=0)


def row_features(features):
    rows = features.transpose(0, 2, 1)
    rows = ahead_pair(rows, "yl")
    rows = ahead_pair(rows, "c").transpose(1, 0, 2, 3, 4)
    return rows.reshape((SIDE,) + rows.shape[2:])


def ahead_pair(value, axis):
    other = ahead(value, axis, 1)
    first = lax.axis_index(axis) == 0
    return jnp.stack([jnp.where(first, value, other), jnp.where(first, other, value)])


def whole(block_pos, queries, keys, values, attention_output, output_gradient, log_softmax_norm, features):
    places = block_pos.T
    norm = log_softmax_norm.transpose(1, 0, 2)
    q_own, kv_own = pack(
        places, queries, output_gradient, attention_output, norm, keys, values
    )
    q_all = swap(q_own, "x")
    kv_all = lax.all_gather(kv_own, "zh", axis=0)
    dq, dkv = attention_grads(q_all, kv_all)

    dkv = swap(dkv, "zh")
    key_gradient = total(dkv[:, :BLOCK]).astype(jnp.bfloat16)
    value_gradient = total(dkv[:, BLOCK:]).astype(jnp.bfloat16)
    here = lax.axis_index("x")
    pieces = [lax.dynamic_index_in_dim(dq, (here + s) % SIDE, 0, keepdims=False) for s in range(SIDE)]
    dq = pieces[:1] + [ahead(pieces[s], "x", s) for s in (1, 2, 3)]
    grad_q = total(jnp.stack(dq))
    grad_q = grad_q.reshape(HEAD_SIZE, HEADS, BLOCK).transpose(2, 1, 0).reshape(BLOCK, STACK)

    weights = row_features(features)
    gathered = swap(copies(key_gradient, 8), ("zl", "yh"))
    partial = jnp.einsum("fsit,stj->fij", weights, gathered, preferred_element_type=jnp.float32)
    partial = copies(partial.astype(jnp.bfloat16), SIDE).reshape((16,) + partial.shape[1:])
    partial = swap(partial, ("x", "yl", "c"))
    mine = total(partial.reshape((SIDE, SIDE) + partial.shape[1:])).astype(jnp.bfloat16)
    mine = lax.all_gather(mine, "zh", axis=0)
    width = features.shape[-1]
    grad_wk = total(mine).transpose(1, 0, 2).reshape(width, SIDE * HEAD_SIZE)
    return (grad_q.astype(jnp.bfloat16)[None], key_gradient[None], value_gradient[None], grad_wk)


def solution(mesh):
    fine = Mesh(mesh.devices.reshape(4, 4, 4, 2, 2, 2), CTX + FSDP)
    return jax.shard_map(
        whole,
        mesh=fine,
        in_specs=(
            P(None, CTX),
            P(FSDP, CTX, None),
            P(FSDP, CTX, None),
            P(FSDP, CTX, None),
            P(FSDP, CTX, None),
            P(FSDP, CTX, None),
            P(FSDP, None, CTX),
            P(None, CTX, FSDP),
        ),
        out_specs=(P(FSDP, CTX, None), P(FSDP, CTX, None), P(FSDP, CTX, None), P(FSDP, None)),
        check_vma=False,
    )
```

time: 159 us -> 124 us (0.78)
  the two profiles are of different devices: /device:TPU:1 before, /device:TPU:121 now
where the time goes in v3:
time: 124 us; the launch traced here: 123 us
  starting transfers between devices  45.1 us (36%)
  blocking collectives  44.3 us (36%)
  waiting for transfers between devices  18.6 us (15%)
  Pallas kernels  9.56 us (8%)
  local copies, waits for them, and re-layouts  3.47 us (3%)
    all_to_all x4, starting transfers between devices, swap(): return lax.all_to_all(value, axis, 0, 0, tiled=True)  27.7 us
    all_gather x1, blocking collectives, whole(): mine = lax.all_gather(mine, 'zh', axis=0)  22.4 us
    all_gather x1, blocking collectives, whole(): kv_all = lax.all_gather(kv_own, 'zh', axis=0)  21.9 us
    ppermute x5, starting transfers between devices, ahead(): return lax.ppermute(value, axis, pairs)  17.3 us
    all_to_all x4, waiting for transfers between devices, swap(): return lax.all_to_all(value, axis, 0, 0, tiled=True)  13.6 us
    pallas_call x1, Pallas kernels, attention_grads(): pl.pallas_call(attention_kernel, out_shape=(struct((SIDE, HEAD_SIZE, STAC...  7.11 us
    ppermute x5, waiting for transfers between devices, ahead(): return lax.ppermute(value, axis, pairs)  4.94 us
  transfers between devices with their start and end apart: 9, of which 5 were waited for; matrix products, arithmetic and copies ran while one was open for 2% of the time, Pallas kernels for 0%

profile of v3, /device:TPU:121, one launch (start us, length us, event | category | flops | bytes accessed | tf_op | source)
XLA Modules:
  0.0 123.1 jit_solution(6915956167785000125)
XLA Ops:
  0.6 2.5 %pack.1 = (bf16[4,1312,128]{2,1,0:T(8,128)(2,1)}, bf16[272,128]{1,0:T(8,128)(2,1)}) custom-call(s32[1,8]{1,0:T(1,128)} %bitcast.64, bf16[1,128,640]{2,1,0:T(8,128)(2,1)} %q_ref.1, bf16[1,128,640]{2,1,0:T(8,128)(2,1)} %g_ref.1, bf16[1,128,640]{2,1,0:T(8,128)(2,1)} %o_ref.1, f32[5,1,128]{2,1,0:T(1,128)} %bitcast.63, bf16[1,128,128]{2,1,0:T(8,128)(2,1)} %k_ref.1, ...), custom_call_target="tpu_custom_call" | custom-call | tf_op jit(solution)/shard_map/pack/pallas_call | solution.py:119
  3.1 0.0 copy-start.2
  3.1 4.1 %all-to-all-start = ((bf16[4,1312,128]{2,1,0:T(8,128)(2,1)}), bf16[4,1312,128]{2,1,0:T(8,128)(2,1)S(1)}, u32[]{:S(2)}, u32[]{:S(2)}) async-start(bf16[4,1312,128]{2,1,0:T(8,128)(2,1)} %get-tuple-element.8), calls=%async_computation | async-start | bytes 2686976 | tf_op jit(solution)/shard_map/all_to_all | solution.py:153
  7.2 0.0 copy-start
  7.2 0.0 copy-done.2
  7.2 21.9 %all-gather = bf16[1088,128]{1,0:T(8,128)(2,1)S(1)} all-gather(bf16[272,128]{1,0:T(8,128)(2,1)S(1)} %copy-done.2), channel_id=2, replica_groups=mesh['x'=4,'zh'=4,'zl'=4,'yh'=2,'yl'=2,'c'=2] {'zh'}, dimensions={0}, use_global_device_ids=true | all-gather | bytes 348160 | tf_op jit(solution)/shard_map/all_gather | solution.py:184
  29.2 0.0 all-to-all-done.q_all
  29.2 7.1 %attention_grads.1 = (bf16[4,128,640]{2,1,0:T(8,128)(2,1)S(1)}, bf16[4,256,128]{2,1,0:T(8,128)(2,1)}) custom-call(bf16[4,1312,128]{2,1,0:T(8,128)(2,1)S(1)} %all-to-all-done.q_all, bf16[4,272,128]{2,1,0:T(8,128)(2,1)S(1)} %bitcast.54), custom_call_target="tpu_custom_call" | custom-call | tf_op jit(solution)/shard_map/attention_grads/pallas_call | solution.py:129
  36.3 5.3 %all-to-all-start.1 = ((bf16[4,256,128]{2,1,0:T(8,128)(2,1)}), bf16[4,256,128]{2,1,0:T(8,128)(2,1)S(1)}, u32[]{:S(2)}, u32[]{:S(2)}) async-start(bf16[4,256,128]{2,1,0:T(8,128)(2,1)} %get-tuple-element.11), calls=%async_computation.1 | async-start | bytes 524288 | tf_op jit(solution)/shard_map/all_to_all | solution.py:153
  41.5 0.0 copy-done
  41.5 2.4 %collective-permute-start.3 = (bf16[8,80,128]{2,1,0:T(8,128)(2,1)S(1)}, bf16[8,80,128]{2,1,0:T(8,128)(2,1)S(1)}, u32[]{:S(2)}, u32[]{:S(2)}) collective-permute-start(bf16[8,80,128]{2,1,0:T(8,128)(2,1)S(1)} %bitcast.60), channel_id=1, source_target_pairs={{0,2},{2,0},{1,3},{3,1},{4,6},{6,4},{5,7},{7,5},{8,10},{10,8},{9,1... | collective-permute-start | bytes 491528 | tf_op jit(solution)/shard_map/ppermute | solution.py:149
  43.9 3.7 %collective-permute-done.3 = bf16[8,80,128]{2,1,0:T(8,128)(2,1)S(1)} collective-permute-done((bf16[8,80,128]{2,1,0:T(8,128)(2,1)S(1)}, bf16[8,80,128]{2,1,0:T(8,128)(2,1)S(1)}, u32[]{:S(2)}, u32[]{:S(2)}) %collective-permute-start.3) | collective-permute-done | bytes 163872 | tf_op jit(solution)/shard_map/ppermute | solution.py:149
  47.6 7.6 %all-to-all-done.1 = bf16[4,256,128]{2,1,0:T(8,128)(2,1)S(1)} async-done(((bf16[4,256,128]{2,1,0:T(8,128)(2,1)}), bf16[4,256,128]{2,1,0:T(8,128)(2,1)S(1)}, u32[]{:S(2)}, u32[]{:S(2)}) %all-to-all-start.1) | async-done | bytes 262176 | tf_op jit(solution)/shard_map/all_to_all | solution.py:153
  55.2 0.6 slice_reduce_fusion
  55.8 0.0 copy-start.1
  55.8 0.7 broadcast_in_dim.10
  56.6 12.9 %all-to-all-start.2 = ((bf16[8,128,128]{2,1,0:T(8,128)(2,1)}), bf16[8,128,128]{2,1,0:T(8,128)(2,1)S(1)}, u32[]{:S(2)}, u32[]{:S(2)}) async-start(bf16[8,128,128]{2,1,0:T(8,128)(2,1)} %broadcast_in_dim.10), calls=%async_computation.2 | async-start | bytes 524288 | tf_op jit(solution)/shard_map/all_to_all | solution.py:153
  69.6 5.2 %collective-permute-start.4 = (bf16[2,8,80,128]{3,2,1,0:T(8,128)(2,1)S(1)}, bf16[2,8,80,128]{3,2,1,0:T(8,128)(2,1)S(1)}, u32[]{:S(2)}, u32[]{:S(2)}) collective-permute-start(bf16[2,8,80,128]{3,2,1,0:T(8,128)(2,1)S(1)} %pad_maximum_fusion), channel_id=1, source_target_pairs={{0,1},{1,0},{2,3},{3,2},{4,5},{5,4},{6,7},{7,6},{8,9},{9,8},{10,11... | collective-permute-start | bytes 983048 | tf_op jit(solution)/shard_map/ppermute | solution.py:149
  74.8 1.2 collective-permute-done.4
  76.0 0.0 copy-done.1
  76.0 0.1 maximum_bitcast_fusion
  76.2 0.1 dynamic-slice_bitcast_fusion.2
  76.2 3.4 %collective-permute-start.2 = (bf16[128,640]{1,0:T(8,128)(2,1)S(1)}, bf16[128,640]{1,0:T(8,128)(2,1)S(1)}, u32[]{:S(2)}, u32[]{:S(2)}) collective-permute-start(bf16[128,640]{1,0:T(8,128)(2,1)S(1)} %get-tuple-element.41), channel_id=1, source_target_pairs={{0,384},{128,0},{256,128},{384,256},{1,385},{129,1},{257,129},{385... | collective-permute-start | bytes 491528 | tf_op jit(solution)/shard_map/ppermute | solution.py:149
  79.7 3.6 %collective-permute-start.1 = (bf16[128,640]{1,0:T(8,128)(2,1)S(1)}, bf16[128,640]{1,0:T(8,128)(2,1)S(1)}, u32[]{:S(2)}, u32[]{:S(2)}) collective-permute-start(bf16[128,640]{1,0:T(8,128)(2,1)S(1)} %get-tuple-element.42), channel_id=1, source_target_pairs={{0,256},{128,384},{256,0},{384,128},{1,257},{129,385},{257,1},{385... | collective-permute-start | bytes 491528 | tf_op jit(solution)/shard_map/ppermute | solution.py:149
  83.3 2.8 %collective-permute-start = (bf16[128,640]{1,0:T(8,128)(2,1)S(1)}, bf16[128,640]{1,0:T(8,128)(2,1)S(1)}, u32[]{:S(2)}, u32[]{:S(2)}) collective-permute-start(bf16[128,640]{1,0:T(8,128)(2,1)S(1)} %get-tuple-element.40), channel_id=1, source_target_pairs={{0,128},{128,256},{256,384},{384,0},{1,129},{129,257},{257,385},{3... | collective-permute-start | bytes 491528 | tf_op jit(solution)/shard_map/ppermute | solution.py:149
  86.0 0.0 all-to-all-done.2
  86.0 0.3 fusion
  86.4 0.8 broadcast_in_dim.22
  87.2 5.4 %all-to-all-start.3 = ((bf16[16,80,128]{2,1,0:T(8,128)(2,1)}), bf16[16,80,128]{2,1,0:T(8,128)(2,1)S(1)}, u32[]{:S(2)}, u32[]{:S(2)}) async-start(bf16[16,80,128]{2,1,0:T(8,128)(2,1)} %bitcast.22), calls=%async_computation.3 | async-start | bytes 655360 | tf_op jit(solution)/shard_map/all_to_all | solution.py:153
  92.6 0.0 collective-permute-done.2
  92.6 0.0 collective-permute-done.1
  92.6 0.1 collective-permute-done
  92.7 0.2 copy.33
  92.9 0.2 copy.34
  93.0 0.8 copy.37
  93.9 6.1 %all-to-all-done.3 = bf16[16,80,128]{2,1,0:T(8,128)(2,1)S(1)} async-done(((bf16[16,80,128]{2,1,0:T(8,128)(2,1)}), bf16[16,80,128]{2,1,0:T(8,128)(2,1)S(1)}, u32[]{:S(2)}, u32[]{:S(2)}) %all-to-all-start.3) | async-done | bytes 327712 | tf_op jit(solution)/shard_map/all_to_all | solution.py:153
  100.0 22.4 %all-gather.1 = bf16[16,80,128]{2,1,0:T(8,128)(2,1)S(1)} all-gather(bf16[4,80,128]{2,1,0:T(8,128)(2,1)S(1)} %reduce_sum.69), channel_id=3, replica_groups=mesh['x'=4,'zh'=4,'zl'=4,'yh'=2,'yl'=2,'c'=2] {'zh'}, dimensions={0}, use_global_device_ids=true | all-gather | bytes 409600 | tf_op jit(solution)/shard_map/all_gather | solution.py:202
  122.4 0.7 copy_bitcast_fusion
  (7 shorter events, 0.3 us)
Async XLA Ops:
  3.1 4.2 %copy-start.2 = (bf16[272,128]{1,0:T(8,128)(2,1)S(1)}, bf16[272,128]{1,0:T(8,128)(2,1)}, u32[]{:S(2)}) copy-start(bf16[272,128]{1,0:T(8,128)(2,1)} %get-tuple-element.9) | copy-start | bytes 208900
  3.1 26.1 %all-to-all-start = ((bf16[4,1312,128]{2,1,0:T(8,128)(2,1)}), bf16[4,1312,128]{2,1,0:T(8,128)(2,1)S(1)}, u32[]{:S(2)}, u32[]{:S(2)}) async-start(bf16[4,1312,128]{2,1,0:T(8,128)(2,1)} %get-tuple-element.8), calls=%async_computation | async-start | bytes 2686976 | tf_op jit(solution)/shard_map/all_to_all | solution.py:153
  7.2 34.3 %copy-start = (bf16[8,128,80]{1,2,0:T(8,128)(2,1)S(1)}, bf16[8,128,80]{1,2,0:T(8,128)(2,1)}, u32[]{:S(2)}) copy-start(bf16[8,128,80]{1,2,0:T(8,128)(2,1)} %param.15) | copy-start | bytes 491524
  36.3 18.9 %all-to-all-start.1 = ((bf16[4,256,128]{2,1,0:T(8,128)(2,1)}), bf16[4,256,128]{2,1,0:T(8,128)(2,1)S(1)}, u32[]{:S(2)}, u32[]{:S(2)}) async-start(bf16[4,256,128]{2,1,0:T(8,128)(2,1)} %get-tuple-element.11), calls=%async_computation.1 | async-start | bytes 524288 | tf_op jit(solution)/shard_map/all_to_all | solution.py:153
  41.5 6.1 %collective-permute-start.3 = (bf16[8,80,128]{2,1,0:T(8,128)(2,1)S(1)}, bf16[8,80,128]{2,1,0:T(8,128)(2,1)S(1)}, u32[]{:S(2)}, u32[]{:S(2)}) collective-permute-start(bf16[8,80,128]{2,1,0:T(8,128)(2,1)S(1)} %bitcast.60), channel_id=1, source_target_pairs={{0,2},{2,0},{1,3},{3,1},{4,6},{6,4},{5,7},{7,5},{8,10},{10,8},{9,1... | collective-permute-start | bytes 491528 | tf_op jit(solution)/shard_map/ppermute | solution.py:149
  55.8 20.2 %copy-start.1 = (bf16[128,128]{1,0:T(8,128)(2,1)}, bf16[128,128]{1,0:T(8,128)(2,1)S(1)}, u32[]{:S(2)}) copy-start(bf16[128,128]{1,0:T(8,128)(2,1)S(1)} %get-tuple-element.37) | copy-start | bytes 98308
  56.6 29.5 %all-to-all-start.2 = ((bf16[8,128,128]{2,1,0:T(8,128)(2,1)}), bf16[8,128,128]{2,1,0:T(8,128)(2,1)S(1)}, u32[]{:S(2)}, u32[]{:S(2)}) async-start(bf16[8,128,128]{2,1,0:T(8,128)(2,1)} %broadcast_in_dim.10), calls=%async_computation.2 | async-start | bytes 524288 | tf_op jit(solution)/shard_map/all_to_all | solution.py:153
  69.6 6.4 %collective-permute-start.4 = (bf16[2,8,80,128]{3,2,1,0:T(8,128)(2,1)S(1)}, bf16[2,8,80,128]{3,2,1,0:T(8,128)(2,1)S(1)}, u32[]{:S(2)}, u32[]{:S(2)}) collective-permute-start(bf16[2,8,80,128]{3,2,1,0:T(8,128)(2,1)S(1)} %pad_maximum_fusion), channel_id=1, source_target_pairs={{0,1},{1,0},{2,3},{3,2},{4,5},{5,4},{6,7},{7,6},{8,9},{9,8},{10,11... | collective-permute-start | bytes 983048 | tf_op jit(solution)/shard_map/ppermute | solution.py:149
  76.2 16.3 %collective-permute-start.2 = (bf16[128,640]{1,0:T(8,128)(2,1)S(1)}, bf16[128,640]{1,0:T(8,128)(2,1)S(1)}, u32[]{:S(2)}, u32[]{:S(2)}) collective-permute-start(bf16[128,640]{1,0:T(8,128)(2,1)S(1)} %get-tuple-element.41), channel_id=1, source_target_pairs={{0,384},{128,0},{256,128},{384,256},{1,385},{129,1},{257,129},{385... | collective-permute-start | bytes 491528 | tf_op jit(solution)/shard_map/ppermute | solution.py:149
  79.7 12.9 %collective-permute-start.1 = (bf16[128,640]{1,0:T(8,128)(2,1)S(1)}, bf16[128,640]{1,0:T(8,128)(2,1)S(1)}, u32[]{:S(2)}, u32[]{:S(2)}) collective-permute-start(bf16[128,640]{1,0:T(8,128)(2,1)S(1)} %get-tuple-element.42), channel_id=1, source_target_pairs={{0,256},{128,384},{256,0},{384,128},{1,257},{129,385},{257,1},{385... | collective-permute-start | bytes 491528 | tf_op jit(solution)/shard_map/ppermute | solution.py:149
  83.3 9.4 %collective-permute-start = (bf16[128,640]{1,0:T(8,128)(2,1)S(1)}, bf16[128,640]{1,0:T(8,128)(2,1)S(1)}, u32[]{:S(2)}, u32[]{:S(2)}) collective-permute-start(bf16[128,640]{1,0:T(8,128)(2,1)S(1)} %get-tuple-element.40), channel_id=1, source_target_pairs={{0,128},{128,256},{256,384},{384,0},{1,129},{129,257},{257,385},{3... | collective-permute-start | bytes 491528 | tf_op jit(solution)/shard_map/ppermute | solution.py:149
  87.2 12.8 %all-to-all-start.3 = ((bf16[16,80,128]{2,1,0:T(8,128)(2,1)}), bf16[16,80,128]{2,1,0:T(8,128)(2,1)S(1)}, u32[]{:S(2)}, u32[]{:S(2)}) async-start(bf16[16,80,128]{2,1,0:T(8,128)(2,1)} %bitcast.22), calls=%async_computation.3 | async-start | bytes 655360 | tf_op jit(solution)/shard_map/all_to_all | solution.py:153

commit v4 on v3

--- a/solution.py
+++ b/solution.py
@@ -65,46 +65,84 @@
     return jnp.max(rows.astype(jnp.float32)).astype(jnp.int32)
 
 
-def attention_kernel(q_all, kv_ref, dq_ref, dkv_ref, dq_acc, dk_acc, dv_acc, k_t, k_place):
+def attention_kernel(
+    q_all, kv_ref, dq_ref, dkv_ref, k_s, v_s, k_t, dk_acc, dv_acc, rank, sorted_place
+):
     dk_acc[...] = jnp.zeros_like(dk_acc)
     dv_acc[...] = jnp.zeros_like(dv_acc)
     key_row = lax.broadcasted_iota(jnp.int32, (BLOCK, STACK), 0)
     query_col = lax.broadcasted_iota(jnp.int32, (BLOCK, STACK), 1) & (BLOCK - 1)
     offset = key_row - query_col
+    places = [place_of(kv_ref[j, 2 * BLOCK :, :]) for j in range(SIDE)]
     for j in range(SIDE):
-        k_t[j] = kv_ref[j, :BLOCK, :].T
-        k_place[j] = place_of(kv_ref[j, 2 * BLOCK :, :])
-    for i in range(SIDE):
+        r = sum((places[m] < places[j]).astype(jnp.int32) for m in range(SIDE) if m != j)
+        rank[j] = r
+        sorted_place[r] = places[j]
+        at = pl.multiple_of(r * BLOCK, BLOCK)
+        k = kv_ref[j, :BLOCK, :]
+        k_s[pl.ds(at, BLOCK), :] = k
+        v_s[pl.ds(at, BLOCK), :] = kv_ref[j, BLOCK : 2 * BLOCK, :]
+        k_t[r] = k.T
+
+    def row(i, carry):
         q_ref = q_all.at[i]
-        dq_acc[...] = jnp.zeros_like(dq_acc)
         extra = q_ref[2 * STACK :, :].astype(jnp.float32)
         norm = extra[0:5] + extra[5:10] + extra[10:15]
         delta = extra[15:20] + extra[20:25] + extra[25:30]
         norm = jnp.concatenate([norm[h : h + 1] for h in range(HEADS)], axis=1)
         delta = jnp.concatenate([delta[h : h + 1] for h in range(HEADS)], axis=1)
         here = place_of(extra[30:32])
-
-        def pair(j, carry):
-            ahead = (here - k_place[j]) * BLOCK
-
-            @pl.when(ahead >= 0)
-            def _():
+        seen = sum((sorted_place[j] <= here).astype(jnp.int32) for j in range(SIDE))
+
+        @pl.when(seen == 0)
+        def _():
+            dq_ref[i] = jnp.zeros((HEAD_SIZE, STACK), jnp.bfloat16)
+
+        for count in range(1, SIDE + 1):
+
+            @pl.when(seen == count)
+            def _(count=count):
+                rows = count * BLOCK
                 q = q_ref[:STACK, :]
                 g = q_ref[STACK : 2 * STACK, :]
-                scores = dot(kv_ref[j, :BLOCK, :], q, ((1,), (1,))) * (SCALE * LOG2E)
-                probs = jnp.where(offset <= ahead, jnp.exp2(scores - norm), 0.0)
-                dprobs = dot(kv_ref[j, BLOCK : 2 * BLOCK, :], g, ((1,), (1,)))
+                last = (here - sorted_place[count - 1]) * BLOCK
+                scores = dot(k_s[:rows, :], q, ((1,), (1,))) * (SCALE * LOG2E)
+                probs = jnp.exp2(scores - norm)
+                tail = jnp.where(offset <= last, probs[rows - BLOCK :], 0.0)
+                probs = jnp.concatenate([probs[: rows - BLOCK], tail], axis=0) if count > 1 else tail
+                dprobs = dot(v_s[:rows, :], g, ((1,), (1,)))
                 dscores = (probs * (dprobs - delta) * SCALE).astype(jnp.bfloat16)
-                dv_acc[j] += dot(probs.astype(jnp.bfloat16), g, ((1,), (0,)))
-                dk_acc[j] += dot(dscores, q, ((1,), (0,)))
-                dq_acc[...] += dot(k_t[j], dscores, ((1,), (0,)))
-
-            return carry
-
-        lax.fori_loop(0, SIDE, pair, 0)
-        dq_ref[i] = dq_acc[...].astype(jnp.bfloat16)
-    dkv_ref[:, :BLOCK, :] = dk_acc[...].astype(jnp.bfloat16)
-    dkv_ref[:, BLOCK:, :] = dv_acc[...].astype(jnp.bfloat16)
+                dv_acc[:rows, :] += dot(probs.astype(jnp.bfloat16), g, ((1,), (0,)))
+                dk_acc[:rows, :] += dot(dscores, q, ((1,), (0,)))
+                k_cols = jnp.concatenate([k_t[j] for j in range(count)], axis=1)
+                dq_ref[i] = dot(k_cols, dscores, ((1,), (0,))).astype(jnp.bfloat16)
+
+        return carry
+
+    lax.fori_loop(0, SIDE, row, 0)
+    for j in range(SIDE):
+        at = pl.multiple_of(rank[j] * BLOCK, BLOCK)
+        dkv_ref[j, :BLOCK, :] = dk_acc[pl.ds(at, BLOCK), :].astype(jnp.bfloat16)
+        dkv_ref[j, BLOCK:, :] = dv_acc[pl.ds(at, BLOCK), :].astype(jnp.bfloat16)
+
+
+def fold_kernel(parts, copies_out, key_out, value_out):
+    key = sum(parts[j, :BLOCK, :].astype(jnp.float32) for j in range(SIDE)).astype(jnp.bfloat16)
+    for copy in range(8):
+        copies_out[copy] = key
+    key_out[0] = key
+    value = sum(parts[j, BLOCK:, :].astype(jnp.float32) for j in range(SIDE))
+    value_out[0] = value.astype(jnp.bfloat16)
+
+
+def weight_kernel(rows, keys, out_ref):
+    for f in range(SIDE):
+        total = dot(rows[f, 0], keys[0], ((1,), (0,)))
+        for s in range(1, 8):
+            total += dot(rows[f, s], keys[s], ((1,), (0,)))
+        total = total.astype(jnp.bfloat16)
+        for copy in range(SIDE):
+            out_ref[copy * SIDE + f] = total
 
 
 SMEM = pl.BlockSpec(memory_space=pltpu.SMEM)
@@ -132,10 +170,12 @@
         in_specs=[VMEM] * 2,
         out_specs=(VMEM,) * 2,
         scratch_shapes=[
-            pltpu.VMEM((HEAD_SIZE, STACK), jnp.float32),
-            pltpu.VMEM((SIDE, BLOCK, HEAD_SIZE), jnp.float32),
-            pltpu.VMEM((SIDE, BLOCK, HEAD_SIZE), jnp.float32),
+            pltpu.VMEM((SIDE * BLOCK, HEAD_SIZE), jnp.bfloat16),
+            pltpu.VMEM((SIDE * BLOCK, HEAD_SIZE), jnp.bfloat16),
             pltpu.VMEM((SIDE, HEAD_SIZE, BLOCK), jnp.bfloat16),
+            pltpu.VMEM((SIDE * BLOCK, HEAD_SIZE), jnp.float32),
+            pltpu.VMEM((SIDE * BLOCK, HEAD_SIZE), jnp.float32),
+            pltpu.SMEM((SIDE,), jnp.int32),
             pltpu.SMEM((SIDE,), jnp.int32),
         ],
         compiler_params=pltpu.CompilerParams(vmem_limit_bytes=GRANT),
@@ -143,6 +183,29 @@
     )(q_all, kv_all)
 
 
+def fold(parts):
+    block = (1, BLOCK, HEAD_SIZE)
+    return pl.pallas_call(
+        fold_kernel,
+        out_shape=(struct((8, BLOCK, HEAD_SIZE)), struct(block), struct(block)),
+        in_specs=[VMEM],
+        out_specs=(VMEM,) * 3,
+        compiler_params=pltpu.CompilerParams(vmem_limit_bytes=GRANT),
+        name="fold",
+    )(parts)
+
+
+def weight_products(rows, keys):
+    return pl.pallas_call(
+        weight_kernel,
+        out_shape=struct((SIDE * SIDE, rows.shape[2], HEAD_SIZE)),
+        in_specs=[VMEM] * 2,
+        out_specs=VMEM,
+        compiler_params=pltpu.CompilerParams(vmem_limit_bytes=GRANT),
+        name="weight_products",
+    )(rows, keys)
+
+
 def ahead(value, axis, steps):
     count = lax.axis_size(axis)
     pairs = [(source, (source + steps) % count) for source in range(count)]
@@ -151,10 +214,6 @@
 
 def swap(value, axis):
     return lax.all_to_all(value, axis, 0, 0, tiled=True)
-
-
-def copies(value, count):
-    return jnp.broadcast_to(value[None], (count,) + value.shape)
 
 
 def total(parts):
@@ -185,8 +244,7 @@
     dq, dkv = attention_grads(q_all, kv_all)
 
     dkv = swap(dkv, "zh")
-    key_gradient = total(dkv[:, :BLOCK]).astype(jnp.bfloat16)
-    value_gradient = total(dkv[:, BLOCK:]).astype(jnp.bfloat16)
+    key_copies, key_gradient, value_gradient = fold(dkv)
     here = lax.axis_index("x")
     pieces = [lax.dynamic_index_in_dim(dq, (here + s) % SIDE, 0, keepdims=False) for s in range(SIDE)]
     dq = pieces[:1] + [ahead(pieces[s], "x", s) for s in (1, 2, 3)]
@@ -194,15 +252,14 @@
     grad_q = grad_q.reshape(HEAD_SIZE, HEADS, BLOCK).transpose(2, 1, 0).reshape(BLOCK, STACK)
 
     weights = row_features(features)
-    gathered = swap(copies(key_gradient, 8), ("zl", "yh"))
-    partial = jnp.einsum("fsit,stj->fij", weights, gathered, preferred_element_type=jnp.float32)
-    partial = copies(partial.astype(jnp.bfloat16), SIDE).reshape((16,) + partial.shape[1:])
+    gathered = swap(key_copies, ("zl", "yh"))
+    partial = weight_products(weights, gathered)
     partial = swap(partial, ("x", "yl", "c"))
     mine = total(partial.reshape((SIDE, SIDE) + partial.shape[1:])).astype(jnp.bfloat16)
     mine = lax.all_gather(mine, "zh", axis=0)
     width = features.shape[-1]
     grad_wk = total(mine).transpose(1, 0, 2).reshape(width, SIDE * HEAD_SIZE)
-    return (grad_q.astype(jnp.bfloat16)[None], key_gradient[None], value_gradient[None], grad_wk)
+    return (grad_q.astype(jnp.bfloat16)[None], key_gradient, value_gradient, grad_wk)
 
 
 def solution(mesh):

time: 124 us -> 121 us (0.976)
  the two profiles are of different devices: /device:TPU:121 before, /device:TPU:113 now
where the time goes in v4:
time: 121 us; the launch traced here: 120 us
  starting transfers between devices  45.3 us (37%)
  blocking collectives  44.1 us (36%)
  waiting for transfers between devices  18.7 us (15%)
  Pallas kernels  9.04 us (7%)
  local copies, waits for them, and re-layouts  1.95 us (2%)
    all_to_all x4, starting transfers between devices, swap(): return lax.all_to_all(value, axis, 0, 0, tiled=True)  28.4 us
    all_gather x1, blocking collectives, whole(): mine = lax.all_gather(mine, 'zh', axis=0)  22.1 us
    all_gather x1, blocking collectives, whole(): kv_all = lax.all_gather(kv_own, 'zh', axis=0)  21.9 us
    ppermute x5, starting transfers between devices, ahead(): return lax.ppermute(value, axis, pairs)  16.9 us
    all_to_all x4, waiting for transfers between devices, swap(): return lax.all_to_all(value, axis, 0, 0, tiled=True)  13.3 us
    ppermute x5, waiting for transfers between devices, ahead(): return lax.ppermute(value, axis, pairs)  5.47 us
    pallas_call x1, Pallas kernels, attention_grads(): pl.pallas_call(attention_kernel, out_shape=(struct((SIDE, HEAD_SIZE, STAC...  4.64 us
    pallas_call x1, Pallas kernels, pack(): pl.pallas_call(pack_kernel, out_shape=(struct((SIDE, Q_ROWS, HEAD_SIZE)),...  2.45 us
  transfers between devices with their start and end apart: 9, of which 5 were waited for; matrix products, arithmetic and copies ran while one was open for 1% of the time, Pallas kernels for 1%

profile of v4, /device:TPU:113, one launch (start us, length us, event | category | flops | bytes accessed | tf_op | source)
XLA Modules:
  0.0 120.2 jit_solution(13026477816244443824)
XLA Ops:
  0.6 2.4 %pack.1 = (bf16[4,1312,128]{2,1,0:T(8,128)(2,1)}, bf16[272,128]{1,0:T(8,128)(2,1)}) custom-call(s32[1,8]{1,0:T(1,128)} %bitcast.50, bf16[1,128,640]{2,1,0:T(8,128)(2,1)} %q_ref.1, bf16[1,128,640]{2,1,0:T(8,128)(2,1)} %g_ref.1, bf16[1,128,640]{2,1,0:T(8,128)(2,1)} %o_ref.1, f32[5,1,128]{2,1,0:T(1,128)} %bitcast.49, bf16[1,128,128]{2,1,0:T(8,128)(2,1)} %k_ref.1, ...), custom_call_target="tpu_custom_call" | custom-call | tf_op jit(solution)/shard_map/pack/pallas_call | solution.py:157
  3.1 0.0 copy-start.1
  3.1 4.1 %all-to-all-start = ((bf16[4,1312,128]{2,1,0:T(8,128)(2,1)}), bf16[4,1312,128]{2,1,0:T(8,128)(2,1)S(1)}, u32[]{:S(2)}, u32[]{:S(2)}) async-start(bf16[4,1312,128]{2,1,0:T(8,128)(2,1)} %get-tuple-element.11), calls=%async_computation | async-start | bytes 2686976 | tf_op jit(solution)/shard_map/all_to_all | solution.py:216
  7.2 0.0 copy-start
  7.2 0.0 copy-done.1
  7.2 21.9 %all-gather = bf16[1088,128]{1,0:T(8,128)(2,1)S(1)} all-gather(bf16[272,128]{1,0:T(8,128)(2,1)S(1)} %copy-done.1), channel_id=2, replica_groups=mesh['x'=4,'zh'=4,'zl'=4,'yh'=2,'yl'=2,'c'=2] {'zh'}, dimensions={0}, use_global_device_ids=true | all-gather | bytes 348160 | tf_op jit(solution)/shard_map/all_gather | solution.py:243
  29.2 0.0 all-to-all-done.q_all
  29.2 4.6 %attention_grads.1 = (bf16[4,128,640]{2,1,0:T(8,128)(2,1)S(1)}, bf16[4,256,128]{2,1,0:T(8,128)(2,1)}) custom-call(bf16[4,1312,128]{2,1,0:T(8,128)(2,1)S(1)} %all-to-all-done.q_all, bf16[4,272,128]{2,1,0:T(8,128)(2,1)S(1)} %bitcast.43), custom_call_target="tpu_custom_call" | custom-call | tf_op jit(solution)/shard_map/attention_grads/pallas_call | solution.py:167
  33.8 6.3 %all-to-all-start.1 = ((bf16[4,256,128]{2,1,0:T(8,128)(2,1)}), bf16[4,256,128]{2,1,0:T(8,128)(2,1)S(1)}, u32[]{:S(2)}, u32[]{:S(2)}) async-start(bf16[4,256,128]{2,1,0:T(8,128)(2,1)} %get-tuple-element.14), calls=%async_computation.1 | async-start | bytes 524288 | tf_op jit(solution)/shard_map/all_to_all | solution.py:216
  40.1 0.0 copy-done
  40.1 2.9 %collective-permute-start.3 = (bf16[8,80,128]{2,1,0:T(8,128)(2,1)S(1)}, bf16[8,80,128]{2,1,0:T(8,128)(2,1)S(1)}, u32[]{:S(2)}, u32[]{:S(2)}) collective-permute-start(bf16[8,80,128]{2,1,0:T(8,128)(2,1)S(1)} %bitcast.48), channel_id=1, source_target_pairs={{0,2},{2,0},{1,3},{3,1},{4,6},{6,4},{5,7},{7,5},{8,10},{10,8},{9,1... | collective-permute-start | bytes 491528 | tf_op jit(solution)/shard_map/ppermute | solution.py:212
  43.0 3.1 %collective-permute-done.3 = bf16[8,80,128]{2,1,0:T(8,128)(2,1)S(1)} collective-permute-done((bf16[8,80,128]{2,1,0:T(8,128)(2,1)S(1)}, bf16[8,80,128]{2,1,0:T(8,128)(2,1)S(1)}, u32[]{:S(2)}, u32[]{:S(2)}) %collective-permute-start.3) | collective-permute-done | bytes 163872 | tf_op jit(solution)/shard_map/ppermute | solution.py:212
  46.2 7.7 %all-to-all-done.1.parts = bf16[4,256,128]{2,1,0:T(8,128)(2,1)S(1)} async-done(((bf16[4,256,128]{2,1,0:T(8,128)(2,1)}), bf16[4,256,128]{2,1,0:T(8,128)(2,1)S(1)}, u32[]{:S(2)}, u32[]{:S(2)}) %all-to-all-start.1) | async-done | bytes 262176 | tf_op jit(solution)/shard_map/all_to_all | solution.py:216
  53.8 0.7 fold.1
  54.5 12.9 %all-to-all-start.2 = ((bf16[8,128,128]{2,1,0:T(8,128)(2,1)}), bf16[8,128,128]{2,1,0:T(8,128)(2,1)S(1)}, u32[]{:S(2)}, u32[]{:S(2)}) async-start(bf16[8,128,128]{2,1,0:T(8,128)(2,1)} %get-tuple-element.17), calls=%async_computation.2 | async-start | bytes 524288 | tf_op jit(solution)/shard_map/all_to_all | solution.py:216
  67.5 4.8 %collective-permute-start.4 = (bf16[2,8,80,128]{3,2,1,0:T(8,128)(2,1)S(1)}, bf16[2,8,80,128]{3,2,1,0:T(8,128)(2,1)S(1)}, u32[]{:S(2)}, u32[]{:S(2)}) collective-permute-start(bf16[2,8,80,128]{3,2,1,0:T(8,128)(2,1)S(1)} %pad_maximum_fusion), channel_id=1, source_target_pairs={{0,1},{1,0},{2,3},{3,2},{4,5},{5,4},{6,7},{7,6},{8,9},{9,8},{10,11... | collective-permute-start | bytes 983048 | tf_op jit(solution)/shard_map/ppermute | solution.py:212
  72.3 1.2 collective-permute-done.4
  73.6 0.1 dynamic-slice_bitcast_fusion.2
  73.6 4.1 %collective-permute-start.2 = (bf16[128,640]{1,0:T(8,128)(2,1)S(1)}, bf16[128,640]{1,0:T(8,128)(2,1)S(1)}, u32[]{:S(2)}, u32[]{:S(2)}) collective-permute-start(bf16[128,640]{1,0:T(8,128)(2,1)S(1)} %get-tuple-element.41), channel_id=1, source_target_pairs={{0,384},{128,0},{256,128},{384,256},{1,385},{129,1},{257,129},{385... | collective-permute-start | bytes 491528 | tf_op jit(solution)/shard_map/ppermute | solution.py:212
  77.7 2.4 %collective-permute-start.1 = (bf16[128,640]{1,0:T(8,128)(2,1)S(1)}, bf16[128,640]{1,0:T(8,128)(2,1)S(1)}, u32[]{:S(2)}, u32[]{:S(2)}) collective-permute-start(bf16[128,640]{1,0:T(8,128)(2,1)S(1)} %get-tuple-element.42), channel_id=1, source_target_pairs={{0,256},{128,384},{256,0},{384,128},{1,257},{129,385},{257,1},{385... | collective-permute-start | bytes 491528 | tf_op jit(solution)/shard_map/ppermute | solution.py:212
  80.1 2.8 %collective-permute-start = (bf16[128,640]{1,0:T(8,128)(2,1)S(1)}, bf16[128,640]{1,0:T(8,128)(2,1)S(1)}, u32[]{:S(2)}, u32[]{:S(2)}) collective-permute-start(bf16[128,640]{1,0:T(8,128)(2,1)S(1)} %get-tuple-element.40), channel_id=1, source_target_pairs={{0,128},{128,256},{256,384},{384,0},{1,129},{129,257},{257,385},{3... | collective-permute-start | bytes 491528 | tf_op jit(solution)/shard_map/ppermute | solution.py:212
  82.9 0.1 maximum_bitcast_fusion
  83.0 0.0 all-to-all-done.2.keys
  83.0 1.2 %weight_products.1 = bf16[16,80,128]{2,1,0:T(8,128)(2,1)} custom-call(bf16[4,8,80,128]{3,2,1,0:T(8,128)(2,1)S(1)} %bitcast.42, bf16[8,128,128]{2,1,0:T(8,128)(2,1)S(1)} %all-to-all-done.2.keys), custom_call_target="tpu_custom_call" | custom-call | tf_op jit(solution)/shard_map/weight_products/pallas_call | solution.py:199
  84.2 5.0 %all-to-all-start.3 = ((bf16[16,80,128]{2,1,0:T(8,128)(2,1)}), bf16[16,80,128]{2,1,0:T(8,128)(2,1)S(1)}, u32[]{:S(2)}, u32[]{:S(2)}) async-start(bf16[16,80,128]{2,1,0:T(8,128)(2,1)} %weight_products.1), calls=%async_computation.3 | async-start | bytes 655360 | tf_op jit(solution)/shard_map/all_to_all | solution.py:216
  89.3 0.0 collective-permute-done.2
  89.3 0.0 collective-permute-done.1
  89.3 1.1 collective-permute-done
  90.5 0.2 copy.28
  90.7 0.2 copy.29
  90.8 0.8 copy.32
  91.7 5.6 %all-to-all-done.3 = bf16[16,80,128]{2,1,0:T(8,128)(2,1)S(1)} async-done(((bf16[16,80,128]{2,1,0:T(8,128)(2,1)}), bf16[16,80,128]{2,1,0:T(8,128)(2,1)S(1)}, u32[]{:S(2)}, u32[]{:S(2)}) %all-to-all-start.3) | async-done | bytes 327712 | tf_op jit(solution)/shard_map/all_to_all | solution.py:216
  97.3 22.1 %all-gather.1 = bf16[16,80,128]{2,1,0:T(8,128)(2,1)S(1)} all-gather(bf16[4,80,128]{2,1,0:T(8,128)(2,1)S(1)} %reduce_sum.43), channel_id=3, replica_groups=mesh['x'=4,'zh'=4,'zl'=4,'yh'=2,'yl'=2,'c'=2] {'zh'}, dimensions={0}, use_global_device_ids=true | all-gather | bytes 409600 | tf_op jit(solution)/shard_map/all_gather | solution.py:259
  119.5 0.7 copy_bitcast_fusion
  (7 shorter events, 0.3 us)
Async XLA Ops:
  3.1 4.2 %copy-start.1 = (bf16[272,128]{1,0:T(8,128)(2,1)S(1)}, bf16[272,128]{1,0:T(8,128)(2,1)}, u32[]{:S(2)}) copy-start(bf16[272,128]{1,0:T(8,128)(2,1)} %get-tuple-element.12) | copy-start | bytes 208900
  3.1 26.1 %all-to-all-start = ((bf16[4,1312,128]{2,1,0:T(8,128)(2,1)}), bf16[4,1312,128]{2,1,0:T(8,128)(2,1)S(1)}, u32[]{:S(2)}, u32[]{:S(2)}) async-start(bf16[4,1312,128]{2,1,0:T(8,128)(2,1)} %get-tuple-element.11), calls=%async_computation | async-start | bytes 2686976 | tf_op jit(solution)/shard_map/all_to_all | solution.py:216
  7.2 32.8 %copy-start = (bf16[8,128,80]{1,2,0:T(8,128)(2,1)S(1)}, bf16[8,128,80]{1,2,0:T(8,128)(2,1)}, u32[]{:S(2)}) copy-start(bf16[8,128,80]{1,2,0:T(8,128)(2,1)} %param.15) | copy-start | bytes 491524
  33.8 20.0 %all-to-all-start.1 = ((bf16[4,256,128]{2,1,0:T(8,128)(2,1)}), bf16[4,256,128]{2,1,0:T(8,128)(2,1)S(1)}, u32[]{:S(2)}, u32[]{:S(2)}) async-start(bf16[4,256,128]{2,1,0:T(8,128)(2,1)} %get-tuple-element.14), calls=%async_computation.1 | async-start | bytes 524288 | tf_op jit(solution)/shard_map/all_to_all | solution.py:216
  40.1 6.1 %collective-permute-start.3 = (bf16[8,80,128]{2,1,0:T(8,128)(2,1)S(1)}, bf16[8,80,128]{2,1,0:T(8,128)(2,1)S(1)}, u32[]{:S(2)}, u32[]{:S(2)}) collective-permute-start(bf16[8,80,128]{2,1,0:T(8,128)(2,1)S(1)} %bitcast.48), channel_id=1, source_target_pairs={{0,2},{2,0},{1,3},{3,1},{4,6},{6,4},{5,7},{7,5},{8,10},{10,8},{9,1... | collective-permute-start | bytes 491528 | tf_op jit(solution)/shard_map/ppermute | solution.py:212
  54.5 28.5 %all-to-all-start.2 = ((bf16[8,128,128]{2,1,0:T(8,128)(2,1)}), bf16[8,128,128]{2,1,0:T(8,128)(2,1)S(1)}, u32[]{:S(2)}, u32[]{:S(2)}) async-start(bf16[8,128,128]{2,1,0:T(8,128)(2,1)} %get-tuple-element.17), calls=%async_computation.2 | async-start | bytes 524288 | tf_op jit(solution)/shard_map/all_to_all | solution.py:216
  67.5 6.0 %collective-permute-start.4 = (bf16[2,8,80,128]{3,2,1,0:T(8,128)(2,1)S(1)}, bf16[2,8,80,128]{3,2,1,0:T(8,128)(2,1)S(1)}, u32[]{:S(2)}, u32[]{:S(2)}) collective-permute-start(bf16[2,8,80,128]{3,2,1,0:T(8,128)(2,1)S(1)} %pad_maximum_fusion), channel_id=1, source_target_pairs={{0,1},{1,0},{2,3},{3,2},{4,5},{5,4},{6,7},{7,6},{8,9},{9,8},{10,11... | collective-permute-start | bytes 983048 | tf_op jit(solution)/shard_map/ppermute | solution.py:212
  73.6 15.7 %collective-permute-start.2 = (bf16[128,640]{1,0:T(8,128)(2,1)S(1)}, bf16[128,640]{1,0:T(8,128)(2,1)S(1)}, u32[]{:S(2)}, u32[]{:S(2)}) collective-permute-start(bf16[128,640]{1,0:T(8,128)(2,1)S(1)} %get-tuple-element.41), channel_id=1, source_target_pairs={{0,384},{128,0},{256,128},{384,256},{1,385},{129,1},{257,129},{385... | collective-permute-start | bytes 491528 | tf_op jit(solution)/shard_map/ppermute | solution.py:212
  77.7 11.6 %collective-permute-start.1 = (bf16[128,640]{1,0:T(8,128)(2,1)S(1)}, bf16[128,640]{1,0:T(8,128)(2,1)S(1)}, u32[]{:S(2)}, u32[]{:S(2)}) collective-permute-start(bf16[128,640]{1,0:T(8,128)(2,1)S(1)} %get-tuple-element.42), channel_id=1, source_target_pairs={{0,256},{128,384},{256,0},{384,128},{1,257},{129,385},{257,1},{385... | collective-permute-start | bytes 491528 | tf_op jit(solution)/shard_map/ppermute | solution.py:212
  80.1 10.3 %collective-permute-start = (bf16[128,640]{1,0:T(8,128)(2,1)S(1)}, bf16[128,640]{1,0:T(8,128)(2,1)S(1)}, u32[]{:S(2)}, u32[]{:S(2)}) collective-permute-start(bf16[128,640]{1,0:T(8,128)(2,1)S(1)} %get-tuple-element.40), channel_id=1, source_target_pairs={{0,128},{128,256},{256,384},{384,0},{1,129},{129,257},{257,385},{3... | collective-permute-start | bytes 491528 | tf_op jit(solution)/shard_map/ppermute | solution.py:212
  84.2 13.0 %all-to-all-start.3 = ((bf16[16,80,128]{2,1,0:T(8,128)(2,1)}), bf16[16,80,128]{2,1,0:T(8,128)(2,1)S(1)}, u32[]{:S(2)}, u32[]{:S(2)}) async-start(bf16[16,80,128]{2,1,0:T(8,128)(2,1)} %weight_products.1), calls=%async_computation.3 | async-start | bytes 655360 | tf_op jit(solution)/shard_map/all_to_all | solution.py:216

commit v5 on v4

--- a/solution.py
+++ b/solution.py
@@ -61,19 +61,24 @@
     kv_out[2 * BLOCK :, :] = tail.astype(jnp.float32).astype(jnp.bfloat16)
 
 
-def place_of(rows):
-    return jnp.max(rows.astype(jnp.float32)).astype(jnp.int32)
+def places_of(blocks):
+    digits = sum(rows.astype(jnp.float32) * 16.0**j for j, rows in enumerate(blocks))
+    word = jnp.max(digits).astype(jnp.int32)
+    return [(word >> (4 * j)) & 15 for j in range(len(blocks))]
 
 
 def attention_kernel(
-    q_all, kv_ref, dq_ref, dkv_ref, k_s, v_s, k_t, dk_acc, dv_acc, rank, sorted_place
+    q_all, kv_ref, dq_ref, dkv_ref, k_s, v_s, k_t, dk_acc, dv_acc, rank, sorted_place, q_place
 ):
     dk_acc[...] = jnp.zeros_like(dk_acc)
     dv_acc[...] = jnp.zeros_like(dv_acc)
     key_row = lax.broadcasted_iota(jnp.int32, (BLOCK, STACK), 0)
     query_col = lax.broadcasted_iota(jnp.int32, (BLOCK, STACK), 1) & (BLOCK - 1)
     offset = key_row - query_col
-    places = [place_of(kv_ref[j, 2 * BLOCK :, :]) for j in range(SIDE)]
+    places = places_of([kv_ref[j, 2 * BLOCK :, :] for j in range(SIDE)])
+    tails = [q_all[i, 2 * STACK + 16 :, :].astype(jnp.float32)[14:] for i in range(SIDE)]
+    for i, place in enumerate(places_of(tails)):
+        q_place[i] = place
     for j in range(SIDE):
         r = sum((places[m] < places[j]).astype(jnp.int32) for m in range(SIDE) if m != j)
         rank[j] = r
@@ -91,7 +96,7 @@
         delta = extra[15:20] + extra[20:25] + extra[25:30]
         norm = jnp.concatenate([norm[h : h + 1] for h in range(HEADS)], axis=1)
         delta = jnp.concatenate([delta[h : h + 1] for h in range(HEADS)], axis=1)
-        here = place_of(extra[30:32])
+        here = q_place[i]
         seen = sum((sorted_place[j] <= here).astype(jnp.int32) for j in range(SIDE))
 
         @pl.when(seen == 0)
@@ -136,13 +141,22 @@
 
 
 def weight_kernel(rows, keys, out_ref):
+    keys = keys[...].reshape(8 * BLOCK, HEAD_SIZE)
     for f in range(SIDE):
-        total = dot(rows[f, 0], keys[0], ((1,), (0,)))
-        for s in range(1, 8):
-            total += dot(rows[f, s], keys[s], ((1,), (0,)))
-        total = total.astype(jnp.bfloat16)
+        left = jnp.concatenate([rows[f, s] for s in range(8)], axis=1)
+        total = dot(left, keys, ((1,), (0,))).astype(jnp.bfloat16)
         for copy in range(SIDE):
             out_ref[copy * SIDE + f] = total
+
+
+def finish_kernel(parts, d0, d1, d2, d3, wk_out, q_out):
+    for r in range(SIDE):
+        total = sum(parts[b * SIDE + r].astype(jnp.float32) for b in range(SIDE))
+        wk_out[:, r * HEAD_SIZE : (r + 1) * HEAD_SIZE] = total
+    for h in range(HEADS):
+        cols = slice(h * HEAD_SIZE, (h + 1) * HEAD_SIZE)
+        total = sum(d[:, cols].astype(jnp.float32) for d in (d0, d1, d2, d3))
+        q_out[0, :, cols] = total.T.astype(jnp.bfloat16)
 
 
 SMEM = pl.BlockSpec(memory_space=pltpu.SMEM)
@@ -177,6 +191,7 @@
             pltpu.VMEM((SIDE * BLOCK, HEAD_SIZE), jnp.float32),
             pltpu.SMEM((SIDE,), jnp.int32),
             pltpu.SMEM((SIDE,), jnp.int32),
+            pltpu.SMEM((SIDE,), jnp.int32),
         ],
         compiler_params=pltpu.CompilerParams(vmem_limit_bytes=GRANT),
         name="attention_grads",
@@ -204,6 +219,21 @@
         compiler_params=pltpu.CompilerParams(vmem_limit_bytes=GRANT),
         name="weight_products",
     )(rows, keys)
+
+
+def finish(parts, dq):
+    width = parts.shape[1]
+    return pl.pallas_call(
+        finish_kernel,
+        out_shape=(
+            struct((width, SIDE * HEAD_SIZE), jnp.float32),
+            struct((1, BLOCK, STACK)),
+        ),
+        in_specs=[VMEM] * 5,
+        out_specs=(VMEM,) * 2,
+        compiler_params=pltpu.CompilerParams(vmem_limit_bytes=GRANT),
+        name="finish",
+    )(parts, *dq)
 
 
 def ahead(value, axis, steps):
@@ -248,18 +278,15 @@
     here = lax.axis_index("x")
     pieces = [lax.dynamic_index_in_dim(dq, (here + s) % SIDE, 0, keepdims=False) for s in range(SIDE)]
     dq = pieces[:1] + [ahead(pieces[s], "x", s) for s in (1, 2, 3)]
-    grad_q = total(jnp.stack(dq))
-    grad_q = grad_q.reshape(HEAD_SIZE, HEADS, BLOCK).transpose(2, 1, 0).reshape(BLOCK, STACK)
-
     weights = row_features(features)
     gathered = swap(key_copies, ("zl", "yh"))
     partial = weight_products(weights, gathered)
     partial = swap(partial, ("x", "yl", "c"))
     mine = total(partial.reshape((SIDE, SIDE) + partial.shape[1:])).astype(jnp.bfloat16)
-    mine = lax.all_gather(mine, "zh", axis=0)
-    width = features.shape[-1]
-    grad_wk = total(mine).transpose(1, 0, 2).reshape(width, SIDE * HEAD_SIZE)
-    return (grad_q.astype(jnp.bfloat16)[None], key_gradient, value_gradient, grad_wk)
+    mine = mine.reshape(SIDE, features.shape[-1], HEAD_SIZE)
+    mine = lax.all_gather(mine, "zh", axis=0, tiled=True)
+    grad_wk, grad_q = finish(mine, dq)
+    return (grad_q, key_gradient, value_gradient, grad_wk)
 
 
 def solution(mesh):

time: 121 us -> 120 us (level)
  the two profiles are of different devices: /device:TPU:113 before, /device:TPU:8 now
where the time goes in v5:
time: 120 us; the launch traced here: 119 us
  blocking collectives  47.9 us (40%)
  starting transfers between devices  39.4 us (33%)
  waiting for transfers between devices  22.7 us (19%)
  Pallas kernels  8.26 us (7%)
    all_gather x1, blocking collectives, whole(): kv_all = lax.all_gather(kv_own, 'zh', axis=0)  26.7 us
    all_to_all x4, starting transfers between devices, swap(): return lax.all_to_all(value, axis, 0, 0, tiled=True)  23.8 us
    all_gather x1, blocking collectives, whole(): mine = lax.all_gather(mine, 'zh', axis=0, tiled=True)  21.2 us
    all_to_all x4, waiting for transfers between devices, swap(): return lax.all_to_all(value, axis, 0, 0, tiled=True)  21.1 us
    ppermute x5, starting transfers between devices, ahead(): return lax.ppermute(value, axis, pairs)  15.6 us
    pallas_call x1, Pallas kernels, attention_grads(): pl.pallas_call(attention_kernel, out_shape=(struct((SIDE, HEAD_SIZE, STAC...  3.16 us
    pallas_call x1, Pallas kernels, pack(): pl.pallas_call(pack_kernel, out_shape=(struct((SIDE, Q_ROWS, HEAD_SIZE)),...  2.45 us
  transfers between devices with their start and end apart: 9, of which 3 were waited for; matrix products, arithmetic and copies ran while one was open for 0% of the time, Pallas kernels for 1%

profile of v5, /device:TPU:8, one launch (start us, length us, event | category | flops | bytes accessed | tf_op | source)
XLA Modules:
  0.0 119.4 jit_solution(6823641223435911666)
XLA Ops:
  0.6 2.4 %pack.1 = (bf16[4,1312,128]{2,1,0:T(8,128)(2,1)}, bf16[272,128]{1,0:T(8,128)(2,1)}) custom-call(s32[1,8]{1,0:T(1,128)} %bitcast.31, bf16[1,128,640]{2,1,0:T(8,128)(2,1)} %q_ref.1, bf16[1,128,640]{2,1,0:T(8,128)(2,1)} %g_ref.1, bf16[1,128,640]{2,1,0:T(8,128)(2,1)} %o_ref.1, f32[5,1,128]{2,1,0:T(1,128)} %bitcast.30, bf16[1,128,128]{2,1,0:T(8,128)(2,1)} %k_ref.1, ...), custom_call_target="tpu_custom_call" | custom-call | tf_op jit(solution)/shard_map/pack/pallas_call | solution.py:171
  3.1 0.0 copy-start.1
  3.1 4.4 %all-to-all-start = ((bf16[4,1312,128]{2,1,0:T(8,128)(2,1)}), bf16[4,1312,128]{2,1,0:T(8,128)(2,1)S(1)}, u32[]{:S(2)}, u32[]{:S(2)}) async-start(bf16[4,1312,128]{2,1,0:T(8,128)(2,1)} %get-tuple-element.13), calls=%async_computation | async-start | bytes 2686976 | tf_op jit(solution)/shard_map/all_to_all | solution.py:246
  7.5 0.0 copy-start
  7.5 0.0 copy-done.1
  7.5 26.7 %all-gather = bf16[1088,128]{1,0:T(8,128)(2,1)S(1)} all-gather(bf16[272,128]{1,0:T(8,128)(2,1)S(1)} %copy-done.1), channel_id=2, replica_groups=mesh['x'=4,'zh'=4,'zl'=4,'yh'=2,'yl'=2,'c'=2] {'zh'}, dimensions={0}, use_global_device_ids=true | all-gather | bytes 348160 | tf_op jit(solution)/shard_map/all_gather | solution.py:273
  34.2 0.0 all-to-all-done.q_all
  34.2 3.2 %attention_grads.1 = (bf16[4,128,640]{2,1,0:T(8,128)(2,1)S(1)}, bf16[4,256,128]{2,1,0:T(8,128)(2,1)}) custom-call(bf16[4,1312,128]{2,1,0:T(8,128)(2,1)S(1)} %all-to-all-done.q_all, bf16[4,272,128]{2,1,0:T(8,128)(2,1)S(1)} %bitcast.27), custom_call_target="tpu_custom_call" | custom-call | tf_op jit(solution)/shard_map/attention_grads/pallas_call | solution.py:181
  37.4 7.5 %all-to-all-start.1 = ((bf16[4,256,128]{2,1,0:T(8,128)(2,1)}), bf16[4,256,128]{2,1,0:T(8,128)(2,1)S(1)}, u32[]{:S(2)}, u32[]{:S(2)}) async-start(bf16[4,256,128]{2,1,0:T(8,128)(2,1)} %get-tuple-element.15), calls=%async_computation.1 | async-start | bytes 524288 | tf_op jit(solution)/shard_map/all_to_all | solution.py:246
  44.9 0.0 copy-done
  44.9 2.3 %collective-permute-start = (bf16[8,80,128]{2,1,0:T(8,128)(2,1)S(1)}, bf16[8,80,128]{2,1,0:T(8,128)(2,1)S(1)}, u32[]{:S(2)}, u32[]{:S(2)}) collective-permute-start(bf16[8,80,128]{2,1,0:T(8,128)(2,1)S(1)} %bitcast.29), channel_id=1, source_target_pairs={{0,2},{2,0},{1,3},{3,1},{4,6},{6,4},{5,7},{7,5},{8,10},{10,8},{9,1... | collective-permute-start | bytes 491528 | tf_op jit(solution)/shard_map/ppermute | solution.py:242
  47.2 15.2 %all-to-all-done.1.parts = bf16[4,256,128]{2,1,0:T(8,128)(2,1)S(1)} async-done(((bf16[4,256,128]{2,1,0:T(8,128)(2,1)}), bf16[4,256,128]{2,1,0:T(8,128)(2,1)S(1)}, u32[]{:S(2)}, u32[]{:S(2)}) %all-to-all-start.1) | async-done | bytes 262176 | tf_op jit(solution)/shard_map/all_to_all | solution.py:246
  62.4 0.7 fold.1
  63.1 6.2 %all-to-all-start.2 = ((bf16[8,128,128]{2,1,0:T(8,128)(2,1)}), bf16[8,128,128]{2,1,0:T(8,128)(2,1)S(1)}, u32[]{:S(2)}, u32[]{:S(2)}) async-start(bf16[8,128,128]{2,1,0:T(8,128)(2,1)} %get-tuple-element.16), calls=%async_computation.2 | async-start | bytes 524288 | tf_op jit(solution)/shard_map/all_to_all | solution.py:246
  69.3 0.0 collective-permute-done
  69.4 1.9 %collective-permute-start.1 = (bf16[2,8,80,128]{3,2,1,0:T(8,128)(2,1)S(1)}, bf16[2,8,80,128]{3,2,1,0:T(8,128)(2,1)S(1)}, u32[]{:S(2)}, u32[]{:S(2)}) collective-permute-start(bf16[2,8,80,128]{3,2,1,0:T(8,128)(2,1)S(1)} %pad_maximum_fusion), channel_id=1, source_target_pairs={{0,1},{1,0},{2,3},{3,2},{4,5},{5,4},{6,7},{7,6},{8,9},{9,8},{10,11... | collective-permute-start | bytes 983048 | tf_op jit(solution)/shard_map/ppermute | solution.py:242
  71.3 1.6 %collective-permute-done.1 = bf16[2,8,80,128]{3,2,1,0:T(8,128)(2,1)S(1)} collective-permute-done((bf16[2,8,80,128]{3,2,1,0:T(8,128)(2,1)S(1)}, bf16[2,8,80,128]{3,2,1,0:T(8,128)(2,1)S(1)}, u32[]{:S(2)}, u32[]{:S(2)}) %collective-permute-start.1) | collective-permute-done | bytes 327712 | tf_op jit(solution)/shard_map/ppermute | solution.py:242
  73.0 0.1 maximum_bitcast_fusion
  73.1 5.9 %all-to-all-done.2.keys = bf16[8,128,128]{2,1,0:T(8,128)(2,1)S(1)} async-done(((bf16[8,128,128]{2,1,0:T(8,128)(2,1)}), bf16[8,128,128]{2,1,0:T(8,128)(2,1)S(1)}, u32[]{:S(2)}, u32[]{:S(2)}) %all-to-all-start.2) | async-done | bytes 262176 | tf_op jit(solution)/shard_map/all_to_all | solution.py:246
  79.0 1.1 weight_products.1
  80.1 5.7 %all-to-all-start.3 = ((bf16[16,80,128]{2,1,0:T(8,128)(2,1)}), bf16[16,80,128]{2,1,0:T(8,128)(2,1)S(1)}, u32[]{:S(2)}, u32[]{:S(2)}) async-start(bf16[16,80,128]{2,1,0:T(8,128)(2,1)} %weight_products.1), calls=%async_computation.3 | async-start | bytes 655360 | tf_op jit(solution)/shard_map/all_to_all | solution.py:246
  85.8 0.1 dynamic-slice_bitcast_fusion
  85.8 3.4 %collective-permute-start.2 = (bf16[128,640]{1,0:T(8,128)(2,1)S(1)}, bf16[128,640]{1,0:T(8,128)(2,1)S(1)}, u32[]{:S(2)}, u32[]{:S(2)}) collective-permute-start(bf16[128,640]{1,0:T(8,128)(2,1)S(1)} %get-tuple-element.24), channel_id=1, source_target_pairs={{0,128},{128,256},{256,384},{384,0},{1,129},{129,257},{257,385},{3... | collective-permute-start | bytes 491528 | tf_op jit(solution)/shard_map/ppermute | solution.py:242
  89.2 4.6 %collective-permute-start.3 = (bf16[128,640]{1,0:T(8,128)(2,1)S(1)}, bf16[128,640]{1,0:T(8,128)(2,1)S(1)}, u32[]{:S(2)}, u32[]{:S(2)}) collective-permute-start(bf16[128,640]{1,0:T(8,128)(2,1)S(1)} %get-tuple-element.23), channel_id=1, source_target_pairs={{0,256},{128,384},{256,0},{384,128},{1,257},{129,385},{257,1},{385... | collective-permute-start | bytes 491528 | tf_op jit(solution)/shard_map/ppermute | solution.py:242
  93.8 3.4 %collective-permute-start.4 = (bf16[128,640]{1,0:T(8,128)(2,1)S(1)}, bf16[128,640]{1,0:T(8,128)(2,1)S(1)}, u32[]{:S(2)}, u32[]{:S(2)}) collective-permute-start(bf16[128,640]{1,0:T(8,128)(2,1)S(1)} %get-tuple-element.22), channel_id=1, source_target_pairs={{0,384},{128,0},{256,128},{384,256},{1,385},{129,1},{257,129},{385... | collective-permute-start | bytes 491528 | tf_op jit(solution)/shard_map/ppermute | solution.py:242
  97.2 0.0 all-to-all-done.3
  97.2 0.1 reduce_sum.12
  97.3 21.2 %all_gather.11.parts = bf16[16,80,128]{2,1,0:T(8,128)(2,1)S(1)} all-gather(bf16[4,80,128]{2,1,0:T(8,128)(2,1)S(1)} %reduce_sum.12), channel_id=1, replica_groups=mesh['x'=4,'zh'=4,'zl'=4,'yh'=2,'yl'=2,'c'=2] {'zh'}, dimensions={0}, use_global_device_ids=true | all-gather | bytes 409600 | tf_op jit(solution)/shard_map/all_gather | solution.py:287
  118.5 0.0 collective-permute-done.2.d1
  118.5 0.0 collective-permute-done.3.d2
  118.5 0.0 collective-permute-done.4.d3
  118.5 0.9 finish.1
  (4 shorter events, 0.2 us)
Async XLA Ops:
  3.1 4.4 %copy-start.1 = (bf16[272,128]{1,0:T(8,128)(2,1)S(1)}, bf16[272,128]{1,0:T(8,128)(2,1)}, u32[]{:S(2)}) copy-start(bf16[272,128]{1,0:T(8,128)(2,1)} %get-tuple-element.14) | copy-start | bytes 208900
  3.1 31.1 %all-to-all-start = ((bf16[4,1312,128]{2,1,0:T(8,128)(2,1)}), bf16[4,1312,128]{2,1,0:T(8,128)(2,1)S(1)}, u32[]{:S(2)}, u32[]{:S(2)}) async-start(bf16[4,1312,128]{2,1,0:T(8,128)(2,1)} %get-tuple-element.13), calls=%async_computation | async-start | bytes 2686976 | tf_op jit(solution)/shard_map/all_to_all | solution.py:246
  7.5 37.3 %copy-start = (bf16[8,128,80]{1,2,0:T(8,128)(2,1)S(1)}, bf16[8,128,80]{1,2,0:T(8,128)(2,1)}, u32[]{:S(2)}) copy-start(bf16[8,128,80]{1,2,0:T(8,128)(2,1)} %param.15) | copy-start | bytes 491524
  37.4 25.0 %all-to-all-start.1 = ((bf16[4,256,128]{2,1,0:T(8,128)(2,1)}), bf16[4,256,128]{2,1,0:T(8,128)(2,1)S(1)}, u32[]{:S(2)}, u32[]{:S(2)}) async-start(bf16[4,256,128]{2,1,0:T(8,128)(2,1)} %get-tuple-element.15), calls=%async_computation.1 | async-start | bytes 524288 | tf_op jit(solution)/shard_map/all_to_all | solution.py:246
  44.9 24.4 %collective-permute-start = (bf16[8,80,128]{2,1,0:T(8,128)(2,1)S(1)}, bf16[8,80,128]{2,1,0:T(8,128)(2,1)S(1)}, u32[]{:S(2)}, u32[]{:S(2)}) collective-permute-start(bf16[8,80,128]{2,1,0:T(8,128)(2,1)S(1)} %bitcast.29), channel_id=1, source_target_pairs={{0,2},{2,0},{1,3},{3,1},{4,6},{6,4},{5,7},{7,5},{8,10},{10,8},{9,1... | collective-permute-start | bytes 491528 | tf_op jit(solution)/shard_map/ppermute | solution.py:242
  63.1 15.9 %all-to-all-start.2 = ((bf16[8,128,128]{2,1,0:T(8,128)(2,1)}), bf16[8,128,128]{2,1,0:T(8,128)(2,1)S(1)}, u32[]{:S(2)}, u32[]{:S(2)}) async-start(bf16[8,128,128]{2,1,0:T(8,128)(2,1)} %get-tuple-element.16), calls=%async_computation.2 | async-start | bytes 524288 | tf_op jit(solution)/shard_map/all_to_all | solution.py:246
  69.4 3.5 %collective-permute-start.1 = (bf16[2,8,80,128]{3,2,1,0:T(8,128)(2,1)S(1)}, bf16[2,8,80,128]{3,2,1,0:T(8,128)(2,1)S(1)}, u32[]{:S(2)}, u32[]{:S(2)}) collective-permute-start(bf16[2,8,80,128]{3,2,1,0:T(8,128)(2,1)S(1)} %pad_maximum_fusion), channel_id=1, source_target_pairs={{0,1},{1,0},{2,3},{3,2},{4,5},{5,4},{6,7},{7,6},{8,9},{9,8},{10,11... | collective-permute-start | bytes 983048 | tf_op jit(solution)/shard_map/ppermute | solution.py:242
  80.1 17.1 %all-to-all-start.3 = ((bf16[16,80,128]{2,1,0:T(8,128)(2,1)}), bf16[16,80,128]{2,1,0:T(8,128)(2,1)S(1)}, u32[]{:S(2)}, u32[]{:S(2)}) async-start(bf16[16,80,128]{2,1,0:T(8,128)(2,1)} %weight_products.1), calls=%async_computation.3 | async-start | bytes 655360 | tf_op jit(solution)/shard_map/all_to_all | solution.py:246
  85.8 32.6 %collective-permute-start.2 = (bf16[128,640]{1,0:T(8,128)(2,1)S(1)}, bf16[128,640]{1,0:T(8,128)(2,1)S(1)}, u32[]{:S(2)}, u32[]{:S(2)}) collective-permute-start(bf16[128,640]{1,0:T(8,128)(2,1)S(1)} %get-tuple-element.24), channel_id=1, source_target_pairs={{0,128},{128,256},{256,384},{384,0},{1,129},{129,257},{257,385},{3... | collective-permute-start | bytes 491528 | tf_op jit(solution)/shard_map/ppermute | solution.py:242
  89.2 29.3 %collective-permute-start.3 = (bf16[128,640]{1,0:T(8,128)(2,1)S(1)}, bf16[128,640]{1,0:T(8,128)(2,1)S(1)}, u32[]{:S(2)}, u32[]{:S(2)}) collective-permute-start(bf16[128,640]{1,0:T(8,128)(2,1)S(1)} %get-tuple-element.23), channel_id=1, source_target_pairs={{0,256},{128,384},{256,0},{384,128},{1,257},{129,385},{257,1},{385... | collective-permute-start | bytes 491528 | tf_op jit(solution)/shard_map/ppermute | solution.py:242
  93.8 24.7 %collective-permute-start.4 = (bf16[128,640]{1,0:T(8,128)(2,1)S(1)}, bf16[128,640]{1,0:T(8,128)(2,1)S(1)}, u32[]{:S(2)}, u32[]{:S(2)}) collective-permute-start(bf16[128,640]{1,0:T(8,128)(2,1)S(1)} %get-tuple-element.22), channel_id=1, source_target_pairs={{0,384},{128,0},{256,128},{384,256},{1,385},{129,1},{257,129},{385... | collective-permute-start | bytes 491528 | tf_op jit(solution)/shard_map/ppermute | solution.py:242

commit v6 on v5

--- a/solution.py
+++ b/solution.py
@@ -15,8 +15,10 @@
 SCALE = HEAD_SIZE ** (-0.5)
 LOG2E = 1.4426950408889634
 CTX = ("x", "zh")
-FSDP = ("zl", "yh", "yl", "c")
+FSDP = ("s", "yl", "c")
 GRANT = 16 * 2**20
+Z_ORDER = (1, 0, 3, 2)
+S_ORDER = (4, 5, 2, 3, 6, 7, 0, 1)
 Q_ROWS = 2 * STACK + 32
 KV_ROWS = 2 * BLOCK + 16
 
@@ -34,7 +36,7 @@
 
 
 def own_place(places):
-    return places[0, lax.axis_index("zl") * 2 + lax.axis_index("yh")]
+    return places[0, lax.axis_index("s")]
 
 
 def pack_kernel(places, q_ref, g_ref, o_ref, norm_ref, k_ref, v_ref, q_out, kv_out):
@@ -127,8 +129,9 @@
     lax.fori_loop(0, SIDE, row, 0)
     for j in range(SIDE):
         at = pl.multiple_of(rank[j] * BLOCK, BLOCK)
-        dkv_ref[j, :BLOCK, :] = dk_acc[pl.ds(at, BLOCK), :].astype(jnp.bfloat16)
-        dkv_ref[j, BLOCK:, :] = dv_acc[pl.ds(at, BLOCK), :].astype(jnp.bfloat16)
+        slot = Z_ORDER.index(j)
+        dkv_ref[slot, :BLOCK, :] = dk_acc[pl.ds(at, BLOCK), :].astype(jnp.bfloat16)
+        dkv_ref[slot, BLOCK:, :] = dv_acc[pl.ds(at, BLOCK), :].astype(jnp.bfloat16)
 
 
 def fold_kernel(parts, copies_out, key_out, value_out):
@@ -143,7 +146,7 @@
 def weight_kernel(rows, keys, out_ref):
     keys = keys[...].reshape(8 * BLOCK, HEAD_SIZE)
     for f in range(SIDE):
-        left = jnp.concatenate([rows[f, s] for s in range(8)], axis=1)
+        left = jnp.concatenate([rows[f, s] for s in S_ORDER], axis=1)
         total = dot(left, keys, ((1,), (0,))).astype(jnp.bfloat16)
         for copy in range(SIDE):
             out_ref[copy * SIDE + f] = total
@@ -273,13 +276,15 @@
     kv_all = lax.all_gather(kv_own, "zh", axis=0)
     dq, dkv = attention_grads(q_all, kv_all)
 
-    dkv = swap(dkv, "zh")
+    groups = [list(Z_ORDER)]
+    dkv = lax.all_to_all(dkv, "zh", 0, 0, tiled=True, axis_index_groups=groups)
     key_copies, key_gradient, value_gradient = fold(dkv)
     here = lax.axis_index("x")
     pieces = [lax.dynamic_index_in_dim(dq, (here + s) % SIDE, 0, keepdims=False) for s in range(SIDE)]
     dq = pieces[:1] + [ahead(pieces[s], "x", s) for s in (1, 2, 3)]
     weights = row_features(features)
-    gathered = swap(key_copies, ("zl", "yh"))
+    groups = [list(S_ORDER)]
+    gathered = lax.all_to_all(key_copies, "s", 0, 0, tiled=True, axis_index_groups=groups)
     partial = weight_products(weights, gathered)
     partial = swap(partial, ("x", "yl", "c"))
     mine = total(partial.reshape((SIDE, SIDE) + partial.shape[1:])).astype(jnp.bfloat16)
@@ -290,7 +295,7 @@
 
 
 def solution(mesh):
-    fine = Mesh(mesh.devices.reshape(4, 4, 4, 2, 2, 2), CTX + FSDP)
+    fine = Mesh(mesh.devices.reshape(4, 4, 8, 2, 2), CTX + FSDP)
     return jax.shard_map(
         whole,
         mesh=fine,

time: 120 us -> 118 us (0.983)
  waiting for transfers between devices: 22.7 us -> 15 us
  starting transfers between devices: 39.4 us -> 43.9 us
    all_to_all x4 -> x2, waiting for transfers between devices: 21.1 us -> 0.01 us  [swap(): return lax.all_to_all(value, axis, 0, 0, tiled=True)]
    all_to_all x0 -> x2, starting transfers between devices: none -> 18.8 us  [the longest x1 10.8 us: whole(): dkv = lax.all_to_all(dkv, 'zh', 0, 0, tiled=True, axis_index_groups=groups)]
    all_to_all x4 -> x2, starting transfers between devices: 23.8 us -> 9.51 us  [swap(): return lax.all_to_all(value, axis, 0, 0, tiled=True)]
    all_to_all x0 -> x2, waiting for transfers between devices: none -> 13.4 us  [the longest x1 9.66 us: whole(): dkv = lax.all_to_all(dkv, 'zh', 0, 0, tiled=True, axis_index_groups=groups)]
where the time goes in v6:
time: 118 us; the launch traced here: 117 us
  blocking collectives  48.6 us (41%)
  starting transfers between devices  43.9 us (37%)
  waiting for transfers between devices  15 us (13%)
  Pallas kernels  8.26 us (7%)
    all_gather x1, blocking collectives, whole(): kv_all = lax.all_gather(kv_own, 'zh', axis=0)  26.7 us
    all_gather x1, blocking collectives, whole(): mine = lax.all_gather(mine, 'zh', axis=0, tiled=True)  22 us
    ppermute x5, starting transfers between devices, ahead(): return lax.ppermute(value, axis, pairs)  15.6 us
    all_to_all x1, starting transfers between devices, whole(): dkv = lax.all_to_all(dkv, 'zh', 0, 0, tiled=True, axis_index_groups=groups)  10.8 us
    all_to_all x1, waiting for transfers between devices, whole(): dkv = lax.all_to_all(dkv, 'zh', 0, 0, tiled=True, axis_index_groups=groups)  9.66 us
    all_to_all x2, starting transfers between devices, swap(): return lax.all_to_all(value, axis, 0, 0, tiled=True)  9.51 us
    all_to_all x1, starting transfers between devices, whole(): lax.all_to_all(key_copies, 's', 0, 0, tiled=True, axis_index_groups=groups)  8.06 us
    all_to_all x1, waiting for transfers between devices, whole(): lax.all_to_all(key_copies, 's', 0, 0, tiled=True, axis_index_groups=groups)  3.7 us
  transfers between devices with their start and end apart: 9, of which 3 were waited for; matrix products, arithmetic and copies ran while one was open for 0% of the time, Pallas kernels for 1%

profile of v6, /device:TPU:8, one launch (start us, length us, event | category | flops | bytes accessed | tf_op | source)
XLA Modules:
  0.0 116.9 jit_solution(5366841568825515768)
XLA Ops:
  0.6 2.4 %pack.1 = (bf16[4,1312,128]{2,1,0:T(8,128)(2,1)}, bf16[272,128]{1,0:T(8,128)(2,1)}) custom-call(s32[1,8]{1,0:T(1,128)} %bitcast.31, bf16[1,128,640]{2,1,0:T(8,128)(2,1)} %q_ref.1, bf16[1,128,640]{2,1,0:T(8,128)(2,1)} %g_ref.1, bf16[1,128,640]{2,1,0:T(8,128)(2,1)} %o_ref.1, f32[5,1,128]{2,1,0:T(1,128)} %bitcast.30, bf16[1,128,128]{2,1,0:T(8,128)(2,1)} %k_ref.1, ...), custom_call_target="tpu_custom_call" | custom-call | tf_op jit(solution)/shard_map/pack/pallas_call | solution.py:174
  3.1 0.0 copy-start.1
  3.1 4.4 %all-to-all-start = ((bf16[4,1312,128]{2,1,0:T(8,128)(2,1)}), bf16[4,1312,128]{2,1,0:T(8,128)(2,1)S(1)}, u32[]{:S(2)}, u32[]{:S(2)}) async-start(bf16[4,1312,128]{2,1,0:T(8,128)(2,1)} %get-tuple-element.13), calls=%async_computation | async-start | bytes 2686976 | tf_op jit(solution)/shard_map/all_to_all | solution.py:249
  7.5 0.0 copy-start
  7.5 0.0 copy-done.1
  7.5 26.7 %all-gather = bf16[1088,128]{1,0:T(8,128)(2,1)S(1)} all-gather(bf16[272,128]{1,0:T(8,128)(2,1)S(1)} %copy-done.1), channel_id=2, replica_groups=mesh['x'=4,'zh'=4,'s'=8,'yl'=2,'c'=2] {'zh'}, dimensions={0}, use_global_device_ids=true | all-gather | bytes 348160 | tf_op jit(solution)/shard_map/all_gather | solution.py:276
  34.2 0.0 all-to-all-done.q_all
  34.2 3.2 %attention_grads.1 = (bf16[4,128,640]{2,1,0:T(8,128)(2,1)S(1)}, bf16[4,256,128]{2,1,0:T(8,128)(2,1)}) custom-call(bf16[4,1312,128]{2,1,0:T(8,128)(2,1)S(1)} %all-to-all-done.q_all, bf16[4,272,128]{2,1,0:T(8,128)(2,1)S(1)} %bitcast.27), custom_call_target="tpu_custom_call" | custom-call | tf_op jit(solution)/shard_map/attention_grads/pallas_call | solution.py:184
  37.4 10.8 %all-to-all-start.1 = ((bf16[4,256,128]{2,1,0:T(8,128)(2,1)}), bf16[4,256,128]{2,1,0:T(8,128)(2,1)S(1)}, u32[]{:S(2)}, u32[]{:S(2)}) async-start(bf16[4,256,128]{2,1,0:T(8,128)(2,1)} %get-tuple-element.15), calls=%async_computation.1 | async-start | bytes 524288 | tf_op jit(solution)/shard_map/all_to_all | solution.py:280
  48.1 0.0 copy-done
  48.1 2.3 %collective-permute-start = (bf16[8,80,128]{2,1,0:T(8,128)(2,1)S(1)}, bf16[8,80,128]{2,1,0:T(8,128)(2,1)S(1)}, u32[]{:S(2)}, u32[]{:S(2)}) collective-permute-start(bf16[8,80,128]{2,1,0:T(8,128)(2,1)S(1)} %bitcast.29), channel_id=1, source_target_pairs={{0,2},{2,0},{1,3},{3,1},{4,6},{6,4},{5,7},{7,5},{8,10},{10,8},{9,1... | collective-permute-start | bytes 491528 | tf_op jit(solution)/shard_map/ppermute | solution.py:245
  50.5 9.7 %all-to-all-done.1.parts = bf16[4,256,128]{2,1,0:T(8,128)(2,1)S(1)} async-done(((bf16[4,256,128]{2,1,0:T(8,128)(2,1)}), bf16[4,256,128]{2,1,0:T(8,128)(2,1)S(1)}, u32[]{:S(2)}, u32[]{:S(2)}) %all-to-all-start.1) | async-done | bytes 262176 | tf_op jit(solution)/shard_map/all_to_all | solution.py:280
  60.1 0.7 fold.1
  60.9 8.1 %all-to-all-start.2 = ((bf16[8,128,128]{2,1,0:T(8,128)(2,1)}), bf16[8,128,128]{2,1,0:T(8,128)(2,1)S(1)}, u32[]{:S(2)}, u32[]{:S(2)}) async-start(bf16[8,128,128]{2,1,0:T(8,128)(2,1)} %get-tuple-element.16), calls=%async_computation.2 | async-start | bytes 524288 | tf_op jit(solution)/shard_map/all_to_all | solution.py:287
  68.9 0.0 collective-permute-done
  69.0 1.9 %collective-permute-start.1 = (bf16[2,8,80,128]{3,2,1,0:T(8,128)(2,1)S(1)}, bf16[2,8,80,128]{3,2,1,0:T(8,128)(2,1)S(1)}, u32[]{:S(2)}, u32[]{:S(2)}) collective-permute-start(bf16[2,8,80,128]{3,2,1,0:T(8,128)(2,1)S(1)} %pad_maximum_fusion), channel_id=1, source_target_pairs={{0,1},{1,0},{2,3},{3,2},{4,5},{5,4},{6,7},{7,6},{8,9},{9,8},{10,11... | collective-permute-start | bytes 983048 | tf_op jit(solution)/shard_map/ppermute | solution.py:245
  71.0 1.6 %collective-permute-done.1 = bf16[2,8,80,128]{3,2,1,0:T(8,128)(2,1)S(1)} collective-permute-done((bf16[2,8,80,128]{3,2,1,0:T(8,128)(2,1)S(1)}, bf16[2,8,80,128]{3,2,1,0:T(8,128)(2,1)S(1)}, u32[]{:S(2)}, u32[]{:S(2)}) %collective-permute-start.1) | collective-permute-done | bytes 327712 | tf_op jit(solution)/shard_map/ppermute | solution.py:245
  72.6 0.1 maximum_bitcast_fusion
  72.7 3.7 %all-to-all-done.2.keys = bf16[8,128,128]{2,1,0:T(8,128)(2,1)S(1)} async-done(((bf16[8,128,128]{2,1,0:T(8,128)(2,1)}), bf16[8,128,128]{2,1,0:T(8,128)(2,1)S(1)}, u32[]{:S(2)}, u32[]{:S(2)}) %all-to-all-start.2) | async-done | bytes 262176 | tf_op jit(solution)/shard_map/all_to_all | solution.py:287
  76.4 1.1 weight_products.1
  77.5 5.1 %all-to-all-start.3 = ((bf16[16,80,128]{2,1,0:T(8,128)(2,1)}), bf16[16,80,128]{2,1,0:T(8,128)(2,1)S(1)}, u32[]{:S(2)}, u32[]{:S(2)}) async-start(bf16[16,80,128]{2,1,0:T(8,128)(2,1)} %weight_products.1), calls=%async_computation.3 | async-start | bytes 655360 | tf_op jit(solution)/shard_map/all_to_all | solution.py:249
  82.6 0.1 dynamic-slice_bitcast_fusion
  82.6 3.4 %collective-permute-start.2 = (bf16[128,640]{1,0:T(8,128)(2,1)S(1)}, bf16[128,640]{1,0:T(8,128)(2,1)S(1)}, u32[]{:S(2)}, u32[]{:S(2)}) collective-permute-start(bf16[128,640]{1,0:T(8,128)(2,1)S(1)} %get-tuple-element.24), channel_id=1, source_target_pairs={{0,128},{128,256},{256,384},{384,0},{1,129},{129,257},{257,385},{3... | collective-permute-start | bytes 491528 | tf_op jit(solution)/shard_map/ppermute | solution.py:245
  86.0 4.6 %collective-permute-start.3 = (bf16[128,640]{1,0:T(8,128)(2,1)S(1)}, bf16[128,640]{1,0:T(8,128)(2,1)S(1)}, u32[]{:S(2)}, u32[]{:S(2)}) collective-permute-start(bf16[128,640]{1,0:T(8,128)(2,1)S(1)} %get-tuple-element.23), channel_id=1, source_target_pairs={{0,256},{128,384},{256,0},{384,128},{1,257},{129,385},{257,1},{385... | collective-permute-start | bytes 491528 | tf_op jit(solution)/shard_map/ppermute | solution.py:245
  90.6 3.4 %collective-permute-start.4 = (bf16[128,640]{1,0:T(8,128)(2,1)S(1)}, bf16[128,640]{1,0:T(8,128)(2,1)S(1)}, u32[]{:S(2)}, u32[]{:S(2)}) collective-permute-start(bf16[128,640]{1,0:T(8,128)(2,1)S(1)} %get-tuple-element.22), channel_id=1, source_target_pairs={{0,384},{128,0},{256,128},{384,256},{1,385},{129,1},{257,129},{385... | collective-permute-start | bytes 491528 | tf_op jit(solution)/shard_map/ppermute | solution.py:245
  94.0 0.0 all-to-all-done.3
  94.0 0.1 reduce_sum.12
  94.0 22.0 %all_gather.11.parts = bf16[16,80,128]{2,1,0:T(8,128)(2,1)S(1)} all-gather(bf16[4,80,128]{2,1,0:T(8,128)(2,1)S(1)} %reduce_sum.12), channel_id=1, replica_groups=mesh['x'=4,'zh'=4,'s'=8,'yl'=2,'c'=2] {'zh'}, dimensions={0}, use_global_device_ids=true | all-gather | bytes 409600 | tf_op jit(solution)/shard_map/all_gather | solution.py:292
  116.0 0.0 collective-permute-done.2.d1
  116.0 0.0 collective-permute-done.3.d2
  116.0 0.0 collective-permute-done.4.d3
  116.0 0.9 finish.1
  (4 shorter events, 0.2 us)
Async XLA Ops:
  3.1 4.4 %copy-start.1 = (bf16[272,128]{1,0:T(8,128)(2,1)S(1)}, bf16[272,128]{1,0:T(8,128)(2,1)}, u32[]{:S(2)}) copy-start(bf16[272,128]{1,0:T(8,128)(2,1)} %get-tuple-element.14) | copy-start | bytes 208900
  3.1 31.1 %all-to-all-start = ((bf16[4,1312,128]{2,1,0:T(8,128)(2,1)}), bf16[4,1312,128]{2,1,0:T(8,128)(2,1)S(1)}, u32[]{:S(2)}, u32[]{:S(2)}) async-start(bf16[4,1312,128]{2,1,0:T(8,128)(2,1)} %get-tuple-element.13), calls=%async_computation | async-start | bytes 2686976 | tf_op jit(solution)/shard_map/all_to_all | solution.py:249
  7.5 40.6 %copy-start = (bf16[8,128,80]{1,2,0:T(8,128)(2,1)S(1)}, bf16[8,128,80]{1,2,0:T(8,128)(2,1)}, u32[]{:S(2)}) copy-start(bf16[8,128,80]{1,2,0:T(8,128)(2,1)} %param.15) | copy-start | bytes 491524
  37.4 22.8 %all-to-all-start.1 = ((bf16[4,256,128]{2,1,0:T(8,128)(2,1)}), bf16[4,256,128]{2,1,0:T(8,128)(2,1)S(1)}, u32[]{:S(2)}, u32[]{:S(2)}) async-start(bf16[4,256,128]{2,1,0:T(8,128)(2,1)} %get-tuple-element.15), calls=%async_computation.1 | async-start | bytes 524288 | tf_op jit(solution)/shard_map/all_to_all | solution.py:280
  48.1 20.8 %collective-permute-start = (bf16[8,80,128]{2,1,0:T(8,128)(2,1)S(1)}, bf16[8,80,128]{2,1,0:T(8,128)(2,1)S(1)}, u32[]{:S(2)}, u32[]{:S(2)}) collective-permute-start(bf16[8,80,128]{2,1,0:T(8,128)(2,1)S(1)} %bitcast.29), channel_id=1, source_target_pairs={{0,2},{2,0},{1,3},{3,1},{4,6},{6,4},{5,7},{7,5},{8,10},{10,8},{9,1... | collective-permute-start | bytes 491528 | tf_op jit(solution)/shard_map/ppermute | solution.py:245
  60.9 15.5 %all-to-all-start.2 = ((bf16[8,128,128]{2,1,0:T(8,128)(2,1)}), bf16[8,128,128]{2,1,0:T(8,128)(2,1)S(1)}, u32[]{:S(2)}, u32[]{:S(2)}) async-start(bf16[8,128,128]{2,1,0:T(8,128)(2,1)} %get-tuple-element.16), calls=%async_computation.2 | async-start | bytes 524288 | tf_op jit(solution)/shard_map/all_to_all | solution.py:287
  69.0 3.5 %collective-permute-start.1 = (bf16[2,8,80,128]{3,2,1,0:T(8,128)(2,1)S(1)}, bf16[2,8,80,128]{3,2,1,0:T(8,128)(2,1)S(1)}, u32[]{:S(2)}, u32[]{:S(2)}) collective-permute-start(bf16[2,8,80,128]{3,2,1,0:T(8,128)(2,1)S(1)} %pad_maximum_fusion), channel_id=1, source_target_pairs={{0,1},{1,0},{2,3},{3,2},{4,5},{5,4},{6,7},{7,6},{8,9},{9,8},{10,11... | collective-permute-start | bytes 983048 | tf_op jit(solution)/shard_map/ppermute | solution.py:245
  77.5 16.5 %all-to-all-start.3 = ((bf16[16,80,128]{2,1,0:T(8,128)(2,1)}), bf16[16,80,128]{2,1,0:T(8,128)(2,1)S(1)}, u32[]{:S(2)}, u32[]{:S(2)}) async-start(bf16[16,80,128]{2,1,0:T(8,128)(2,1)} %weight_products.1), calls=%async_computation.3 | async-start | bytes 655360 | tf_op jit(solution)/shard_map/all_to_all | solution.py:249
  82.6 33.4 %collective-permute-start.2 = (bf16[128,640]{1,0:T(8,128)(2,1)S(1)}, bf16[128,640]{1,0:T(8,128)(2,1)S(1)}, u32[]{:S(2)}, u32[]{:S(2)}) collective-permute-start(bf16[128,640]{1,0:T(8,128)(2,1)S(1)} %get-tuple-element.24), channel_id=1, source_target_pairs={{0,128},{128,256},{256,384},{384,0},{1,129},{129,257},{257,385},{3... | collective-permute-start | bytes 491528 | tf_op jit(solution)/shard_map/ppermute | solution.py:245
  86.0 30.0 %collective-permute-start.3 = (bf16[128,640]{1,0:T(8,128)(2,1)S(1)}, bf16[128,640]{1,0:T(8,128)(2,1)S(1)}, u32[]{:S(2)}, u32[]{:S(2)}) collective-permute-start(bf16[128,640]{1,0:T(8,128)(2,1)S(1)} %get-tuple-element.23), channel_id=1, source_target_pairs={{0,256},{128,384},{256,0},{384,128},{1,257},{129,385},{257,1},{385... | collective-permute-start | bytes 491528 | tf_op jit(solution)/shard_map/ppermute | solution.py:245
  90.6 25.4 %collective-permute-start.4 = (bf16[128,640]{1,0:T(8,128)(2,1)S(1)}, bf16[128,640]{1,0:T(8,128)(2,1)S(1)}, u32[]{:S(2)}, u32[]{:S(2)}) collective-permute-start(bf16[128,640]{1,0:T(8,128)(2,1)S(1)} %get-tuple-element.22), channel_id=1, source_target_pairs={{0,384},{128,0},{256,128},{384,256},{1,385},{129,1},{257,129},{385... | collective-permute-start | bytes 491528 | tf_op jit(solution)/shard_map/ppermute | solution.py:245

commit v7 on v6

--- a/solution.py
+++ b/solution.py
@@ -18,7 +18,7 @@
 FSDP = ("s", "yl", "c")
 GRANT = 16 * 2**20
 Z_ORDER = (1, 0, 3, 2)
-S_ORDER = (4, 5, 2, 3, 6, 7, 0, 1)
+S_ORDER = (4, 2, 6, 0, 5, 3, 7, 1)
 Q_ROWS = 2 * STACK + 32
 KV_ROWS = 2 * BLOCK + 16
 
@@ -149,7 +149,7 @@
         left = jnp.concatenate([rows[f, s] for s in S_ORDER], axis=1)
         total = dot(left, keys, ((1,), (0,))).astype(jnp.bfloat16)
         for copy in range(SIDE):
-            out_ref[copy * SIDE + f] = total
+            out_ref[f * SIDE + copy] = total
 
 
 def finish_kernel(parts, d0, d1, d2, d3, wk_out, q_out):
@@ -249,10 +249,6 @@
     return lax.all_to_all(value, axis, 0, 0, tiled=True)
 
 
-def total(parts):
-    return jnp.sum(parts.astype(jnp.float32), axis=0)
-
-
 def row_features(features):
     rows = features.transpose(0, 2, 1)
     rows = ahead_pair(rows, "yl")
@@ -286,8 +282,9 @@
     groups = [list(S_ORDER)]
     gathered = lax.all_to_all(key_copies, "s", 0, 0, tiled=True, axis_index_groups=groups)
     partial = weight_products(weights, gathered)
-    partial = swap(partial, ("x", "yl", "c"))
-    mine = total(partial.reshape((SIDE, SIDE) + partial.shape[1:])).astype(jnp.bfloat16)
+    partial = swap(partial, ("yl", "c", "x"))
+    partial = partial.reshape((SIDE, SIDE) + partial.shape[1:]).astype(jnp.float32)
+    mine = jnp.sum(partial, axis=1).astype(jnp.bfloat16)
     mine = mine.reshape(SIDE, features.shape[-1], HEAD_SIZE)
     mine = lax.all_gather(mine, "zh", axis=0, tiled=True)
     grad_wk, grad_q = finish(mine, dq)

time: 118 us -> 117 us (level)
  no operation moved by 1% of the time
where the time goes in v7:
time: 117 us; the launch traced here: 116 us
  blocking collectives  48.3 us (41%)
  starting transfers between devices  43.9 us (38%)
  waiting for transfers between devices  14.9 us (13%)
  Pallas kernels  8.26 us (7%)
    all_gather x1, blocking collectives, whole(): kv_all = lax.all_gather(kv_own, 'zh', axis=0)  26.7 us
    all_gather x1, blocking collectives, whole(): mine = lax.all_gather(mine, 'zh', axis=0, tiled=True)  21.6 us
    ppermute x5, starting transfers between devices, ahead(): return lax.ppermute(value, axis, pairs)  15.6 us
    all_to_all x1, starting transfers between devices, whole(): dkv = lax.all_to_all(dkv, 'zh', 0, 0, tiled=True, axis_index_groups=groups)  10.8 us
    all_to_all x1, waiting for transfers between devices, whole(): dkv = lax.all_to_all(dkv, 'zh', 0, 0, tiled=True, axis_index_groups=groups)  9.66 us
    all_to_all x2, starting transfers between devices, swap(): return lax.all_to_all(value, axis, 0, 0, tiled=True)  9.52 us
    all_to_all x1, starting transfers between devices, whole(): lax.all_to_all(key_copies, 's', 0, 0, tiled=True, axis_index_groups=groups)  8.06 us
    all_to_all x1, waiting for transfers between devices, whole(): lax.all_to_all(key_copies, 's', 0, 0, tiled=True, axis_index_groups=groups)  3.59 us
  transfers between devices with their start and end apart: 9, of which 3 were waited for; matrix products, arithmetic and copies ran while one was open for 0% of the time, Pallas kernels for 1%

profile of v7, /device:TPU:8, one launch (start us, length us, event | category | flops | bytes accessed | tf_op | source)
XLA Modules:
  0.0 116.4 jit_solution(16894818612885682030)
XLA Ops:
  0.6 2.4 %pack.1 = (bf16[4,1312,128]{2,1,0:T(8,128)(2,1)}, bf16[272,128]{1,0:T(8,128)(2,1)}) custom-call(s32[1,8]{1,0:T(1,128)} %bitcast.31, bf16[1,128,640]{2,1,0:T(8,128)(2,1)} %q_ref.1, bf16[1,128,640]{2,1,0:T(8,128)(2,1)} %g_ref.1, bf16[1,128,640]{2,1,0:T(8,128)(2,1)} %o_ref.1, f32[5,1,128]{2,1,0:T(1,128)} %bitcast.30, bf16[1,128,128]{2,1,0:T(8,128)(2,1)} %k_ref.1, ...), custom_call_target="tpu_custom_call" | custom-call | tf_op jit(solution)/shard_map/pack/pallas_call | solution.py:174
  3.1 0.0 copy-start.1
  3.1 4.4 %all-to-all-start = ((bf16[4,1312,128]{2,1,0:T(8,128)(2,1)}), bf16[4,1312,128]{2,1,0:T(8,128)(2,1)S(1)}, u32[]{:S(2)}, u32[]{:S(2)}) async-start(bf16[4,1312,128]{2,1,0:T(8,128)(2,1)} %get-tuple-element.13), calls=%async_computation | async-start | bytes 2686976 | tf_op jit(solution)/shard_map/all_to_all | solution.py:249
  7.5 0.0 copy-start
  7.5 0.0 copy-done.1
  7.5 26.7 %all-gather = bf16[1088,128]{1,0:T(8,128)(2,1)S(1)} all-gather(bf16[272,128]{1,0:T(8,128)(2,1)S(1)} %copy-done.1), channel_id=2, replica_groups=mesh['x'=4,'zh'=4,'s'=8,'yl'=2,'c'=2] {'zh'}, dimensions={0}, use_global_device_ids=true | all-gather | bytes 348160 | tf_op jit(solution)/shard_map/all_gather | solution.py:272
  34.2 0.0 all-to-all-done.q_all
  34.2 3.2 %attention_grads.1 = (bf16[4,128,640]{2,1,0:T(8,128)(2,1)S(1)}, bf16[4,256,128]{2,1,0:T(8,128)(2,1)}) custom-call(bf16[4,1312,128]{2,1,0:T(8,128)(2,1)S(1)} %all-to-all-done.q_all, bf16[4,272,128]{2,1,0:T(8,128)(2,1)S(1)} %bitcast.28), custom_call_target="tpu_custom_call" | custom-call | tf_op jit(solution)/shard_map/attention_grads/pallas_call | solution.py:184
  37.4 10.8 %all-to-all-start.1 = ((bf16[4,256,128]{2,1,0:T(8,128)(2,1)}), bf16[4,256,128]{2,1,0:T(8,128)(2,1)S(1)}, u32[]{:S(2)}, u32[]{:S(2)}) async-start(bf16[4,256,128]{2,1,0:T(8,128)(2,1)} %get-tuple-element.15), calls=%async_computation.1 | async-start | bytes 524288 | tf_op jit(solution)/shard_map/all_to_all | solution.py:276
  48.1 0.0 copy-done
  48.1 2.3 %collective-permute-start = (bf16[8,80,128]{2,1,0:T(8,128)(2,1)S(1)}, bf16[8,80,128]{2,1,0:T(8,128)(2,1)S(1)}, u32[]{:S(2)}, u32[]{:S(2)}) collective-permute-start(bf16[8,80,128]{2,1,0:T(8,128)(2,1)S(1)} %bitcast.29), channel_id=1, source_target_pairs={{0,2},{2,0},{1,3},{3,1},{4,6},{6,4},{5,7},{7,5},{8,10},{10,8},{9,1... | collective-permute-start | bytes 491528 | tf_op jit(solution)/shard_map/ppermute | solution.py:245
  50.5 9.7 %all-to-all-done.1.parts = bf16[4,256,128]{2,1,0:T(8,128)(2,1)S(1)} async-done(((bf16[4,256,128]{2,1,0:T(8,128)(2,1)}), bf16[4,256,128]{2,1,0:T(8,128)(2,1)S(1)}, u32[]{:S(2)}, u32[]{:S(2)}) %all-to-all-start.1) | async-done | bytes 262176 | tf_op jit(solution)/shard_map/all_to_all | solution.py:276
  60.1 0.7 fold.1
  60.9 8.1 %all-to-all-start.2 = ((bf16[8,128,128]{2,1,0:T(8,128)(2,1)}), bf16[8,128,128]{2,1,0:T(8,128)(2,1)S(1)}, u32[]{:S(2)}, u32[]{:S(2)}) async-start(bf16[8,128,128]{2,1,0:T(8,128)(2,1)} %get-tuple-element.16), calls=%async_computation.2 | async-start | bytes 524288 | tf_op jit(solution)/shard_map/all_to_all | solution.py:283
  68.9 0.0 collective-permute-done
  69.0 1.9 %collective-permute-start.1 = (bf16[2,8,80,128]{3,2,1,0:T(8,128)(2,1)S(1)}, bf16[2,8,80,128]{3,2,1,0:T(8,128)(2,1)S(1)}, u32[]{:S(2)}, u32[]{:S(2)}) collective-permute-start(bf16[2,8,80,128]{3,2,1,0:T(8,128)(2,1)S(1)} %pad_maximum_fusion), channel_id=1, source_target_pairs={{0,1},{1,0},{2,3},{3,2},{4,5},{5,4},{6,7},{7,6},{8,9},{9,8},{10,11... | collective-permute-start | bytes 983048 | tf_op jit(solution)/shard_map/ppermute | solution.py:245
  71.0 1.6 %collective-permute-done.1 = bf16[2,8,80,128]{3,2,1,0:T(8,128)(2,1)S(1)} collective-permute-done((bf16[2,8,80,128]{3,2,1,0:T(8,128)(2,1)S(1)}, bf16[2,8,80,128]{3,2,1,0:T(8,128)(2,1)S(1)}, u32[]{:S(2)}, u32[]{:S(2)}) %collective-permute-start.1) | collective-permute-done | bytes 327712 | tf_op jit(solution)/shard_map/ppermute | solution.py:245
  72.6 0.1 maximum_bitcast_fusion
  72.7 3.6 %all-to-all-done.2.keys = bf16[8,128,128]{2,1,0:T(8,128)(2,1)S(1)} async-done(((bf16[8,128,128]{2,1,0:T(8,128)(2,1)}), bf16[8,128,128]{2,1,0:T(8,128)(2,1)S(1)}, u32[]{:S(2)}, u32[]{:S(2)}) %all-to-all-start.2) | async-done | bytes 262176 | tf_op jit(solution)/shard_map/all_to_all | solution.py:283
  76.3 1.1 weight_products.1
  77.4 5.1 %all-to-all-start.3 = ((bf16[16,80,128]{2,1,0:T(8,128)(2,1)}), bf16[16,80,128]{2,1,0:T(8,128)(2,1)S(1)}, u32[]{:S(2)}, u32[]{:S(2)}) async-start(bf16[16,80,128]{2,1,0:T(8,128)(2,1)} %weight_products.1), calls=%async_computation.3 | async-start | bytes 655360 | tf_op jit(solution)/shard_map/all_to_all | solution.py:249
  82.5 0.1 dynamic-slice_bitcast_fusion
  82.5 3.4 %collective-permute-start.2 = (bf16[128,640]{1,0:T(8,128)(2,1)S(1)}, bf16[128,640]{1,0:T(8,128)(2,1)S(1)}, u32[]{:S(2)}, u32[]{:S(2)}) collective-permute-start(bf16[128,640]{1,0:T(8,128)(2,1)S(1)} %get-tuple-element.24), channel_id=1, source_target_pairs={{0,128},{128,256},{256,384},{384,0},{1,129},{129,257},{257,385},{3... | collective-permute-start | bytes 491528 | tf_op jit(solution)/shard_map/ppermute | solution.py:245
  85.9 4.6 %collective-permute-start.3 = (bf16[128,640]{1,0:T(8,128)(2,1)S(1)}, bf16[128,640]{1,0:T(8,128)(2,1)S(1)}, u32[]{:S(2)}, u32[]{:S(2)}) collective-permute-start(bf16[128,640]{1,0:T(8,128)(2,1)S(1)} %get-tuple-element.23), channel_id=1, source_target_pairs={{0,256},{128,384},{256,0},{384,128},{1,257},{129,385},{257,1},{385... | collective-permute-start | bytes 491528 | tf_op jit(solution)/shard_map/ppermute | solution.py:245
  90.5 3.4 %collective-permute-start.4 = (bf16[128,640]{1,0:T(8,128)(2,1)S(1)}, bf16[128,640]{1,0:T(8,128)(2,1)S(1)}, u32[]{:S(2)}, u32[]{:S(2)}) collective-permute-start(bf16[128,640]{1,0:T(8,128)(2,1)S(1)} %get-tuple-element.22), channel_id=1, source_target_pairs={{0,384},{128,0},{256,128},{384,256},{1,385},{129,1},{257,129},{385... | collective-permute-start | bytes 491528 | tf_op jit(solution)/shard_map/ppermute | solution.py:245
  93.9 0.0 all-to-all-done.3
  93.9 21.6 %all_gather.11.parts = bf16[16,80,128]{2,1,0:T(8,128)(2,1)S(1)} all-gather(bf16[4,80,128]{2,1,0:T(8,128)(2,1)S(1)} %bitcast_reduce_fusion), channel_id=1, replica_groups=mesh['x'=4,'zh'=4,'s'=8,'yl'=2,'c'=2] {'zh'}, dimensions={0}, use_global_device_ids=true | all-gather | bytes 409600 | tf_op jit(solution)/shard_map/all_gather | solution.py:289
  115.6 0.0 collective-permute-done.2.d1
  115.6 0.0 collective-permute-done.3.d2
  115.6 0.0 collective-permute-done.4.d3
  115.6 0.9 finish.1
  (5 shorter events, 0.2 us)
Async XLA Ops:
  3.1 4.4 %copy-start.1 = (bf16[272,128]{1,0:T(8,128)(2,1)S(1)}, bf16[272,128]{1,0:T(8,128)(2,1)}, u32[]{:S(2)}) copy-start(bf16[272,128]{1,0:T(8,128)(2,1)} %get-tuple-element.14) | copy-start | bytes 208900
  3.1 31.1 %all-to-all-start = ((bf16[4,1312,128]{2,1,0:T(8,128)(2,1)}), bf16[4,1312,128]{2,1,0:T(8,128)(2,1)S(1)}, u32[]{:S(2)}, u32[]{:S(2)}) async-start(bf16[4,1312,128]{2,1,0:T(8,128)(2,1)} %get-tuple-element.13), calls=%async_computation | async-start | bytes 2686976 | tf_op jit(solution)/shard_map/all_to_all | solution.py:249
  7.5 40.6 %copy-start = (bf16[8,128,80]{1,2,0:T(8,128)(2,1)S(1)}, bf16[8,128,80]{1,2,0:T(8,128)(2,1)}, u32[]{:S(2)}) copy-start(bf16[8,128,80]{1,2,0:T(8,128)(2,1)} %param.15) | copy-start | bytes 491524
  37.4 22.8 %all-to-all-start.1 = ((bf16[4,256,128]{2,1,0:T(8,128)(2,1)}), bf16[4,256,128]{2,1,0:T(8,128)(2,1)S(1)}, u32[]{:S(2)}, u32[]{:S(2)}) async-start(bf16[4,256,128]{2,1,0:T(8,128)(2,1)} %get-tuple-element.15), calls=%async_computation.1 | async-start | bytes 524288 | tf_op jit(solution)/shard_map/all_to_all | solution.py:276
  48.1 20.8 %collective-permute-start = (bf16[8,80,128]{2,1,0:T(8,128)(2,1)S(1)}, bf16[8,80,128]{2,1,0:T(8,128)(2,1)S(1)}, u32[]{:S(2)}, u32[]{:S(2)}) collective-permute-start(bf16[8,80,128]{2,1,0:T(8,128)(2,1)S(1)} %bitcast.29), channel_id=1, source_target_pairs={{0,2},{2,0},{1,3},{3,1},{4,6},{6,4},{5,7},{7,5},{8,10},{10,8},{9,1... | collective-permute-start | bytes 491528 | tf_op jit(solution)/shard_map/ppermute | solution.py:245
  60.9 15.4 %all-to-all-start.2 = ((bf16[8,128,128]{2,1,0:T(8,128)(2,1)}), bf16[8,128,128]{2,1,0:T(8,128)(2,1)S(1)}, u32[]{:S(2)}, u32[]{:S(2)}) async-start(bf16[8,128,128]{2,1,0:T(8,128)(2,1)} %get-tuple-element.16), calls=%async_computation.2 | async-start | bytes 524288 | tf_op jit(solution)/shard_map/all_to_all | solution.py:283
  69.0 3.5 %collective-permute-start.1 = (bf16[2,8,80,128]{3,2,1,0:T(8,128)(2,1)S(1)}, bf16[2,8,80,128]{3,2,1,0:T(8,128)(2,1)S(1)}, u32[]{:S(2)}, u32[]{:S(2)}) collective-permute-start(bf16[2,8,80,128]{3,2,1,0:T(8,128)(2,1)S(1)} %pad_maximum_fusion), channel_id=1, source_target_pairs={{0,1},{1,0},{2,3},{3,2},{4,5},{5,4},{6,7},{7,6},{8,9},{9,8},{10,11... | collective-permute-start | bytes 983048 | tf_op jit(solution)/shard_map/ppermute | solution.py:245
  77.4 16.5 %all-to-all-start.3 = ((bf16[16,80,128]{2,1,0:T(8,128)(2,1)}), bf16[16,80,128]{2,1,0:T(8,128)(2,1)S(1)}, u32[]{:S(2)}, u32[]{:S(2)}) async-start(bf16[16,80,128]{2,1,0:T(8,128)(2,1)} %weight_products.1), calls=%async_computation.3 | async-start | bytes 655360 | tf_op jit(solution)/shard_map/all_to_all | solution.py:249
  82.5 33.0 %collective-permute-start.2 = (bf16[128,640]{1,0:T(8,128)(2,1)S(1)}, bf16[128,640]{1,0:T(8,128)(2,1)S(1)}, u32[]{:S(2)}, u32[]{:S(2)}) collective-permute-start(bf16[128,640]{1,0:T(8,128)(2,1)S(1)} %get-tuple-element.24), channel_id=1, source_target_pairs={{0,128},{128,256},{256,384},{384,0},{1,129},{129,257},{257,385},{3... | collective-permute-start | bytes 491528 | tf_op jit(solution)/shard_map/ppermute | solution.py:245
  85.9 29.7 %collective-permute-start.3 = (bf16[128,640]{1,0:T(8,128)(2,1)S(1)}, bf16[128,640]{1,0:T(8,128)(2,1)S(1)}, u32[]{:S(2)}, u32[]{:S(2)}) collective-permute-start(bf16[128,640]{1,0:T(8,128)(2,1)S(1)} %get-tuple-element.23), channel_id=1, source_target_pairs={{0,256},{128,384},{256,0},{384,128},{1,257},{129,385},{257,1},{385... | collective-permute-start | bytes 491528 | tf_op jit(solution)/shard_map/ppermute | solution.py:245
  90.5 25.1 %collective-permute-start.4 = (bf16[128,640]{1,0:T(8,128)(2,1)S(1)}, bf16[128,640]{1,0:T(8,128)(2,1)S(1)}, u32[]{:S(2)}, u32[]{:S(2)}) collective-permute-start(bf16[128,640]{1,0:T(8,128)(2,1)S(1)} %get-tuple-element.22), channel_id=1, source_target_pairs={{0,384},{128,0},{256,128},{384,256},{1,385},{129,1},{257,129},{385... | collective-permute-start | bytes 491528 | tf_op jit(solution)/shard_map/ppermute | solution.py:245
